TPU v7x, 512 devices: a whole 4x8x8 slice. The times are simulated.
512 devices in a mesh: blk: 8 (over y_lo, x), dom: 64 (over y_hi, z, core).
Axes of the slice: x: 4, y: 8 (y_hi: 4, y_lo: 2; y = y_hi * 2 + y_lo), z: 8, core: 2. Of those that a mesh axis runs over, the one named last changes fastest.
Arguments:
- node_feat: bfloat16 [131072, 256], P(('blk', 'dom')), may hold values from -6 to 6
- cotangent: bfloat16 [131072, 256], P(('blk', 'dom')), may hold values from -6 to 6
- self_weight: bfloat16 [256, 256], replicated, may hold values from -0.375 to 0.375
- neigh_weight: bfloat16 [256, 256], replicated, may hold values from -0.375 to 0.375
- tile_weights: bfloat16 [512, 8, 4, 128, 128], P(('blk', 'dom')), as said below
- tile_dest: int32 [512, 8, 4], P(('blk', 'dom')), may hold values from 0 to 2, as said below
- tile_source: int32 [512, 8, 4], P(('blk', 'dom')), may hold values from 0 to 1
- hub_weights: bfloat16 [512, 64, 32, 128], P(('blk', 'dom')), as said below
- hub_source: int32 [512, 64], P(('blk', 'dom')), may hold values from 0 to 1
- hub_slots: int32 [512, 64, 32], P(('blk', 'dom')), may hold values from 0 to 256, as said below
Outputs:
- layer_out: bfloat16 [131072, 256], P(('blk', 'dom'))
- feat_grad: bfloat16 [131072, 256], P(('blk', 'dom'))
- self_grad: float32 [256, 256], replicated
- neigh_grad: float32 [256, 256], replicated
Inputs may be any that keep to these rules, and one draw needn't show every extreme that they name: `tile_weights`: nonnegative edge weights, zero where there is no edge. `hub_weights`: nonnegative edge weights, zero where there is no edge. `tile_dest`: 2 marks an empty slot; in the slots of one range for one panel the filled ones come first. `hub_slots`: 256 marks a padded slot; rows may repeat.
All inputs are finite; a program needn't handle non-finite values.
Results may differ from a plain program's by a relative error of at most 0.019.
Values may be sent and summed in bfloat16 or wider, within the bound.
No kernel may reach another device: no remote copies, remote signals or barrier semaphores. Data moves between devices by JAX's collectives and lax.ppermute only.
A program may use at most 64 MiB of HBM per device.

v0:
```python
import jax
import jax.numpy as jnp
from jax import lax
from jax.sharding import PartitionSpec as P


def panel_sum(tiles, dests, sources, blocks, nblocks):
    picked = jnp.take(blocks, sources, axis=0)
    contrib = jnp.einsum("krc,kcf->krf", tiles, picked, preferred_element_type=jnp.float32)
    placing = jax.nn.one_hot(dests, nblocks, dtype=jnp.float32)
    return jnp.einsum("kn,krf->nrf", placing, contrib)


def panel_back(tiles, dests, sources, padded_blocks, nblocks):
    picked = jnp.take(padded_blocks, dests, axis=0)
    contrib = jnp.einsum("krc,krf->kcf", tiles, picked, preferred_element_type=jnp.float32)
    placing = jax.nn.one_hot(sources, nblocks, dtype=jnp.float32)
    return jnp.einsum("kn,kcf->ncf", placing, contrib)


def pick_panel(array, panel):
    return lax.dynamic_index_in_dim(array, panel, 0, False)


def per_device(
    node_feat,
    cotangent,
    self_weight,
    neigh_weight,
    tile_weights,
    tile_dest,
    tile_source,
    hub_weights,
    hub_source,
    hub_slots,
):
    rows, width = node_feat.shape
    tile = tile_weights.shape[3]
    nblocks = rows // tile
    tiles = tile_weights[0]
    dests = tile_dest[0]
    sources = tile_source[0]
    own_blocks = node_feat.reshape(nblocks, tile, width)
    empty_blocks = jnp.zeros((nblocks, tile, width), jnp.float32)
    total = empty_blocks
    piece = lax.all_gather(node_feat, "blk", axis=0, tiled=True)
    start = jnp.int32(0)
    for offset in range(piece.shape[0] // rows):
        panel = start // rows + offset
        shard = piece[offset * rows : (offset + 1) * rows].reshape(nblocks, tile, width)
        total = total + panel_sum(
            pick_panel(tiles, panel),
            pick_panel(dests, panel),
            pick_panel(sources, panel),
            shard,
            nblocks,
        )
    local_degree = jnp.einsum(
        "qkn,qkr->nr",
        jax.nn.one_hot(dests, nblocks, dtype=jnp.float32),
        jnp.sum(tiles, axis=-1, dtype=jnp.float32),
    )
    hub_tiles = hub_weights[0]
    hub_blocks = jnp.take(own_blocks, hub_source[0], axis=0)
    hub_part = jnp.einsum("ohc,ocf->ohf", hub_tiles, hub_blocks, preferred_element_type=jnp.float32)
    hub_degree = jnp.sum(hub_tiles, axis=-1, dtype=jnp.float32)
    got_part, got_degree = (
        lax.all_to_all(hub_part, "dom", split_axis=0, concat_axis=0, tiled=True),
        lax.all_to_all(hub_degree, "dom", split_axis=0, concat_axis=0, tiled=True),
    )
    slot_index = hub_slots[0].reshape(-1)
    summed = total.reshape(rows, width).at[slot_index].add(got_part.reshape(-1, width), mode="drop")
    degree = local_degree.reshape(rows).at[slot_index].add(got_degree.reshape(-1), mode="drop")
    scale = lax.rsqrt(degree + 1.0)
    neigh = (summed * scale[:, None]).astype(jnp.bfloat16)
    pre = jnp.dot(node_feat, self_weight, preferred_element_type=jnp.float32) + jnp.dot(
        neigh, neigh_weight, preferred_element_type=jnp.float32
    )
    layer_out = jax.nn.silu(pre).astype(jnp.bfloat16)
    sig = jax.nn.sigmoid(pre)
    slope = sig * (1.0 + pre * (1.0 - sig))
    dpre = (cotangent.astype(jnp.float32) * slope).astype(jnp.bfloat16)
    over_rows = (((0,), (0,)), ((), ()))
    self_part = lax.dot_general(node_feat, dpre, over_rows, preferred_element_type=jnp.float32)
    neigh_part = lax.dot_general(neigh, dpre, over_rows, preferred_element_type=jnp.float32)
    self_grad, neigh_grad = lax.psum((self_part, neigh_part), ("blk", "dom"))
    over_cols = (((1,), (1,)), ((), ()))
    self_back = lax.dot_general(dpre, self_weight, over_cols, preferred_element_type=jnp.float32)
    neigh_back = lax.dot_general(dpre, neigh_weight, over_cols, preferred_element_type=jnp.float32)
    grad_norm = (neigh_back * scale[:, None]).astype(jnp.bfloat16)
    padded_grad = jnp.concatenate([grad_norm, jnp.zeros((1, width), jnp.bfloat16)], axis=0)
    hub_grad = jnp.take(padded_grad, hub_slots[0], axis=0)
    back_grad = lax.all_to_all(hub_grad, "dom", split_axis=0, concat_axis=0, tiled=True)
    block_ids = jnp.arange(nblocks, dtype=jnp.int32)
    selected = (hub_source[0][:, None] == block_ids[None, :]).astype(jnp.bfloat16)
    hub_pieces = []
    for block in range(nblocks):
        masked = hub_tiles * selected[:, block][:, None, None]
        hub_pieces.append(
            jnp.einsum("ohc,ohf->cf", masked, back_grad, preferred_element_type=jnp.float32)
        )
    hub_total = jnp.stack(hub_pieces, axis=0)
    zero_block = jnp.zeros((1, tile, width), jnp.bfloat16)
    grad_blocks = jnp.concatenate([grad_norm.reshape(nblocks, tile, width), zero_block], axis=0)
    start = jnp.int32(0)
    count = rows * lax.axis_size("blk")
    pieces = []
    for offset in range(count // rows):
        panel = start // rows + offset
        term = panel_back(
            pick_panel(tiles, panel),
            pick_panel(dests, panel),
            pick_panel(sources, panel),
            grad_blocks,
            nblocks,
        )
        pieces.append(term.reshape(rows, width))
    source_total = lax.psum_scatter(
        jnp.concatenate(pieces, axis=0), "blk", scatter_dimension=0, tiled=True
    )
    feat_grad = (self_back + source_total + hub_total.reshape(rows, width)).astype(jnp.bfloat16)
    return (layer_out, feat_grad, self_grad, neigh_grad)


def solution(mesh):
    in_specs = (
        P(("blk", "dom"), None),
        P(("blk", "dom"), None),
        P(),
        P(),
        P(("blk", "dom"), None, None, None, None),
        P(("blk", "dom"), None, None),
        P(("blk", "dom"), None, None),
        P(("blk", "dom"), None, None, None),
        P(("blk", "dom"), None),
        P(("blk", "dom"), None, None),
    )
    out_specs = (P(("blk", "dom"), None), P(("blk", "dom"), None), P(), P())
    return jax.shard_map(
        per_device, mesh=mesh, in_specs=in_specs, out_specs=out_specs, check_vma=False
    )
```

profile of v0, /device:TPU:1, one launch (start us, length us, event | category | flops | bytes accessed | tf_op | source)
XLA Modules:
  0.0 491.5 jit_solution(17142006115666522738)
XLA Ops:
  7.9 2.0 convert_reduce_fusion.1
  9.9 17.6 %all-to-all-start.1 = ((f32[64,1,32]{2,1,0:T(1,128)}), f32[64,1,32]{2,1,0:T(1,128)S(1)}, u32[]{:S(2)}, u32[]{:S(2)}) async-start(f32[64,1,32]{2,1,0:T(1,128)} %bitcast.44), calls=%async_computation.1 | async-start | bytes 65536 | tf_op jit(solution)/shard_map/all_to_all | solution.py:69
  27.6 1.3 slice_reduce_fusion
  32.5 1.3 slice_reduce_fusion.1
  38.2 1.6 convert_reduce_fusion
  40.0 2.8 gather_fusion
  48.0 4.5 fusion.4
  53.1 12.9 %all-to-all-start = ((f32[64,32,256]{2,1,0:T(8,128)}), f32[64,32,256]{2,1,0:T(8,128)}, u32[]{:S(2)}, u32[]{:S(2)}) async-start(f32[64,32,256]{2,1,0:T(8,128)} %fusion.4), calls=%async_computation | async-start | bytes 4194304 | tf_op jit(solution)/shard_map/all_to_all | solution.py:68
  68.1 14.8 %scatter_fusion.1 = f32[256]{0:T(256)S(1)} fusion(f32[256]{0:T(256)S(1)} %fusion.11, s32[2048]{0:T(1024)S(1)} %bitcast.239, f32[2048]{0:T(1024)S(1)} %reshape.454), kind=kCustom, calls=%fused_computation.19 | custom fusion | flops 2048 | bytes 32768 | tf_op jit(solution)/shard_map/scatter-add | solution.py:73
  83.0 1.4 fusion.191
  102.9 1.3 convolution_add_fusion.6
  105.5 14.3 %all-to-all-done = f32[64,32,256]{2,1,0:T(8,128)} async-done(((f32[64,32,256]{2,1,0:T(8,128)}), f32[64,32,256]{2,1,0:T(8,128)}, u32[]{:S(2)}, u32[]{:S(2)}) %all-to-all-start) | async-done | bytes 2097184 | tf_op jit(solution)/shard_map/all_to_all | solution.py:68
  119.8 12.4 %scatter_fusion = f32[256,256]{1,0:T(8,128)S(1)} fusion(f32[256,256]{1,0:T(8,128)S(1)} %bitcast.217, s32[2048]{0:T(1024)S(1)} %bitcast.240, f32[2048,256]{1,0:T(8,128)} %bitcast.40), kind=kCustom, calls=%fused_computation.18 | custom fusion | flops 524288 | bytes 6299648 | tf_op jit(solution)/shard_map/scatter-add | solution.py:72
  147.8 1.1 convolution_bitcast_fusion.1
  148.9 1.1 copy.108
  151.0 1.1 convolution_bitcast_fusion
  152.1 1.2 copy.111
  159.1 7.5 %gather_fusion.1 = bf16[2048,256]{1,0:T(8,128)(2,1)S(1)} fusion(bf16[257,256]{1,0:T(8,128)(2,1)S(1)} %concatenate.11, s32[2048]{0:T(1024)S(1)} %broadcast_clamp_fusion), kind=kCustom, calls=%fused_computation.17 | custom fusion | bytes 2105344 | tf_op jit(solution)/shard_map/jit(_take)/gather | solution.py:92
  166.7 1.2 broadcast_select_fusion
  167.9 8.2 %all-to-all-start.2 = ((bf16[64,32,256]{2,1,0:T(8,128)(2,1)}), bf16[64,32,256]{2,1,0:T(8,128)(2,1)S(1)}, u32[]{:S(2)}, u32[]{:S(2)}) async-start(bf16[64,32,256]{2,1,0:T(8,128)(2,1)} %broadcast_select_fusion), calls=%async_computation.3 | async-start | bytes 2097152 | tf_op jit(solution)/shard_map/all_to_all | solution.py:93
  176.2 263.7 %all-reduce.5.cloned.1.call-done = (f32[256,256]{0,1:T(8,128)}, f32[256,256]{1,0:T(8,128)}) async-done(((f32[256,256]{0,1:T(8,128)}, f32[256,256]{1,0:T(8,128)}), (f32[256,256]{0,1:T(8,128)}, f32[256,256]{1,0:T(8,128)})) %all-reduce.5.cloned.1.call-update) | async-done | bytes 524304 | tf_op jit(solution)/shard_map/psum | solution.py:86
  439.9 1.8 copy.115
  442.7 39.7 %reduce-scatter.2.cloned.1.call-done = f32[256,256]{1,0:T(8,128)} async-done(((f32[2048,256]{1,0:T(8,128)}), f32[256,256]{1,0:T(8,128)}) %reduce-scatter.2.cloned.1.call-update) | async-done | bytes 262160 | tf_op jit(solution)/shard_map/reduce_scatter | solution.py:118
  482.4 1.8 fusion.8
  (271 shorter events, 59.7 us)
Async XLA Ops:
  7.2 125.0 %copy-start = (bf16[256,256]{1,0:T(8,128)(2,1)S(1)}, bf16[256,256]{1,0:T(8,128)(2,1)}, u32[]{:S(2)}) copy-start(bf16[256,256]{1,0:T(8,128)(2,1)} %param.17) | copy-start | bytes 393220
  7.2 32.7 %copy-start.1 = (bf16[256,256]{1,0:T(8,128)(2,1)S(1)}, bf16[256,256]{1,0:T(8,128)(2,1)}, u32[]{:S(2)}) copy-start(bf16[256,256]{1,0:T(8,128)(2,1)} %param.14) | copy-start | bytes 393220
  7.2 75.8 %all-gather.2.cloned.1.call-start = ((), (), s32[]{:S(2)}) async-start(), calls=%async_computation.4 | async-start | bytes 1179648 | tf_op jit(solution)/shard_map/all_gather | solution.py:46
  9.9 43.1 %all-to-all-start.1 = ((f32[64,1,32]{2,1,0:T(1,128)}), f32[64,1,32]{2,1,0:T(1,128)S(1)}, u32[]{:S(2)}, u32[]{:S(2)}) async-start(f32[64,1,32]{2,1,0:T(1,128)} %bitcast.44), calls=%async_computation.1 | async-start | bytes 65536 | tf_op jit(solution)/shard_map/all_to_all | solution.py:69
  28.9 11.0 %copy-start.20 = (s32[4]{0:T(128)}, s32[4]{0:T(128)S(1)}, u32[]{:S(2)}) copy-start(s32[4]{0:T(128)S(1)} %get-tuple-element.31) | copy-start | bytes 52
  28.9 11.0 %copy-start.22 = (s32[4]{0:T(128)}, s32[4]{0:T(128)S(1)}, u32[]{:S(2)}) copy-start(s32[4]{0:T(128)S(1)} %get-tuple-element.32) | copy-start | bytes 52
  28.9 11.0 %copy-start.24 = (s32[4]{0:T(128)}, s32[4]{0:T(128)S(1)}, u32[]{:S(2)}) copy-start(s32[4]{0:T(128)S(1)} %get-tuple-element.33) | copy-start | bytes 52
  28.9 11.0 %copy-start.26 = (s32[4]{0:T(128)}, s32[4]{0:T(128)S(1)}, u32[]{:S(2)}) copy-start(s32[4]{0:T(128)S(1)} %get-tuple-element.34) | copy-start | bytes 52
  28.9 11.0 %copy-start.28 = (s32[4]{0:T(128)}, s32[4]{0:T(128)S(1)}, u32[]{:S(2)}) copy-start(s32[4]{0:T(128)S(1)} %get-tuple-element.35) | copy-start | bytes 52
  28.9 11.0 %copy-start.30 = (s32[4]{0:T(128)}, s32[4]{0:T(128)S(1)}, u32[]{:S(2)}) copy-start(s32[4]{0:T(128)S(1)} %get-tuple-element.36) | copy-start | bytes 52
  28.9 13.8 %copy-start.18 = (s32[4]{0:T(128)}, s32[4]{0:T(128)S(1)}, u32[]{:S(2)}) copy-start(s32[4]{0:T(128)S(1)} %get-tuple-element.37) | copy-start | bytes 52
  33.8 12.2 %copy-start.38 = (s32[4]{0:T(128)}, s32[4]{0:T(128)S(1)}, u32[]{:S(2)}) copy-start(s32[4]{0:T(128)S(1)} %get-tuple-element.24) | copy-start | bytes 52
  33.8 12.2 %copy-start.40 = (s32[4]{0:T(128)}, s32[4]{0:T(128)S(1)}, u32[]{:S(2)}) copy-start(s32[4]{0:T(128)S(1)} %get-tuple-element.25) | copy-start | bytes 52
  33.8 12.7 %copy-start.34 = (s32[4]{0:T(128)}, s32[4]{0:T(128)S(1)}, u32[]{:S(2)}) copy-start(s32[4]{0:T(128)S(1)} %get-tuple-element.22) | copy-start | bytes 52
  33.8 12.7 %copy-start.36 = (s32[4]{0:T(128)}, s32[4]{0:T(128)S(1)}, u32[]{:S(2)}) copy-start(s32[4]{0:T(128)S(1)} %get-tuple-element.23) | copy-start | bytes 52
  53.1 66.7 %all-to-all-start = ((f32[64,32,256]{2,1,0:T(8,128)}), f32[64,32,256]{2,1,0:T(8,128)}, u32[]{:S(2)}, u32[]{:S(2)}) async-start(f32[64,32,256]{2,1,0:T(8,128)} %fusion.4), calls=%async_computation | async-start | bytes 4194304 | tf_op jit(solution)/shard_map/all_to_all | solution.py:68
  66.0 373.9 %all-reduce.5.cloned.1.call-start = ((), (), s32[]{:S(2)}) async-start(), calls=%async_computation.6 | async-start | bytes 1048576 | tf_op jit(solution)/shard_map/psum | solution.py:86
  119.8 12.4 %copy-start.8 = (f32[256,256]{1,0:T(8,128)S(1)}, f32[256,256]{1,0:T(8,128)}, u32[]{:S(2)}) copy-start(f32[256,256]{1,0:T(8,128)} %fusion.192) | copy-start | bytes 786436
  119.8 12.4 %copy-start.60 = (bf16[256,256]{1,0:T(8,128)(2,1)S(1)}, bf16[256,256]{1,0:T(8,128)(2,1)}, u32[]{:S(2)}) copy-start(bf16[256,256]{1,0:T(8,128)(2,1)} %param.15) | copy-start | bytes 393220
  153.6 328.8 %reduce-scatter.2.cloned.1.call-start = ((), (), s32[]{:S(2)}) async-start(), calls=%async_computation.5 | async-start | bytes 2359296 | tf_op jit(solution)/shard_map/reduce_scatter | solution.py:118
  166.7 9.5 %copy-start.61 = (s32[1,64]{1,0:T(1,128)S(1)}, s32[1,64]{1,0:T(1,128)}, u32[]{:S(2)}) copy-start(s32[1,64]{1,0:T(1,128)} %param.22) | copy-start | bytes 772
  167.9 273.8 %all-to-all-start.2 = ((bf16[64,32,256]{2,1,0:T(8,128)(2,1)}), bf16[64,32,256]{2,1,0:T(8,128)(2,1)S(1)}, u32[]{:S(2)}, u32[]{:S(2)}) async-start(bf16[64,32,256]{2,1,0:T(8,128)(2,1)} %broadcast_select_fusion), calls=%async_computation.3 | async-start | bytes 2097152 | tf_op jit(solution)/shard_map/all_to_all | solution.py:93
  441.7 40.7 %copy-start.7 = (bf16[256,256]{1,0:T(8,128)(2,1)S(1)}, bf16[256,256]{1,0:T(8,128)(2,1)}, u32[]{:S(2)}) copy-start(bf16[256,256]{1,0:T(8,128)(2,1)} %param.16) | copy-start | bytes 393220
  441.7 42.5 %copy-start.9 = (f32[256,256]{1,0:T(8,128)S(1)}, f32[256,256]{1,0:T(8,128)}, u32[]{:S(2)}) copy-start(f32[256,256]{1,0:T(8,128)} %get-tuple-element.87) | copy-start | bytes 786436
  (44 other events, 162.3 us)
Sparse Core Ops, SparseCore 0:
  10.1 44.8 all-gather.1
  153.7 286.1 all-reduce.4
  443.0 39.3 reduce-scatter.1
where the time goes:
time: 496 us; the launch traced here: 491 us
  waiting for transfers between devices  319 us (64%)
  local copies, waits for them, and re-layouts  47.7 us (10%)
  other arithmetic  45.2 us (9%)
  starting transfers between devices  38.9 us (8%)
  matrix products  26 us (5%)
  between operations  15.2 us (3%)
    psum x1, waiting for transfers between devices, per_device(): self_grad, neigh_grad = lax.psum((self_part, neigh_part), ('blk', 'dom'))  264 us
    reduce_scatter x1, waiting for transfers between devices, per_device(): lax.psum_scatter(jnp.concatenate(pieces, axis=0), 'blk', scatter_dimensio...  39.7 us
    all_to_all x1, starting transfers between devices, per_device(): lax.all_to_all(hub_degree, 'dom', split_axis=0, concat_axis=0, tiled=True)  17.6 us
    scatter-add x1, other arithmetic, per_device(): local_degree.reshape(rows).at[slot_index]  14.8 us
    all_to_all x1, waiting for transfers between devices, per_device(): lax.all_to_all(hub_part, 'dom', split_axis=0, concat_axis=0, tiled=True)  14.3 us
    all_to_all x1, starting transfers between devices, per_device(): lax.all_to_all(hub_part, 'dom', split_axis=0, concat_axis=0, tiled=True)  12.9 us
    scatter-add x1, other arithmetic, per_device(): total.reshape(rows, width).at[slot_index]  12.4 us
  transfers between devices with their start and end apart: 6, of which 3 were waited for; matrix products, arithmetic and copies ran while one was open for 17% of the time, Pallas kernels for 0%

commit v1 on v0

v1 whole, which is shorter than its diff:
```python
import functools

import jax
import jax.numpy as jnp
from jax import lax
from jax.experimental import pallas as pl
from jax.experimental.pallas import tpu as pltpu
from jax.sharding import PartitionSpec as P

F32 = jnp.float32
BF16 = jnp.bfloat16
LANES = 128
EXTRA = 8
NT = (((1,), (1,)), ((), ()))
NN = (((1,), (0,)), ((), ()))


def dot(a, b, dims=NN):
    return lax.dot_general(a, b, dims, preferred_element_type=F32)


def call(kernel, out_shape, n_smem, n_vmem, flops, bytes_accessed, scratch=()):
    smem = pl.BlockSpec(memory_space=pltpu.SMEM)
    vmem = pl.BlockSpec(memory_space=pltpu.VMEM)
    return pl.pallas_call(
        kernel,
        out_shape=out_shape,
        in_specs=[smem] * n_smem + [vmem] * n_vmem,
        out_specs=jax.tree.map(lambda _: vmem, out_shape),
        scratch_shapes=list(scratch),
        compiler_params=pltpu.CompilerParams(vmem_limit_bytes=40 << 20),
        cost_estimate=pl.CostEstimate(
            flops=flops, bytes_accessed=bytes_accessed, transcendentals=0
        ),
    )


def shape(dims, dtype):
    return jax.ShapeDtypeStruct(dims, dtype)


def hub_send_kernel(src, w_ref, x_ref, msg_ref, wm_ref):
    owners, hub, tile = w_ref.shape
    nblk = x_ref.shape[0] // tile
    for o in range(owners):
        w = w_ref[o]
        for b in range(nblk):
            wm_ref[o * hub : (o + 1) * hub, b * tile : (b + 1) * tile] = jnp.where(
                src[o] == b, w, jnp.zeros_like(w)
            )
    part = dot(wm_ref[...], x_ref[...]).astype(BF16)
    width = x_ref.shape[1]
    for c in range(width // LANES):
        msg_ref[:, c * hub : (c + 1) * hub, :] = part[:, c * LANES : (c + 1) * LANES].reshape(
            owners, hub, LANES
        )
    flat = w_ref[...].reshape(owners * hub, tile)
    weight = dot(jnp.ones((EXTRA, tile), BF16), flat, NT)
    high = weight.astype(BF16).astype(F32)
    row = lax.broadcasted_iota(jnp.int32, weight.shape, 0)
    pair = jnp.where(row < EXTRA // 2, high, weight - high).astype(BF16)
    per = LANES // hub
    top = (width // LANES) * hub
    for o in range(owners):
        g = o // per
        msg_ref[o, top : top + EXTRA, :] = pair[:, g * LANES : (g + 1) * LANES]


def prepare_kernel(
    dest, source, me, t_ref, wm_ref, row_ref, col_ref, x_ref, sw_ref,
    place_ref, back_ref, onehot_ref, onehot_t_ref, hub_t_ref, xt_ref, xs_ref, deg_ref, pick_ref, mask_ref,
):
    n, tile, _ = t_ref.shape
    rows, width = x_ref.shape
    nblk = rows // tile
    per = back_ref.shape[2] // tile
    for i in range(n):
        t = t_ref[i]
        d = dest[i]
        s = source[i]
        zero = jnp.zeros_like(t)
        tt = t.T
        q, k = i // per, i % per
        for b in range(nblk):
            place_ref[b * tile : (b + 1) * tile, i * tile : (i + 1) * tile] = jnp.where(d == b, t, zero)
            keep = jnp.logical_and(s == b, d < nblk)
            back_ref[q, b * tile : (b + 1) * tile, k * tile : (k + 1) * tile] = jnp.where(keep, tt, zero)
    deg_ref[...] = dot(place_ref[...], jnp.ones((n * tile, LANES), BF16))
    slots = row_ref.shape[1]
    r = lax.broadcasted_iota(jnp.int32, (rows, slots), 0)
    onehot_ref[...] = jnp.where(r == row_ref[...], 1.0, 0.0).astype(BF16)
    c = lax.broadcasted_iota(jnp.int32, (slots, rows), 1)
    onehot_t_ref[...] = jnp.where(c == col_ref[...], 1.0, 0.0).astype(BF16)
    hub_t_ref[...] = wm_ref[...].T
    xt_ref[...] = x_ref[...].T
    xs_ref[...] = dot(x_ref[...], sw_ref[...])
    senders = pick_ref.shape[1]
    hub = slots // senders
    a = lax.broadcasted_iota(jnp.int32, (slots, senders), 0)
    b = lax.broadcasted_iota(jnp.int32, (slots, senders), 1)
    pick_ref[...] = jnp.where(a // hub == b, 1.0, 0.0).astype(BF16)
    a = lax.broadcasted_iota(jnp.int32, (slots, LANES), 0)
    b = lax.broadcasted_iota(jnp.int32, (slots, LANES), 1)
    lane = lax.rem(me[0], LANES // hub) * hub + lax.rem(a, hub)
    mask_ref[...] = jnp.where(b == lane, 1.0, 0.0).astype(BF16)


def tiles_kernel(source, place_ref, halo_ref, out_ref, rhs_ref):
    tile = LANES
    n = place_ref.shape[1] // tile
    panels = halo_ref.shape[0] // (out_ref.shape[0])
    per = n // panels
    nblk = out_ref.shape[0] // tile
    for i in range(n):
        at = pl.multiple_of(((i // per) * nblk + source[i]) * tile, tile)
        rhs_ref[i * tile : (i + 1) * tile, :] = halo_ref[pl.ds(at, tile), :]
    out_ref[...] = dot(place_ref[...], rhs_ref[...])


def middle_kernel(
    got_ref, sum_ref, deg_ref, onehot_ref, onehot_t_ref, pick_ref, mask_ref,
    x_ref, xt_ref, xs_ref, cot_ref, nw_ref,
    out_ref, dpre_ref, gn_ref, wpart_ref, hubg_ref, rhs_ref,
):
    senders, _, _ = got_ref.shape
    rows, width = x_ref.shape
    slots = onehot_ref.shape[1]
    hub = slots // senders
    parts = width // LANES
    for c in range(parts):
        rhs_ref[:, c * LANES : (c + 1) * LANES] = got_ref[:, c * hub : (c + 1) * hub, :].reshape(
            slots, LANES
        )
    top = parts * hub
    for h in range(2):
        line = got_ref[:, top + h * (EXTRA // 2), :]
        spread = dot(pick_ref[...], line).astype(BF16)
        rhs_ref[:, (parts + h) * LANES : (parts + h + 1) * LANES] = spread * mask_ref[...]
    hubs = dot(onehot_ref[...], rhs_ref[...])
    summed = sum_ref[...] + hubs[:, :width]
    hub_deg = jnp.sum(
        hubs[:, width : width + LANES] + hubs[:, width + LANES : width + 2 * LANES],
        axis=1, keepdims=True,
    )
    scale = lax.rsqrt(deg_ref[:, :1] + hub_deg + 1.0)
    neigh = (summed * scale).astype(BF16)
    pre = xs_ref[...] + dot(neigh, nw_ref[...])
    sig = 1.0 / (1.0 + jnp.exp(-pre))
    out_ref[...] = (pre * sig).astype(BF16)
    dpre = (cot_ref[...].astype(F32) * (sig * (1.0 + pre * (1.0 - sig)))).astype(BF16)
    dpre_ref[...] = dpre
    gn = (dot(dpre, nw_ref[...], NT) * scale).astype(BF16)
    gn_ref[...] = gn
    hubg_ref[...] = dot(onehot_t_ref[...], gn).astype(BF16).reshape(hubg_ref.shape)
    wpart_ref[:width, :] = dot(xt_ref[...], dpre)
    wpart_ref[width:, :] = dot(neigh.T, dpre)


def panels_kernel(dest, back_ref, gn_ref, out_ref, rhs_ref):
    panels, rows, depth = back_ref.shape
    tile = LANES
    per = depth // tile
    nblk = rows // tile
    for q in range(panels):
        for k in range(per):
            d = jnp.minimum(dest[q * per + k], nblk - 1)
            at = pl.multiple_of(d * tile, tile)
            rhs_ref[k * tile : (k + 1) * tile, :] = gn_ref[pl.ds(at, tile), :]
        out_ref[q * rows : (q + 1) * rows, :] = dot(back_ref[q], rhs_ref[...])


def final_kernel(panel_ref, back_ref, hub_t_ref, dpre_ref, sw_ref, out_ref):
    slots = hub_t_ref.shape[1]
    width = out_ref.shape[1]
    total = panel_ref[...] + dot(dpre_ref[...], sw_ref[...], NT)
    total = total + dot(hub_t_ref[...], back_ref[...].reshape(slots, width))
    out_ref[...] = total.astype(BF16)


def exchange(x, axis):
    return lax.all_to_all(x, axis, split_axis=0, concat_axis=0, tiled=True)


def sum_everywhere(part, nb, nd):
    depth, width = part.shape
    got = exchange(part.reshape(nb, depth // nb, width), "blk")
    chunk = jnp.sum(got, axis=0)
    got = exchange(chunk.reshape(nd, depth // (nb * nd), width), "dom")
    small = jnp.sum(got, axis=0)
    got = exchange(jnp.broadcast_to(small[None], (nd,) + small.shape), "dom")
    chunk = got.reshape(depth // nb, width)
    got = exchange(jnp.broadcast_to(chunk[None], (nb,) + chunk.shape), "blk")
    return got.reshape(depth, width)


def per_device(
    node_feat, cotangent, self_weight, neigh_weight, tile_weights,
    tile_dest, tile_source, hub_weights, hub_source, hub_slots,
):
    rows, width = node_feat.shape
    _, panels, per, tile, _ = tile_weights.shape
    _, owners, hub, _ = hub_weights.shape
    n = panels * per
    slots = owners * hub
    high = (width // LANES) * hub + EXTRA
    halo = lax.all_gather(node_feat, "blk", axis=0, tiled=True)
    msg, placed_hub = call(
        hub_send_kernel,
        (shape((owners, high, LANES), BF16), shape((slots, rows), BF16)),
        1, 2, 2 * slots * rows * width, 4 << 20,
    )(hub_source[0], hub_weights[0], node_feat)
    got = exchange(msg, "dom")
    dest = tile_dest.reshape(n)
    source = tile_source.reshape(n)
    me = lax.axis_index("dom").astype(jnp.int32).reshape(1)
    slot_row = hub_slots.reshape(1, slots)
    slot_col = hub_slots.reshape(slots, 1)
    place, back, onehot, onehot_t, hub_t, xt, xs, deg, pick, mask = call(
        prepare_kernel,
        (
            shape((rows, n * tile), BF16),
            shape((panels, rows, per * tile), BF16),
            shape((rows, slots), BF16),
            shape((slots, rows), BF16),
            shape((rows, slots), BF16),
            shape((width, rows), BF16),
            shape((rows, width), F32),
            shape((rows, LANES), F32),
            shape((slots, owners), BF16),
            shape((slots, LANES), BF16),
        ),
        3, 6, 2 * rows * n * tile * LANES, 12 << 20,
    )(
        dest, source, me, tile_weights.reshape(n, tile, tile), placed_hub,
        slot_row, slot_col, node_feat, self_weight,
    )
    local = call(
        tiles_kernel, shape((rows, width), F32), 1, 2,
        2 * rows * n * tile * width, 4 << 20, [pltpu.VMEM((n * tile, width), BF16)],
    )(source, place, halo)
    layer_out, dpre, gn, wpart, hub_grad = call(
        middle_kernel,
        (
            shape((rows, width), BF16),
            shape((rows, width), BF16),
            shape((rows, width), BF16),
            shape((2 * width, width), F32),
            shape((owners, hub, width), BF16),
        ),
        0, 12, 6 * slots * rows * width, 8 << 20,
        [pltpu.VMEM((slots, width + 2 * LANES), BF16)],
    )(
        got, local, deg, onehot, onehot_t, pick, mask,
        node_feat, xt, xs, cotangent, neigh_weight,
    )
    back_rows = exchange(hub_grad, "dom")
    terms = call(
        panels_kernel, shape((panels * rows, width), F32), 1, 2,
        2 * rows * n * tile * width, 6 << 20, [pltpu.VMEM((per * tile, width), BF16)],
    )(dest, back, gn)
    panel_total = lax.psum_scatter(terms, "blk", scatter_dimension=0, tiled=True)
    grads = sum_everywhere(wpart, lax.axis_size("blk"), lax.axis_size("dom"))
    feat_grad = call(
        final_kernel, shape((rows, width), BF16), 0, 5,
        2 * slots * rows * width, 4 << 20,
    )(panel_total, back_rows, hub_t, dpre, self_weight)
    return layer_out, feat_grad, grads[:width], grads[width:]


def solution(mesh):
    split = P(("blk", "dom"))
    in_specs = (split, split, P(), P(), split, split, split, split, split, split)
    out_specs = (split, split, P(), P())
    return jax.shard_map(
        per_device, mesh=mesh, in_specs=in_specs, out_specs=out_specs, check_vma=False
    )
```

time: 496 us -> 222 us (0.45)
  the two profiles are of different devices: /device:TPU:1 before, /device:TPU:75 now
where the time goes in v1:
time: 222 us; the launch traced here: 221 us
  waiting for transfers between devices  69.7 us (31%)
  blocking collectives  69.3 us (31%)
  local copies, waits for them, and re-layouts  32.6 us (15%)
  starting transfers between devices  20.9 us (9%)
  between operations  14.2 us (6%)
  Pallas kernels  13.8 us (6%)
    all_to_all x4, blocking collectives, exchange(): return lax.all_to_all(x, axis, split_axis=0, concat_axis=0, tiled=True)  69.3 us
    all_to_all x2, waiting for transfers between devices, exchange(): return lax.all_to_all(x, axis, split_axis=0, concat_axis=0, tiled=True)  38.4 us
    all_gather x1, waiting for transfers between devices, per_device(): halo = lax.all_gather(node_feat, 'blk', axis=0, tiled=True)  30.6 us
    unnamed x82, local copies, waits for them, and re-layouts  30.3 us
    all_to_all x2, starting transfers between devices, exchange(): return lax.all_to_all(x, axis, split_axis=0, concat_axis=0, tiled=True)  20.8 us
  transfers between devices with their start and end apart: 4, of which 2 were waited for; matrix products, arithmetic and copies ran while one was open for 1% of the time, Pallas kernels for 2%

profile of v1, /device:TPU:75, one launch (start us, length us, event | category | flops | bytes accessed | tf_op | source)
XLA Modules:
  0.0 220.7 jit_solution(1939514810234551086)
XLA Ops:
  8.1 1.0 copy-done.34
  9.8 2.2 shard_map.129
  13.0 15.2 %all-to-all-start = ((bf16[64,72,128]{2,1,0:T(8,128)(2,1)}), bf16[64,72,128]{2,1,0:T(8,128)(2,1)S(1)}, u32[]{:S(2)}, u32[]{:S(2)}) async-start(bf16[64,72,128]{2,1,0:T(8,128)(2,1)} %get-tuple-element.21), calls=%async_computation | async-start | bytes 2359296 | tf_op jit(solution)/shard_map/all_to_all | solution.py:181
  29.1 1.1 reshape.49.col_ref
  30.6 1.2 copy-done.7
  31.8 1.2 copy-done.9
  33.0 3.2 %shard_map.130 = (bf16[256,4096]{1,0:T(8,128)(2,1)S(1)}, bf16[8,256,512]{2,1,0:T(8,128)(2,1)S(1)}, bf16[256,2048]{1,0:T(8,128)(2,1)S(1)}, bf16[2048,256]{1,0:T(8...) custom-call(s32[32]{0:T(128)S(1)} %reshape.42.dest, ...), custom_call_target="tpu_custom_call" | custom-call | flops 268435456 | bytes 12582912 | tf_op jit(solution)/shard_map/pallas_call | solution.py:218
  36.2 1.3 copy-done
  37.6 1.3 copy-done.2
  44.5 30.6 %all-gather.2.cloned.1.call-done.halo_ref = bf16[2048,256]{1,0:T(8,128)(2,1)} async-done(((bf16[256,256]{1,0:T(8,128)(2,1)}), bf16[2048,256]{1,0:T(8,128)(2,1)}) %all-gather.2.cloned.1.call-update) | async-done | bytes 1048592 | tf_op jit(solution)/shard_map/all_gather | solution.py:206
  75.1 1.6 copy-done.3
  76.7 1.2 copy-done.6
  77.9 1.3 shard_map.131.sum_ref
  79.9 1.2 copy-done.13
  82.1 1.0 copy-done.19
  88.7 3.4 %shard_map.132 = (bf16[256,256]{1,0:T(8,128)(2,1)}, bf16[256,256]{1,0:T(8,128)(2,1)S(1)}, bf16[256,256]{1,0:T(8,128)(2,1)S(1)}, f32[512,256]{1,0:T(8,128)S(1)}, bf16[64,32,256]{2,1,0:T(8,128)(2,1)}) custom-call(bf16[64,72,128]{2,1,0:T(8,128)(2,1)S(1)} %all-to-all-done.got_ref, f32[256,256]{1,0:T(8,128)S(1)} %copy-done.15, f32[256,128]{1,0:T(8,128)S(1)} %copy-done.31, ...), custom_call_target="tpu_custom_call" | custom-call | flops 805306368 | bytes 8388608 | tf_op jit(solution)/shard_map/pallas_call | solution.py:241
  93.6 2.6 %shard_map.133 = f32[2048,256]{1,0:T(8,128)} custom-call(s32[32]{0:T(128)S(1)} %reshape.42.dest, bf16[8,256,512]{2,1,0:T(8,128)(2,1)S(1)} %copy-done.1, bf16[256,256]{1,0:T(8,128)(2,1)S(1)} %get-tuple-element.33.gn_ref), custom_call_target="tpu_custom_call" | custom-call | flops 536870912 | bytes 6291456 | tf_op jit(solution)/shard_map/pallas_call | solution.py:257
  97.2 11.9 %all_to_all.30 = f32[8,64,256]{2,1,0:T(8,128)S(1)} all-to-all(f32[8,64,256]{2,1,0:T(8,128)S(1)} %bitcast.11), channel_id=1, replica_groups=mesh['blk'=8,'dom'=64] {'blk'}, dimensions={0} | all-to-all | bytes 1048576 | tf_op jit(solution)/shard_map/all_to_all | solution.py:181
  109.2 28.4 %all_to_all.31 = f32[64,1,256]{2,1,0:T(1,128)S(1)} all-to-all(f32[64,1,256]{2,1,0:T(1,128)S(1)} %reshape.48), channel_id=1, replica_groups=mesh['blk'=8,'dom'=64] {'dom'}, dimensions={0} | all-to-all | bytes 131072 | tf_op jit(solution)/shard_map/all_to_all | solution.py:181
  137.8 15.8 %all_to_all.32 = f32[64,1,256]{2,1,0:T(1,128)S(1)} all-to-all(f32[64,1,256]{2,1,0:T(1,128)S(1)} %broadcast_in_dim.6), channel_id=1, replica_groups=mesh['blk'=8,'dom'=64] {'dom'}, dimensions={0} | all-to-all | bytes 131072 | tf_op jit(solution)/shard_map/all_to_all | solution.py:181
  153.6 13.2 %all_to_all.33 = f32[8,64,256]{2,1,0:T(8,128)S(1)} all-to-all(f32[8,64,256]{2,1,0:T(8,128)S(1)} %broadcast_in_dim.15), channel_id=1, replica_groups=mesh['blk'=8,'dom'=64] {'blk'}, dimensions={0} | all-to-all | bytes 1048576 | tf_op jit(solution)/shard_map/all_to_all | solution.py:181
  166.9 5.6 %all-to-all-start.1 = ((bf16[64,32,256]{2,1,0:T(8,128)(2,1)}), bf16[64,32,256]{2,1,0:T(8,128)(2,1)S(1)}, u32[]{:S(2)}, u32[]{:S(2)}) async-start(bf16[64,32,256]{2,1,0:T(8,128)(2,1)} %get-tuple-element.34), calls=%async_computation.2 | async-start | bytes 2097152 | tf_op jit(solution)/shard_map/all_to_all | solution.py:181
  173.4 38.4 %all-to-all-done.1.back_ref = bf16[64,32,256]{2,1,0:T(8,128)(2,1)S(1)} async-done(((bf16[64,32,256]{2,1,0:T(8,128)(2,1)}), bf16[64,32,256]{2,1,0:T(8,128)(2,1)S(1)}, u32[]{:S(2)}, u32[]{:S(2)}) %all-to-all-start.1) | async-done | bytes 1048608 | tf_op jit(solution)/shard_map/all_to_all | solution.py:181
  212.7 1.1 shard_map.134
  (88 shorter events, 21.3 us)
Async XLA Ops:
  8.1 1.0 copy-start.34
  9.8 19.2 %copy-start.36 = (s32[1,64,32]{1,2,0:T(8,128)S(1)}, s32[1,64,32]{1,2,0:T(8,128)}, u32[]{:S(2)}) copy-start(s32[1,64,32]{1,2,0:T(8,128)} %param.19) | copy-start | bytes 24580
  9.8 20.5 %copy-start.37 = (s32[1,8,4]{1,2,0:T(4,128)S(1)}, s32[1,8,4]{1,2,0:T(4,128)}, u32[]{:S(2)}) copy-start(s32[1,8,4]{1,2,0:T(4,128)} %param.16) | copy-start | bytes 388
  9.8 20.6 %copy-start.38 = (s32[1,8,4]{1,2,0:T(4,128)S(1)}, s32[1,8,4]{1,2,0:T(4,128)}, u32[]{:S(2)}) copy-start(s32[1,8,4]{1,2,0:T(4,128)} %param.15) | copy-start | bytes 388
  9.8 20.8 %copy-start.5 = (bf16[256,256]{1,0:T(8,128)(2,1)S(1)}, bf16[256,256]{1,0:T(8,128)(2,1)}, u32[]{:S(2)}) copy-start(bf16[256,256]{1,0:T(8,128)(2,1)} %x_ref.5) | copy-start | bytes 393220
  9.8 20.8 %copy-start.22 = (bf16[256,256]{1,0:T(8,128)(2,1)S(1)}, bf16[256,256]{1,0:T(8,128)(2,1)}, u32[]{:S(2)}) copy-start(bf16[256,256]{1,0:T(8,128)(2,1)} %sw_ref.3) | copy-start | bytes 393220
  13.0 66.9 %all-to-all-start = ((bf16[64,72,128]{2,1,0:T(8,128)(2,1)}), bf16[64,72,128]{2,1,0:T(8,128)(2,1)S(1)}, u32[]{:S(2)}, u32[]{:S(2)}) async-start(bf16[64,72,128]{2,1,0:T(8,128)(2,1)} %get-tuple-element.21), calls=%async_computation | async-start | bytes 2359296 | tf_op jit(solution)/shard_map/all_to_all | solution.py:181
  28.2 46.9 %all-gather.2.cloned.1.call-start = ((), (), s32[]{:S(2)}) async-start(), calls=%async_computation.7 | async-start | bytes 1179648 | tf_op jit(solution)/shard_map/all_gather | solution.py:206
  28.9 182.8 %reduce-scatter.2.cloned.1.call-start = ((), (), s32[]{:S(2)}) async-start(), calls=%async_computation.8 | async-start | bytes 2359296 | tf_op jit(solution)/shard_map/reduce_scatter | solution.py:261
  30.6 1.2 copy-start.7
  31.8 1.2 copy-start.9
  36.2 1.4 copy-start
  37.6 1.3 copy-start.2
  39.9 1.0 copy-start.12
  75.1 1.6 copy-start.3
  76.7 1.2 copy-start.6
  77.9 2.0 copy-start.11
  79.9 1.2 copy-start.13
  82.1 1.0 copy-start.19
  83.1 1.0 copy-start.21
  88.7 4.9 %copy-start.1 = (bf16[8,256,512]{2,1,0:T(8,128)(2,1)S(1)}, bf16[8,256,512]{2,1,0:T(8,128)(2,1)}, u32[]{:S(2)}) copy-start(bf16[8,256,512]{2,1,0:T(8,128)(2,1)} %copy-done) | copy-start | bytes 6291460
  96.2 1.0 copy-start.17
  153.6 58.1 %copy-start.33 = (bf16[256,256]{1,0:T(8,128)(2,1)S(1)}, bf16[256,256]{1,0:T(8,128)(2,1)}, u32[]{:S(2)}) copy-start(bf16[256,256]{1,0:T(8,128)(2,1)} %copy-done.32) | copy-start | bytes 393220
  166.9 44.9 %all-to-all-start.1 = ((bf16[64,32,256]{2,1,0:T(8,128)(2,1)}), bf16[64,32,256]{2,1,0:T(8,128)(2,1)S(1)}, u32[]{:S(2)}, u32[]{:S(2)}) async-start(bf16[64,32,256]{2,1,0:T(8,128)(2,1)} %get-tuple-element.34), calls=%async_computation.2 | async-start | bytes 2097152 | tf_op jit(solution)/shard_map/all_to_all | solution.py:181
  (19 other events, 15.8 us)
Sparse Core Ops, SparseCore 0:
  31.1 43.9 all-gather.1
  96.4 46.4 reduce-scatter.1

commit v2 on v1

v2 whole, which is shorter than its diff:
```python
import jax
import jax.numpy as jnp
from jax import lax
from jax.experimental import pallas as pl
from jax.experimental.pallas import tpu as pltpu
from jax.sharding import Mesh, PartitionSpec as P

F32 = jnp.float32
BF16 = jnp.bfloat16
LANES = 128
EXTRA = 8
SMALL = 1 << 10
TILE_COST = 30_000_000_000
NT = (((1,), (1,)), ((), ()))
NN = (((1,), (0,)), ((), ()))


def dot(a, b, dims=NN):
    return lax.dot_general(a, b, dims, preferred_element_type=F32)


class Arrival:
    def __init__(self, copy, ref):
        self.copy, self.ref = copy, ref

    def __call__(self):
        if self.copy is not None:
            self.copy.wait()
            self.copy = None
        return self.ref


class Departure:
    def __init__(self, copy, ref):
        self.copy, self.ref, self.sent = copy, ref, False

    def send(self):
        self.copy.start()
        self.sent = True


def call(kernel, out_shape, scalars, arrays, scratch=(), flops=SMALL):
    outs = jax.tree.leaves(out_shape)
    n_smem, n_in, n_out = len(scalars), len(arrays), len(outs)

    def body(*refs):
        smem, refs = refs[:n_smem], refs[n_smem:]
        src, refs = refs[:n_in], refs[n_in:]
        dst, refs = refs[:n_out], refs[n_out:]
        held, refs = refs[:n_in], refs[n_in:]
        made, refs = refs[:n_out], refs[n_out:]
        in_sem, out_sem, refs = refs[0], refs[1], refs[2:]
        ins = []
        for i in range(n_in):
            copy = pltpu.make_async_copy(src[i], held[i], in_sem.at[i])
            copy.start()
            ins.append(Arrival(copy, held[i]))
        leaving = [
            Departure(pltpu.make_async_copy(made[i], dst[i], out_sem.at[i]), made[i])
            for i in range(n_out)
        ]
        kernel(*smem, *ins, *leaving, *refs)
        for x in ins:
            x()
        for x in leaving:
            if not x.sent:
                x.send()
        for x in leaving:
            x.copy.wait()

    smem = pl.BlockSpec(memory_space=pltpu.SMEM)
    hbm = pl.BlockSpec(memory_space=pltpu.MemorySpace.HBM)
    buffers = [pltpu.VMEM(x.shape, x.dtype) for x in list(arrays) + outs]
    return pl.pallas_call(
        body,
        out_shape=out_shape,
        in_specs=[smem] * n_smem + [hbm] * n_in,
        out_specs=jax.tree.map(lambda _: hbm, out_shape),
        scratch_shapes=buffers
        + [pltpu.SemaphoreType.DMA((n_in,)), pltpu.SemaphoreType.DMA((n_out,))]
        + list(scratch),
        cost_estimate=pl.CostEstimate(flops=flops, bytes_accessed=SMALL, transcendentals=0),
    )(*scalars, *arrays)


def shape(dims, dtype):
    return jax.ShapeDtypeStruct(dims, dtype)


def hub_send_kernel(src, core, weights, feat, message, placed):
    w_ref, x_ref = weights(), feat()
    msg_ref, wm_ref = message.ref, placed.ref
    owners, hub, tile = w_ref.shape
    width = x_ref.shape[1]
    nblk = x_ref.shape[0] // tile
    half = owners // 2
    for i in range(owners):
        o = (i % half) * 2 + (core[0] if i < half else 1 - core[0])
        w = w_ref[o]
        s = src[o]
        for b in range(nblk):
            wm_ref[i * hub : (i + 1) * hub, b * tile : (b + 1) * tile] = jnp.where(
                s == b, w, jnp.zeros_like(w)
            )
    placed.send()
    part = dot(wm_ref[...], x_ref[...]).astype(BF16)
    for i in range(owners):
        o = (i % half) * 2 + (core[0] if i < half else 1 - core[0])
        for c in range(width // LANES):
            msg_ref[o, c * hub : (c + 1) * hub, :] = part[
                i * hub : (i + 1) * hub, c * LANES : (c + 1) * LANES
            ]
    flat = w_ref[...].reshape(owners * hub, tile)
    weight = dot(jnp.ones((EXTRA, tile), BF16), flat, NT)
    high = weight.astype(BF16).astype(F32)
    row = lax.broadcasted_iota(jnp.int32, weight.shape, 0)
    pair = jnp.where(row < EXTRA // 2, high, weight - high).astype(BF16)
    per = LANES // hub
    top = (width // LANES) * hub
    for o in range(owners):
        g = o // per
        msg_ref[o, top : top + EXTRA, :] = pair[:, g * LANES : (g + 1) * LANES]


def prepare_kernel(
    dest, source, me, tiles, placed_hub, row, col, feat, self_weight,
    place, back, onehot, onehot_t, hub_t, feat_t, feat_self, degree, pick, mask,
):
    t_ref, x_ref = tiles(), feat()
    place_ref, back_ref = place.ref, back.ref
    n, tile, _ = t_ref.shape
    rows, width = x_ref.shape
    nblk = rows // tile
    per = back_ref.shape[2] // tile
    for i in range(n):
        t = t_ref[i]
        d = dest[i]
        s = source[i]
        zero = jnp.zeros_like(t)
        tt = t.T
        q, k = i // per, i % per
        for b in range(nblk):
            place_ref[b * tile : (b + 1) * tile, i * tile : (i + 1) * tile] = jnp.where(d == b, t, zero)
            keep = jnp.logical_and(s == b, d < nblk)
            back_ref[q, b * tile : (b + 1) * tile, k * tile : (k + 1) * tile] = jnp.where(keep, tt, zero)
    place.send()
    back.send()
    degree.ref[...] = dot(place_ref[...], jnp.ones((n * tile, LANES), BF16))
    slots = onehot.ref.shape[1]
    r = lax.broadcasted_iota(jnp.int32, (rows, slots), 0)
    onehot.ref[...] = jnp.where(r == row()[...], 1.0, 0.0).astype(BF16)
    onehot.send()
    c = lax.broadcasted_iota(jnp.int32, (slots, rows), 1)
    onehot_t.ref[...] = jnp.where(c == col()[...], 1.0, 0.0).astype(BF16)
    onehot_t.send()
    hub_t.ref[...] = placed_hub()[...].T
    feat_t.ref[...] = x_ref[...].T
    feat_self.ref[...] = dot(x_ref[...], self_weight()[...])
    senders = pick.ref.shape[1]
    hub = slots // senders
    a = lax.broadcasted_iota(jnp.int32, (slots, senders), 0)
    b = lax.broadcasted_iota(jnp.int32, (slots, senders), 1)
    pick.ref[...] = jnp.where(a // hub == b, 1.0, 0.0).astype(BF16)
    a = lax.broadcasted_iota(jnp.int32, (slots, LANES), 0)
    b = lax.broadcasted_iota(jnp.int32, (slots, LANES), 1)
    lane = lax.rem(me[0], LANES // hub) * hub + lax.rem(a, hub)
    mask.ref[...] = jnp.where(b == lane, 1.0, 0.0).astype(BF16)


def tiles_kernel(source, place, halo, out, rhs_ref):
    halo_ref = halo()
    tile = LANES
    rows = out.ref.shape[0]
    n = place.ref.shape[1] // tile
    per = n // (halo_ref.shape[0] // rows)
    nblk = rows // tile
    for i in range(n):
        at = pl.multiple_of(((i // per) * nblk + source[i]) * tile, tile)
        rhs_ref[i * tile : (i + 1) * tile, :] = halo_ref[pl.ds(at, tile), :]
    out.ref[...] = dot(place()[...], rhs_ref[...])


def middle_kernel(
    core, got, pick, mask, onehot, local, degree, feat_self, neigh_weight, cotangent,
    onehot_t, feat_t,
    layer_out, dpre_out, gn_out, wkeep, wsend, hkeep, hsend, rhs_ref,
):
    got_ref = got()
    senders, _, _ = got_ref.shape
    rows, width = layer_out.ref.shape
    slots = onehot.ref.shape[1]
    hub = slots // senders
    parts = width // LANES
    for c in range(parts):
        rhs_ref[:, c * LANES : (c + 1) * LANES] = got_ref[:, c * hub : (c + 1) * hub, :].reshape(
            slots, LANES
        )
    top = parts * hub
    pick_v, mask_v = pick()[...], mask()[...]
    for h in range(2):
        line = got_ref[:, top + h * (EXTRA // 2), :]
        spread = dot(pick_v, line).astype(BF16)
        rhs_ref[:, (parts + h) * LANES : (parts + h + 1) * LANES] = spread * mask_v
    hubs = dot(onehot()[...], rhs_ref[...])
    summed = local()[...] + hubs[:, :width]
    hub_deg = jnp.sum(
        hubs[:, width : width + LANES] + hubs[:, width + LANES : width + 2 * LANES],
        axis=1, keepdims=True,
    )
    scale = lax.rsqrt(degree()[:, :1] + hub_deg + 1.0)
    neigh = (summed * scale).astype(BF16)
    nw = neigh_weight()[...]
    pre = feat_self()[...] + dot(neigh, nw)
    sig = 1.0 / (1.0 + jnp.exp(-pre))
    dpre = (cotangent()[...].astype(F32) * (sig * (1.0 + pre * (1.0 - sig)))).astype(BF16)
    gn = (dot(dpre, nw, NT) * scale).astype(BF16)
    gn_out.ref[...] = gn
    hot = onehot_t()
    hsend.ref[...] = dot(hot[slots // 2 :, :], gn).astype(BF16).reshape(hsend.ref.shape)
    hsend.send()
    gn_out.send()
    wself = dot(feat_t()[...], dpre)
    wneigh = dot(neigh.T, dpre)
    wsend.ref[...] = jnp.where(core[0] == 0, wneigh, wself)
    wsend.send()
    wkeep.ref[...] = jnp.where(core[0] == 0, wself, wneigh)
    wkeep.send()
    hkeep.ref[...] = dot(hot[: slots // 2, :], gn).astype(BF16).reshape(hkeep.ref.shape)
    hkeep.send()
    layer_out.ref[...] = (pre * sig).astype(BF16)
    dpre_out.ref[...] = dpre


def assemble_kernel(hkeep, hgot, wkeep, wgot, out):
    far, hub, width = hkeep.ref.shape
    out_ref = out.ref
    out_ref[:, :hub, :] = hkeep()[...]
    out_ref[:, hub : 2 * hub, :] = hgot()[...]
    total = wkeep()[...] + wgot()[...]
    high = total.astype(BF16)
    low = (total - high.astype(F32)).astype(BF16)
    rows = total.shape[0] // far
    out_ref[:, 2 * hub : 2 * hub + rows, :] = high.reshape(far, rows, width)
    out_ref[:, 2 * hub + rows :, :] = low.reshape(far, rows, width)


def sum_pairs_kernel(got, out):
    got_ref = got()
    rows = out.ref.shape[1]
    top = got_ref.shape[1] - 2 * rows
    both = got_ref[:, top:, :].astype(F32)
    total = jnp.sum(both[:, :rows, :] + both[:, rows:, :], axis=0)
    out.ref[...] = jnp.broadcast_to(total[None], out.ref.shape)


def sum_kernel(got, out):
    total = jnp.sum(got()[...], axis=0)
    out.ref[...] = jnp.broadcast_to(total[None], out.ref.shape)


def panels_kernel(dest, gn, back, out, rhs_ref):
    gn_ref, back_ref = gn(), back()
    panels, rows, depth = back_ref.shape
    tile = LANES
    per = depth // tile
    nblk = rows // tile
    for q in range(panels):
        for k in range(per):
            d = jnp.minimum(dest[q * per + k], nblk - 1)
            at = pl.multiple_of(d * tile, tile)
            rhs_ref[k * tile : (k + 1) * tile, :] = gn_ref[pl.ds(at, tile), :]
        out.ref[q * rows : (q + 1) * rows, :] = dot(back_ref[q], rhs_ref[...])


def final_kernel(dpre, self_weight, panel, hub_t, back, out):
    back_ref = back()
    slots = hub_t.ref.shape[1]
    width = out.ref.shape[1]
    far = back_ref.shape[0]
    half = slots // 2
    hub = half // far
    hub_ref = hub_t()
    total = panel()[...] + dot(dpre()[...], self_weight()[...], NT)
    for i in range(2):
        rows = back_ref[:, i * hub : (i + 1) * hub, :].reshape(half, width)
        total = total + dot(hub_ref[:, i * half : (i + 1) * half], rows)
    out.ref[...] = total.astype(BF16)


def exchange(x, axis):
    return lax.all_to_all(x, axis, split_axis=0, concat_axis=0, tiled=True)


def swap_cores(x):
    return lax.ppermute(x, "core", [(0, 1), (1, 0)])


def per_device(
    node_feat, cotangent, self_weight, neigh_weight, tile_weights,
    tile_dest, tile_source, hub_weights, hub_source, hub_slots,
):
    rows, width = node_feat.shape
    _, panels, per, tile, _ = tile_weights.shape
    _, owners, hub, _ = hub_weights.shape
    n = panels * per
    slots = owners * hub
    high = (width // LANES) * hub + EXTRA
    nb = lax.axis_size("blk")
    far = lax.axis_size("far")
    core = lax.axis_index("core").astype(jnp.int32)
    halo = lax.all_gather(node_feat, "blk", axis=0, tiled=True)
    msg, placed_hub = call(
        hub_send_kernel,
        (shape((owners, high, LANES), BF16), shape((slots, rows), BF16)),
        (hub_source[0], core.reshape(1)), (hub_weights[0], node_feat),
    )
    got = exchange(msg, ("far", "core"))
    dest = tile_dest.reshape(n)
    source = tile_source.reshape(n)
    me = (lax.axis_index("far") * 2 + core).astype(jnp.int32).reshape(1)
    slot_row = hub_slots.reshape(1, slots)
    pairs = hub_slots.reshape(far, 2, hub)
    pairs = jnp.where(core == 0, pairs, pairs[:, ::-1])
    slot_col = jnp.swapaxes(pairs, 0, 1).reshape(slots, 1)
    place, back, onehot, onehot_t, hub_t, feat_t, feat_self, degree, pick, mask = call(
        prepare_kernel,
        (
            shape((rows, n * tile), BF16),
            shape((panels, rows, per * tile), BF16),
            shape((rows, slots), BF16),
            shape((slots, rows), BF16),
            shape((rows, slots), BF16),
            shape((width, rows), BF16),
            shape((rows, width), F32),
            shape((rows, LANES), F32),
            shape((slots, owners), BF16),
            shape((slots, LANES), BF16),
        ),
        (dest, source, me),
        (
            tile_weights.reshape(n, tile, tile), placed_hub, slot_row, slot_col,
            node_feat, self_weight,
        ),
    )
    local = call(
        tiles_kernel, shape((rows, width), F32), (source,), (place, halo),
        [pltpu.VMEM((n * tile, width), BF16)], TILE_COST,
    )
    square = shape((rows, width), BF16)
    grad_half = shape((width, width), F32)
    hub_half = shape((far, hub, width), BF16)
    layer_out, dpre, gn, wkeep, wsend, hkeep, hsend = call(
        middle_kernel,
        (square, square, square, grad_half, grad_half, hub_half, hub_half),
        (core.reshape(1),),
        (
            got, pick, mask, onehot, local, degree, feat_self, neigh_weight, cotangent,
            onehot_t, feat_t,
        ),
        [pltpu.VMEM((slots, width + 2 * LANES), BF16)],
    )
    chunk = width // far
    packed = call(
        assemble_kernel, shape((far, 2 * (hub + chunk), width), BF16), (),
        (hkeep, swap_cores(hsend), wkeep, swap_cores(wsend)),
    )
    back_rows = exchange(packed, "far")
    terms = call(
        panels_kernel, shape((panels * rows, width), F32), (dest,), (gn, back),
        [pltpu.VMEM((per * tile, width), BF16)],
    )
    panel_total = lax.psum_scatter(terms, "blk", scatter_dimension=0, tiled=True)
    part = call(sum_pairs_kernel, shape((nb, chunk, width), F32), (), (back_rows,))
    total = call(sum_kernel, shape((far, chunk, width), F32), (), (exchange(part, "blk"),))
    mine = exchange(total, "far").reshape(width, width)
    theirs = swap_cores(mine)
    self_grad = jnp.where(core == 0, mine, theirs)
    neigh_grad = jnp.where(core == 0, theirs, mine)
    feat_grad = call(
        final_kernel, square, (), (dpre, self_weight, panel_total, hub_t, back_rows)
    )
    return layer_out, feat_grad, self_grad, neigh_grad


def solution(mesh):
    nb, nd = mesh.devices.shape
    fine = Mesh(mesh.devices.reshape(nb, nd // 2, 2), ("blk", "far", "core"))
    split = P(("blk", "far", "core"))
    in_specs = (split, split, P(), P(), split, split, split, split, split, split)
    out_specs = (split, split, P(), P())
    return jax.shard_map(
        per_device, mesh=fine, in_specs=in_specs, out_specs=out_specs, check_vma=False
    )
```

time: 222 us -> 204 us (0.919)
  the two profiles are of different devices: /device:TPU:75 before, /device:TPU:1 now
where the time goes in v2:
time: 204 us; the launch traced here: 203 us
  blocking collectives  85.8 us (42%)
  Pallas kernels  33.8 us (17%)
  waiting for transfers between devices  30.9 us (15%)
  starting transfers between devices  30 us (15%)
  between operations  14.2 us (7%)
  local copies, waits for them, and re-layouts  7.24 us (4%)
    all_to_all x3, blocking collectives, exchange(): return lax.all_to_all(x, axis, split_axis=0, concat_axis=0, tiled=True)  85.8 us
    pallas_call x9, Pallas kernels, call(): pl.pallas_call(body, out_shape=out_shape, in_specs=[smem] * n_smem + [hbm...  33.8 us
    all_gather x1, waiting for transfers between devices, per_device(): halo = lax.all_gather(node_feat, 'blk', axis=0, tiled=True)  27.6 us
    all_to_all x1, starting transfers between devices, exchange(): return lax.all_to_all(x, axis, split_axis=0, concat_axis=0, tiled=True)  17.8 us
    ppermute x3, starting transfers between devices, swap_cores(): return lax.ppermute(x, 'core', [(0, 1), (1, 0)])  12.2 us
  transfers between devices with their start and end apart: 6, of which 3 were waited for; matrix products, arithmetic and copies ran while one was open for 3% of the time, Pallas kernels for 12%

profile of v2, /device:TPU:1, one launch (start us, length us, event | category | flops | bytes accessed | tf_op | source)
XLA Modules:
  0.0 202.9 jit_solution(16103940074359739447)
XLA Ops:
  7.9 3.6 %shard_map.129 = (bf16[64,72,128]{2,1,0:T(8,128)(2,1)}, bf16[2048,256]{1,0:T(8,128)(2,1)}) custom-call(s32[64]{0:T(128)} %bitcast.16, s32[1]{0:T(128)} %bitcast.refs_1_.refs_0_, bf16[64,32,128]{2,1,0:T(8,128)(2,1)} %bitcast.13, bf16[256,256]{1,0:T(8,128)(2,1)} %refs_7_.1), custom_call_target="tpu_custom_call" | custom-call | flops 1024 | bytes 1024 | tf_op jit(solution)/shard_map/pallas_call | solution.py:74
  11.6 17.8 %all-to-all-start = ((bf16[64,72,128]{2,1,0:T(8,128)(2,1)}), bf16[64,72,128]{2,1,0:T(8,128)(2,1)S(1)}, u32[]{:S(2)}, u32[]{:S(2)}) async-start(bf16[64,72,128]{2,1,0:T(8,128)(2,1)} %get-tuple-element.23), calls=%async_computation | async-start | bytes 2359296 | tf_op jit(solution)/shard_map/all_to_all | solution.py:291
  31.8 2.0 %reshape.45.refs_6_ = s32[2048,1]{1,0:T(8,128)} reshape(s32[2,32,32]{2,1,0:T(8,128)S(1)} %copy.23) | data formatting | bytes 16384 | tf_op jit(solution)/shard_map/reshape | solution.py:324
  33.8 7.1 %shard_map.130 = (bf16[256,4096]{1,0:T(8,128)(2,1)}, bf16[8,256,512]{2,1,0:T(8,128)(2,1)}, bf16[256,2048]{1,0:T(8,128)(2,1)}, bf16[2048,256]{1,0:T(8,128)(2,1)},...) custom-call(s32[32]{0:T(128)} %reshape.37.refs_0_, ...), custom_call_target="tpu_custom_call" | custom-call | flops 1024 | bytes 1024 | tf_op jit(solution)/shard_map/pallas_call | solution.py:74
  40.9 27.6 %all-gather.2.cloned.1.call-done.refs_2_ = bf16[2048,256]{1,0:T(8,128)(2,1)} async-done(((bf16[256,256]{1,0:T(8,128)(2,1)}), bf16[2048,256]{1,0:T(8,128)(2,1)}) %all-gather.2.cloned.1.call-update) | async-done | bytes 1048592 | tf_op jit(solution)/shard_map/all_gather | solution.py:311
  68.5 4.1 %shard_map.131.refs_5_ = f32[256,256]{1,0:T(8,128)} custom-call(s32[32]{0:T(128)} %reshape.38.refs_1_.refs_0_, bf16[256,4096]{1,0:T(8,128)(2,1)} %get-tuple-element.28.refs_1_, bf16[2048,256]{1,0:T(8,128)(2,1)} %all-gather.2.cloned.1.call-done.refs_2_), custom_call_target="tpu_custom_call" | custom-call | flops 30000001024 | bytes 1024 | tf_op jit(solution)/shard_map/pallas_call | solution.py:74
  72.6 1.0 copy-done
  73.6 5.5 %shard_map.132 = (bf16[256,256]{1,0:T(8,128)(2,1)}, bf16[256,256]{1,0:T(8,128)(2,1)}, bf16[256,256]{1,0:T(8,128)(2,1)}, f32[256,256]{1,0:T(8,128)}, f32[256,256]...) custom-call(s32[1]{0:T(128)} %bitcast.refs_1_.refs_0_, bf16[64,72,128]{2,1,0:T(8,128)(2,1)} %copy-done, ...), custom_call_target="tpu_custom_call" | custom-call | flops 1024 | bytes 1024 | tf_op jit(solution)/shard_map/pallas_call | solution.py:74
  79.1 4.1 %collective-permute-start = (bf16[32,32,256]{2,1,0:T(8,128)(2,1)}, bf16[32,32,256]{2,1,0:T(8,128)(2,1)S(1)}, u32[]{:S(2)}, u32[]{:S(2)}) collective-permute-start(bf16[32,32,256]{2,1,0:T(8,128)(2,1)} %get-tuple-element.39), channel_id=1, source_target_pairs={{0,1},{1,0},{2,3},{3,2},{4,5},{5,4},{6,7},{7,6},{8,9},{9,8},{10,11... | collective-permute-start | bytes 1572872 | tf_op jit(solution)/shard_map/ppermute | solution.py:295
  83.2 4.4 %shard_map.133 = f32[2048,256]{1,0:T(8,128)} custom-call(s32[32]{0:T(128)} %reshape.37.refs_0_, bf16[256,256]{1,0:T(8,128)(2,1)} %get-tuple-element.35.refs_1_, bf16[8,256,512]{2,1,0:T(8,128)(2,1)} %get-tuple-element.36.refs_2_), custom_call_target="tpu_custom_call" | custom-call | flops 1024 | bytes 1024 | tf_op jit(solution)/shard_map/pallas_call | solution.py:74
  87.6 0.9 copy-done.6
  88.6 1.9 collective-permute-start.1
  90.5 1.5 collective-permute-done.1.refs_3_
  92.0 0.7 copy-done.2
  92.9 2.5 %shard_map.134 = bf16[32,80,256]{2,1,0:T(8,128)(2,1)} custom-call(bf16[32,32,256]{2,1,0:T(8,128)(2,1)} %get-tuple-element.38.refs_0_, bf16[32,32,256]{2,1,0:T(8,128)(2,1)} %copy-done.1, f32[256,256]{1,0:T(8,128)} %get-tuple-element.40.refs_2_, f32[256,256]{1,0:T(8,128)} %copy-done.2), custom_call_target="tpu_custom_call" | custom-call | flops 1024 | bytes 1024 | tf_op jit(solution)/shard_map/pallas_call | solution.py:74
  95.4 59.6 %all_to_all.20.refs_4_.refs_0_ = bf16[32,80,256]{2,1,0:T(8,128)(2,1)} all-to-all(bf16[32,80,256]{2,1,0:T(8,128)(2,1)} %shard_map.134), channel_id=1, replica_groups=mesh['blk'=8,'far'=32,'core'=2] {'far'}, dimensions={0} | all-to-all | bytes 2621440 | tf_op jit(solution)/shard_map/all_to_all | solution.py:291
  155.0 2.0 shard_map.136
  157.0 9.2 %all_to_all.21.refs_0_ = f32[8,8,256]{2,1,0:T(8,128)} all-to-all(f32[8,8,256]{2,1,0:T(8,128)} %shard_map.136), channel_id=1, replica_groups=mesh['blk'=8,'far'=32,'core'=2] {'blk'}, dimensions={0} | all-to-all | bytes 131072 | tf_op jit(solution)/shard_map/all_to_all | solution.py:291
  166.2 1.6 shard_map.137
  167.8 17.1 %all_to_all.22 = f32[32,8,256]{2,1,0:T(8,128)S(1)} all-to-all(f32[32,8,256]{2,1,0:T(8,128)} %shard_map.137), channel_id=1, replica_groups=mesh['blk'=8,'far'=32,'core'=2] {'far'}, dimensions={0} | all-to-all | bytes 524288 | tf_op jit(solution)/shard_map/all_to_all | solution.py:291
  184.8 6.2 %collective-permute-start.2 = (f32[256,256]{1,0:T(8,128)S(1)}, f32[256,256]{1,0:T(8,128)S(1)}, u32[]{:S(2)}, u32[]{:S(2)}) collective-permute-start(f32[256,256]{1,0:T(8,128)S(1)} %bitcast.11), channel_id=1, source_target_pairs={{0,1},{1,0},{2,3},{3,2},{4,5},{5,4},{6,7},{7,6},{8,9},{9,8},{10,11... | collective-permute-start | bytes 786440 | tf_op jit(solution)/shard_map/ppermute | solution.py:295
  191.0 1.1 collective-permute-done.2
  192.2 0.8 broadcast_select_fusion
  193.0 3.1 %shard_map.135 = bf16[256,256]{1,0:T(8,128)(2,1)} custom-call(bf16[256,256]{1,0:T(8,128)(2,1)} %get-tuple-element.34.refs_0_, bf16[256,256]{1,0:T(8,128)(2,1)} %refs_1_.1, f32[256,256]{1,0:T(8,128)} %reduce-scatter.2.cloned.1.call-done.refs_2_, bf16[256,2048]{1,0:T(8,128)(2,1)} %get-tuple-element.37.refs_3_, bf16[32,80,256]{2,1,0:T(8,128)(2,1)} %all_to_all.20.refs_4_.refs_0_), custom_call_target="tpu_custom_call" | custom-call | flops 1024 | bytes 1024 | tf_op jit(solution)/shard_map/pallas_call | solution.py:74
  (27 shorter events, 3.4 us)
Async XLA Ops:
  7.2 61.3 %all-gather.2.cloned.1.call-start = ((), (), s32[]{:S(2)}) async-start(), calls=%async_computation.5 | async-start | bytes 1179648 | tf_op jit(solution)/shard_map/all_gather | solution.py:311
  11.5 17.9 %copy-start.4 = (s32[1,8,4]{1,2,0:T(4,128)S(1)}, s32[1,8,4]{1,2,0:T(4,128)}, u32[]{:S(2)}) copy-start(s32[1,8,4]{1,2,0:T(4,128)} %param.15) | copy-start | bytes 388
  11.5 18.6 %copy-start.5 = (s32[1,8,4]{1,2,0:T(4,128)S(1)}, s32[1,8,4]{1,2,0:T(4,128)}, u32[]{:S(2)}) copy-start(s32[1,8,4]{1,2,0:T(4,128)} %param.16) | copy-start | bytes 388
  11.5 19.4 %copy-start.3 = (s32[1,64,32]{1,2,0:T(8,128)S(1)}, s32[1,64,32]{1,2,0:T(8,128)}, u32[]{:S(2)}) copy-start(s32[1,64,32]{1,2,0:T(8,128)} %param.19) | copy-start | bytes 24580
  11.6 61.0 %all-to-all-start = ((bf16[64,72,128]{2,1,0:T(8,128)(2,1)}), bf16[64,72,128]{2,1,0:T(8,128)(2,1)S(1)}, u32[]{:S(2)}, u32[]{:S(2)}) async-start(bf16[64,72,128]{2,1,0:T(8,128)(2,1)} %get-tuple-element.23), calls=%async_computation | async-start | bytes 2359296 | tf_op jit(solution)/shard_map/all_to_all | solution.py:291
  29.3 163.6 %reduce-scatter.2.cloned.1.call-start = ((), (), s32[]{:S(2)}) async-start(), calls=%async_computation.6 | async-start | bytes 2359296 | tf_op jit(solution)/shard_map/reduce_scatter | solution.py:372
  72.6 1.0 copy-start
  79.1 12.9 %collective-permute-start = (bf16[32,32,256]{2,1,0:T(8,128)(2,1)}, bf16[32,32,256]{2,1,0:T(8,128)(2,1)S(1)}, u32[]{:S(2)}, u32[]{:S(2)}) collective-permute-start(bf16[32,32,256]{2,1,0:T(8,128)(2,1)} %get-tuple-element.39), channel_id=1, source_target_pairs={{0,1},{1,0},{2,3},{3,2},{4,5},{5,4},{6,7},{7,6},{8,9},{9,8},{10,11... | collective-permute-start | bytes 1572872 | tf_op jit(solution)/shard_map/ppermute | solution.py:295
  87.6 1.0 copy-start.6
  88.6 3.4 %collective-permute-start.1 = (f32[256,256]{1,0:T(8,128)S(1)}, f32[256,256]{1,0:T(8,128)S(1)}, u32[]{:S(2)}, u32[]{:S(2)}) collective-permute-start(f32[256,256]{1,0:T(8,128)S(1)} %copy-done.6), channel_id=1, source_target_pairs={{0,1},{1,0},{2,3},{3,2},{4,5},{5,4},{6,7},{7,6},{8,9},{9,8},{10,11... | collective-permute-start | bytes 786440 | tf_op jit(solution)/shard_map/ppermute | solution.py:295
  92.0 0.7 copy-start.2
  92.0 0.9 copy-start.1
  184.8 7.3 %collective-permute-start.2 = (f32[256,256]{1,0:T(8,128)S(1)}, f32[256,256]{1,0:T(8,128)S(1)}, u32[]{:S(2)}, u32[]{:S(2)}) collective-permute-start(f32[256,256]{1,0:T(8,128)S(1)} %bitcast.11), channel_id=1, source_target_pairs={{0,1},{1,0},{2,3},{3,2},{4,5},{5,4},{6,7},{7,6},{8,9},{9,8},{10,11... | collective-permute-start | bytes 786440 | tf_op jit(solution)/shard_map/ppermute | solution.py:295
Sparse Core Ops, SparseCore 0:
  10.1 58.3 all-gather.1
  87.8 64.8 reduce-scatter.1

commit v3 on v2

--- a/solution.py
+++ b/solution.py
@@ -39,26 +39,35 @@
         self.sent = True
 
 
-def call(kernel, out_shape, scalars, arrays, scratch=(), flops=SMALL):
+def call(kernel, out_shape, scalars, arrays, scratch=(), flops=SMALL, into=None):
     outs = jax.tree.leaves(out_shape)
+    windows = [x[1] if isinstance(x, tuple) else () for x in arrays]
+    arrays = [x[0] if isinstance(x, tuple) else x for x in arrays]
     n_smem, n_in, n_out = len(scalars), len(arrays), len(outs)
+
+    def cut(ref, window):
+        return ref.at[window] if window else ref
 
     def body(*refs):
         smem, refs = refs[:n_smem], refs[n_smem:]
         src, refs = refs[:n_in], refs[n_in:]
+        if into is not None:
+            refs = refs[1:]
         dst, refs = refs[:n_out], refs[n_out:]
         held, refs = refs[:n_in], refs[n_in:]
         made, refs = refs[:n_out], refs[n_out:]
         in_sem, out_sem, refs = refs[0], refs[1], refs[2:]
         ins = []
         for i in range(n_in):
-            copy = pltpu.make_async_copy(src[i], held[i], in_sem.at[i])
+            copy = pltpu.make_async_copy(cut(src[i], windows[i]), held[i], in_sem.at[i])
             copy.start()
             ins.append(Arrival(copy, held[i]))
-        leaving = [
-            Departure(pltpu.make_async_copy(made[i], dst[i], out_sem.at[i]), made[i])
-            for i in range(n_out)
-        ]
+        leaving = []
+        for i in range(n_out):
+            there = cut(dst[i], into[1]) if into is not None else dst[i]
+            leaving.append(
+                Departure(pltpu.make_async_copy(made[i], there, out_sem.at[i]), made[i])
+            )
         kernel(*smem, *ins, *leaving, *refs)
         for x in ins:
             x()
@@ -68,19 +77,28 @@
         for x in leaving:
             x.copy.wait()
 
+    def size(x, window):
+        dims = list(x.shape)
+        for i, part in enumerate(window):
+            dims[i] = len(range(*part.indices(dims[i])))
+        return pltpu.VMEM(tuple(dims), x.dtype)
+
     smem = pl.BlockSpec(memory_space=pltpu.SMEM)
     hbm = pl.BlockSpec(memory_space=pltpu.MemorySpace.HBM)
-    buffers = [pltpu.VMEM(x.shape, x.dtype) for x in list(arrays) + outs]
+    buffers = [size(x, w) for x, w in zip(arrays, windows)]
+    buffers += [pltpu.VMEM(x.shape, x.dtype) for x in outs]
+    extra = [] if into is None else [into[0]]
     return pl.pallas_call(
         body,
-        out_shape=out_shape,
-        in_specs=[smem] * n_smem + [hbm] * n_in,
+        out_shape=out_shape if into is None else shape(into[0].shape, into[0].dtype),
+        in_specs=[smem] * n_smem + [hbm] * (n_in + len(extra)),
         out_specs=jax.tree.map(lambda _: hbm, out_shape),
         scratch_shapes=buffers
         + [pltpu.SemaphoreType.DMA((n_in,)), pltpu.SemaphoreType.DMA((n_out,))]
         + list(scratch),
+        input_output_aliases={} if into is None else {n_smem + n_in: 0},
         cost_estimate=pl.CostEstimate(flops=flops, bytes_accessed=SMALL, transcendentals=0),
-    )(*scalars, *arrays)
+    )(*scalars, *arrays, *extra)
 
 
 def shape(dims, dtype):
@@ -167,15 +185,23 @@
     mask.ref[...] = jnp.where(b == lane, 1.0, 0.0).astype(BF16)
 
 
-def tiles_kernel(source, place, halo, out, rhs_ref):
-    halo_ref = halo()
+def tiles_kernel(source, here, place, own, beside, *rest):
+    pairs, (out, halo_ref, rhs_ref) = rest[:-3], rest[-3:]
     tile = LANES
     rows = out.ref.shape[0]
     n = place.ref.shape[1] // tile
-    per = n // (halo_ref.shape[0] // rows)
+    nx = len(pairs) + 1
+    per = n // (2 * nx)
     nblk = rows // tile
+    halo_ref[:rows, :] = own()[...]
+    halo_ref[rows : 2 * rows, :] = beside()[...]
+    for i, pair in enumerate(pairs):
+        halo_ref[2 * (i + 1) * rows : 2 * (i + 2) * rows, :] = pair()[...]
     for i in range(n):
-        at = pl.multiple_of(((i // per) * nblk + source[i]) * tile, tile)
+        y, x = (i // per) // nx, (i // per) % nx
+        back = lax.rem(here[1] - x + nx, nx)
+        other = jnp.where(here[0] == y, 0, 1)
+        at = pl.multiple_of(((back * 2 + other) * nblk + source[i]) * tile, tile)
         rhs_ref[i * tile : (i + 1) * tile, :] = halo_ref[pl.ds(at, tile), :]
     out.ref[...] = dot(place()[...], rhs_ref[...])
 
@@ -183,7 +209,7 @@
 def middle_kernel(
     core, got, pick, mask, onehot, local, degree, feat_self, neigh_weight, cotangent,
     onehot_t, feat_t,
-    layer_out, dpre_out, gn_out, wkeep, wsend, hkeep, hsend, rhs_ref,
+    layer_out, dpre_out, gn_out, wkeep, hkeep, send, rhs_ref,
 ):
     got_ref = got()
     senders, _, _ = got_ref.shape
@@ -216,13 +242,13 @@
     gn = (dot(dpre, nw, NT) * scale).astype(BF16)
     gn_out.ref[...] = gn
     hot = onehot_t()
-    hsend.ref[...] = dot(hot[slots // 2 :, :], gn).astype(BF16).reshape(hsend.ref.shape)
-    hsend.send()
-    gn_out.send()
     wself = dot(feat_t()[...], dpre)
     wneigh = dot(neigh.T, dpre)
-    wsend.ref[...] = jnp.where(core[0] == 0, wneigh, wself)
-    wsend.send()
+    put_pairs(send.ref, hub, jnp.where(core[0] == 0, wneigh, wself))
+    send.ref[:, :hub, :] = dot(hot[slots // 2 :, :], gn).astype(BF16).reshape(hkeep.ref.shape)
+    send.send()
+    gn_out.ref[...] = gn
+    gn_out.send()
     wkeep.ref[...] = jnp.where(core[0] == 0, wself, wneigh)
     wkeep.send()
     hkeep.ref[...] = dot(hot[: slots // 2, :], gn).astype(BF16).reshape(hkeep.ref.shape)
@@ -231,30 +257,43 @@
     dpre_out.ref[...] = dpre
 
 
-def assemble_kernel(hkeep, hgot, wkeep, wgot, out):
-    far, hub, width = hkeep.ref.shape
-    out_ref = out.ref
-    out_ref[:, :hub, :] = hkeep()[...]
-    out_ref[:, hub : 2 * hub, :] = hgot()[...]
-    total = wkeep()[...] + wgot()[...]
+def put_pairs(ref, top, total):
+    far, _, width = ref.shape
+    rows = total.shape[0] // far
     high = total.astype(BF16)
     low = (total - high.astype(F32)).astype(BF16)
-    rows = total.shape[0] // far
-    out_ref[:, 2 * hub : 2 * hub + rows, :] = high.reshape(far, rows, width)
-    out_ref[:, 2 * hub + rows :, :] = low.reshape(far, rows, width)
-
-
-def sum_pairs_kernel(got, out):
+    ref[:, top : top + rows, :] = high.reshape(far, rows, width)
+    ref[:, top + rows : top + 2 * rows, :] = low.reshape(far, rows, width)
+
+
+def get_pairs(ref, top):
+    far, deep, width = ref.shape
+    rows = (deep - top) // 2
+    both = ref[:, top:, :].astype(F32)
+    return both[:, :rows, :] + both[:, rows:, :]
+
+
+def assemble_kernel(hkeep, wkeep, got, out):
+    far, hub, width = hkeep.ref.shape
+    out.ref[:, :hub, :] = hkeep()[...]
     got_ref = got()
-    rows = out.ref.shape[1]
-    top = got_ref.shape[1] - 2 * rows
-    both = got_ref[:, top:, :].astype(F32)
-    total = jnp.sum(both[:, :rows, :] + both[:, rows:, :], axis=0)
-    out.ref[...] = jnp.broadcast_to(total[None], out.ref.shape)
+    out.ref[:, hub : 2 * hub, :] = got_ref[:, :hub, :]
+    total = wkeep()[...] + get_pairs(got_ref, hub).reshape(wkeep.ref.shape)
+    put_pairs(out.ref, 2 * hub, total)
+
+
+def sum_rows_kernel(got, out):
+    total = jnp.sum(get_pairs(got(), 0), axis=0)
+    rows = total.shape[0]
+    high = total.astype(BF16)
+    low = (total - high.astype(F32)).astype(BF16)
+    peers = out.ref.shape[0]
+    out.ref[:, :rows, :] = jnp.broadcast_to(high[None], (peers,) + high.shape)
+    out.ref[:, rows:, :] = jnp.broadcast_to(low[None], (peers,) + low.shape)
 
 
 def sum_kernel(got, out):
-    total = jnp.sum(got()[...], axis=0)
+    total = jnp.sum(get_pairs(got(), 0), axis=0)
     out.ref[...] = jnp.broadcast_to(total[None], out.ref.shape)
 
 
@@ -264,27 +303,25 @@
     tile = LANES
     per = depth // tile
     nblk = rows // tile
+    out.ref[:, rows:, :] = jnp.zeros((panels, out.ref.shape[1] - rows, out.ref.shape[2]), BF16)
     for q in range(panels):
         for k in range(per):
             d = jnp.minimum(dest[q * per + k], nblk - 1)
             at = pl.multiple_of(d * tile, tile)
             rhs_ref[k * tile : (k + 1) * tile, :] = gn_ref[pl.ds(at, tile), :]
-        out.ref[q * rows : (q + 1) * rows, :] = dot(back_ref[q], rhs_ref[...])
-
-
-def final_kernel(dpre, self_weight, panel, hub_t, back, out):
-    back_ref = back()
-    slots = hub_t.ref.shape[1]
-    width = out.ref.shape[1]
-    far = back_ref.shape[0]
-    half = slots // 2
-    hub = half // far
-    hub_ref = hub_t()
-    total = panel()[...] + dot(dpre()[...], self_weight()[...], NT)
+        out.ref[q, :rows, :] = dot(back_ref[q], rhs_ref[...]).astype(BF16)
+
+
+def final_kernel(dpre, self_weight, hub_t, back, terms, out):
+    total = dot(dpre()[...], self_weight()[...], NT)
+    back_ref, hub_ref = back(), hub_t()
+    far, both, width = back_ref.shape
+    hub = both // 2
+    half = far * hub
     for i in range(2):
         rows = back_ref[:, i * hub : (i + 1) * hub, :].reshape(half, width)
         total = total + dot(hub_ref[:, i * half : (i + 1) * half], rows)
-    out.ref[...] = total.astype(BF16)
+    out.ref[...] = (total + jnp.sum(terms()[...].astype(F32), axis=0)).astype(BF16)
 
 
 def exchange(x, axis):
@@ -305,23 +342,28 @@
     n = panels * per
     slots = owners * hub
     high = (width // LANES) * hub + EXTRA
-    nb = lax.axis_size("blk")
     far = lax.axis_size("far")
+    nx = lax.axis_size("x")
     core = lax.axis_index("core").astype(jnp.int32)
-    halo = lax.all_gather(node_feat, "blk", axis=0, tiled=True)
+    here = jnp.stack([lax.axis_index("y"), lax.axis_index("x")]).astype(jnp.int32)
+    beside = lax.ppermute(node_feat, "y", [(0, 1), (1, 0)])
     msg, placed_hub = call(
         hub_send_kernel,
         (shape((owners, high, LANES), BF16), shape((slots, rows), BF16)),
         (hub_source[0], core.reshape(1)), (hub_weights[0], node_feat),
     )
     got = exchange(msg, ("far", "core"))
+    pair, _ = lax.optimization_barrier((jnp.concatenate([node_feat, beside], axis=0), msg))
+    pairs = [
+        lax.ppermute(pair, "x", [(i, (i + k) % nx) for i in range(nx)]) for k in range(1, nx)
+    ]
     dest = tile_dest.reshape(n)
     source = tile_source.reshape(n)
     me = (lax.axis_index("far") * 2 + core).astype(jnp.int32).reshape(1)
     slot_row = hub_slots.reshape(1, slots)
-    pairs = hub_slots.reshape(far, 2, hub)
-    pairs = jnp.where(core == 0, pairs, pairs[:, ::-1])
-    slot_col = jnp.swapaxes(pairs, 0, 1).reshape(slots, 1)
+    order = hub_slots.reshape(far, 2, hub)
+    order = jnp.where(core == 0, order, order[:, ::-1])
+    slot_col = jnp.swapaxes(order, 0, 1).reshape(slots, 1)
     place, back, onehot, onehot_t, hub_t, feat_t, feat_self, degree, pick, mask = call(
         prepare_kernel,
         (
@@ -343,15 +385,19 @@
         ),
     )
     local = call(
-        tiles_kernel, shape((rows, width), F32), (source,), (place, halo),
-        [pltpu.VMEM((n * tile, width), BF16)], TILE_COST,
+        tiles_kernel, shape((rows, width), F32), (source, here),
+        (place, node_feat, beside, *pairs),
+        [pltpu.VMEM((panels * rows, width), BF16), pltpu.VMEM((n * tile, width), BF16)],
+        TILE_COST,
     )
     square = shape((rows, width), BF16)
-    grad_half = shape((width, width), F32)
-    hub_half = shape((far, hub, width), BF16)
-    layer_out, dpre, gn, wkeep, wsend, hkeep, hsend = call(
+    chunk = width // far
+    layer_out, dpre, gn, wkeep, hkeep, send = call(
         middle_kernel,
-        (square, square, square, grad_half, grad_half, hub_half, hub_half),
+        (
+            square, square, square, shape((width, width), F32),
+            shape((far, hub, width), BF16), shape((far, hub + 2 * chunk, width), BF16),
+        ),
         (core.reshape(1),),
         (
             got, pick, mask, onehot, local, degree, feat_self, neigh_weight, cotangent,
@@ -359,33 +405,46 @@
         ),
         [pltpu.VMEM((slots, width + 2 * LANES), BF16)],
     )
-    chunk = width // far
     packed = call(
         assemble_kernel, shape((far, 2 * (hub + chunk), width), BF16), (),
-        (hkeep, swap_cores(hsend), wkeep, swap_cores(wsend)),
-    )
-    back_rows = exchange(packed, "far")
+        (hkeep, wkeep, swap_cores(send)),
+    )
+    gathered = exchange(packed, "far")
+    gn, _ = lax.optimization_barrier((gn, packed))
     terms = call(
-        panels_kernel, shape((panels * rows, width), F32), (dest,), (gn, back),
+        panels_kernel, shape((panels, rows + 2 * chunk, width), BF16), (dest,), (gn, back),
         [pltpu.VMEM((per * tile, width), BF16)],
     )
-    panel_total = lax.psum_scatter(terms, "blk", scatter_dimension=0, tiled=True)
-    part = call(sum_pairs_kernel, shape((nb, chunk, width), F32), (), (back_rows,))
-    total = call(sum_kernel, shape((far, chunk, width), F32), (), (exchange(part, "blk"),))
+    tail = slice(rows, rows + 2 * chunk)
+    everything = slice(None)
+    terms = call(
+        sum_rows_kernel, shape((panels, 2 * chunk, width), BF16), (),
+        ((gathered, (everything, slice(2 * hub, 2 * (hub + chunk)))),),
+        into=(terms, (everything, tail)),
+    )
+    terms = exchange(terms, ("y", "x"))
+    total = call(
+        sum_kernel, shape((far, chunk, width), F32), (), ((terms, (everything, tail)),)
+    )
     mine = exchange(total, "far").reshape(width, width)
     theirs = swap_cores(mine)
     self_grad = jnp.where(core == 0, mine, theirs)
     neigh_grad = jnp.where(core == 0, theirs, mine)
+    dpre, _ = lax.optimization_barrier((dpre, total))
     feat_grad = call(
-        final_kernel, square, (), (dpre, self_weight, panel_total, hub_t, back_rows)
+        final_kernel, square, (),
+        (
+            dpre, self_weight, hub_t, (gathered, (everything, slice(0, 2 * hub))),
+            (terms, (everything, slice(0, rows))),
+        ),
     )
     return layer_out, feat_grad, self_grad, neigh_grad
 
 
 def solution(mesh):
     nb, nd = mesh.devices.shape
-    fine = Mesh(mesh.devices.reshape(nb, nd // 2, 2), ("blk", "far", "core"))
-    split = P(("blk", "far", "core"))
+    fine = Mesh(mesh.devices.reshape(2, nb // 2, nd // 2, 2), ("y", "x", "far", "core"))
+    split = P(("y", "x", "far", "core"))
     in_specs = (split, split, P(), P(), split, split, split, split, split, split)
     out_specs = (split, split, P(), P())
     return jax.shard_map(

time: 204 us -> 185 us (0.907)
  blocking collectives: 85.8 us -> 46.3 us
  starting transfers between devices: 30 us -> 51.4 us
  between operations: 14.2 us -> 0.93 us
  waiting for transfers between devices: 30.9 us -> 42.9 us
    all_to_all x1 -> x2, waiting for transfers between devices: 0.01 us -> 40.8 us  [exchange(): return lax.all_to_all(x, axis, split_axis=0, concat_axis=0, tiled=True)]
    all_to_all x3 -> x2, blocking collectives: 85.8 us -> 46.3 us  [exchange(): return lax.all_to_all(x, axis, split_axis=0, concat_axis=0, tiled=True)]
    all_gather x1 -> x0, waiting for transfers between devices: 27.6 us -> none  [per_device(): halo = lax.all_gather(node_feat, 'blk', axis=0, tiled=True)]
    ppermute x0 -> x4, starting transfers between devices: none -> 14.6 us  [the longest x3 10.5 us: per_device(): lax.ppermute(pair, 'x', [(i, (i + k) % nx) for i in range(nx)])]
    all_to_all x1 -> x2, starting transfers between devices: 17.8 us -> 27.1 us  [exchange(): return lax.all_to_all(x, axis, split_axis=0, concat_axis=0, tiled=True)]
    ppermute x3 -> x2, starting transfers between devices: 12.2 us -> 9.7 us  [swap_cores(): return lax.ppermute(x, 'core', [(0, 1), (1, 0)])]
    unnamed x17 -> x25, local copies, waits for them, and re-layouts: 3.09 us -> 4.09 us
  transfers between devices with their start and end apart: 6 -> 8, of which waited for: 3 -> 3; matrix products, arithmetic and copies ran while one was open for 3% -> 3% of each run, Pallas kernels for 12% -> 12%
where the time goes in v3:
time: 185 us; the launch traced here: 184 us
  starting transfers between devices  51.4 us (28%)
  blocking collectives  46.3 us (25%)
  waiting for transfers between devices  42.9 us (23%)
  Pallas kernels  33.1 us (18%)
  local copies, waits for them, and re-layouts  8.21 us (4%)
    all_to_all x2, blocking collectives, exchange(): return lax.all_to_all(x, axis, split_axis=0, concat_axis=0, tiled=True)  46.3 us
    all_to_all x2, waiting for transfers between devices, exchange(): return lax.all_to_all(x, axis, split_axis=0, concat_axis=0, tiled=True)  40.8 us
    pallas_call x9, Pallas kernels, call(): pl.pallas_call(body, out_shape=out_shape if into is None else shape(into[...  33.1 us
    all_to_all x2, starting transfers between devices, exchange(): return lax.all_to_all(x, axis, split_axis=0, concat_axis=0, tiled=True)  27.1 us
    ppermute x3, starting transfers between devices, per_device(): lax.ppermute(pair, 'x', [(i, (i + k) % nx) for i in range(nx)])  10.5 us
    ppermute x2, starting transfers between devices, swap_cores(): return lax.ppermute(x, 'core', [(0, 1), (1, 0)])  9.7 us
    unnamed x25, local copies, waits for them, and re-layouts  4.09 us
    ppermute x1, starting transfers between devices, per_device(): beside = lax.ppermute(node_feat, 'y', [(0, 1), (1, 0)])  4.04 us
  transfers between devices with their start and end apart: 8, of which 3 were waited for; matrix products, arithmetic and copies ran while one was open for 3% of the time, Pallas kernels for 12%

profile of v3, /device:TPU:1, one launch (start us, length us, event | category | flops | bytes accessed | tf_op | source)
XLA Modules:
  0.0 184.4 jit_solution(6707446203079992229)
XLA Ops:
  0.6 4.0 %collective-permute-start = (bf16[256,256]{1,0:T(8,128)(2,1)}, bf16[256,256]{1,0:T(8,128)(2,1)S(1)}, u32[]{:S(2)}, u32[]{:S(2)}) collective-permute-start(bf16[256,256]{1,0:T(8,128)(2,1)} %refs_3_.3), channel_id=1, source_target_pairs={{0,256},{256,0},{1,257},{257,1},{2,258},{258,2},{3,259},{259,3},{4... | collective-permute-start | bytes 393224 | tf_op jit(solution)/shard_map/ppermute | solution.py:349
  4.7 3.7 %shard_map.129 = (bf16[64,72,128]{2,1,0:T(8,128)(2,1)}, bf16[2048,256]{1,0:T(8,128)(2,1)}) custom-call(s32[64]{0:T(128)} %bitcast.18, s32[1]{0:T(128)} %bitcast.refs_1_.refs_0_, bf16[64,32,128]{2,1,0:T(8,128)(2,1)} %bitcast.15, bf16[256,256]{1,0:T(8,128)(2,1)} %refs_3_.3), custom_call_target="tpu_custom_call" | custom-call | flops 1024 | bytes 1024 | tf_op jit(solution)/shard_map/pallas_call | solution.py:91
  8.4 16.3 %all-to-all-start = ((bf16[64,72,128]{2,1,0:T(8,128)(2,1)}), bf16[64,72,128]{2,1,0:T(8,128)(2,1)S(1)}, u32[]{:S(2)}, u32[]{:S(2)}) async-start(bf16[64,72,128]{2,1,0:T(8,128)(2,1)} %get-tuple-element.25), calls=%async_computation | async-start | bytes 2359296 | tf_op jit(solution)/shard_map/all_to_all | solution.py:328
  25.7 3.1 %collective-permute-start.1 = (bf16[512,256]{1,0:T(8,128)(2,1)S(1)}, bf16[512,256]{1,0:T(8,128)(2,1)S(1)}, u32[]{:S(2)}, u32[]{:S(2)}) collective-permute-start(bf16[512,256]{1,0:T(8,128)(2,1)S(1)} %pad_maximum_fusion), channel_id=1, source_target_pairs={{0,64},{64,128},{128,192},{192,0},{1,65},{65,129},{129,193},{193,1... | collective-permute-start | bytes 786440 | tf_op jit(solution)/shard_map/ppermute | solution.py:358
  28.8 4.4 %collective-permute-start.2 = (bf16[512,256]{1,0:T(8,128)(2,1)S(1)}, bf16[512,256]{1,0:T(8,128)(2,1)S(1)}, u32[]{:S(2)}, u32[]{:S(2)}) collective-permute-start(bf16[512,256]{1,0:T(8,128)(2,1)S(1)} %pad_maximum_fusion), channel_id=1, source_target_pairs={{0,128},{64,192},{128,0},{192,64},{1,129},{65,193},{129,1},{193,65... | collective-permute-start | bytes 786440 | tf_op jit(solution)/shard_map/ppermute | solution.py:358
  33.2 3.1 %collective-permute-start.3 = (bf16[512,256]{1,0:T(8,128)(2,1)S(1)}, bf16[512,256]{1,0:T(8,128)(2,1)S(1)}, u32[]{:S(2)}, u32[]{:S(2)}) collective-permute-start(bf16[512,256]{1,0:T(8,128)(2,1)S(1)} %pad_maximum_fusion), channel_id=1, source_target_pairs={{0,192},{64,0},{128,64},{192,128},{1,193},{65,1},{129,65},{193,129... | collective-permute-start | bytes 786440 | tf_op jit(solution)/shard_map/ppermute | solution.py:358
  36.3 2.1 %reshape.45.refs_6_ = s32[2048,1]{1,0:T(8,128)} reshape(s32[2,32,32]{2,1,0:T(8,128)S(1)} %copy.24) | data formatting | bytes 16384 | tf_op jit(solution)/shard_map/reshape | solution.py:366
  39.8 7.0 %shard_map.130 = (bf16[256,4096]{1,0:T(8,128)(2,1)}, bf16[8,256,512]{2,1,0:T(8,128)(2,1)}, bf16[256,2048]{1,0:T(8,128)(2,1)}, bf16[2048,256]{1,0:T(8,128)(2,1)},...) custom-call(s32[32]{0:T(128)} %reshape.37.refs_0_, ...), custom_call_target="tpu_custom_call" | custom-call | flops 1024 | bytes 1024 | tf_op jit(solution)/shard_map/pallas_call | solution.py:91
  48.4 4.1 %shard_map.131.refs_5_ = f32[256,256]{1,0:T(8,128)} custom-call(s32[32]{0:T(128)} %reshape.38.refs_1_.refs_0_, s32[2]{0:T(128)} %pad_add_fusion.refs_1_, bf16[256,4096]{1,0:T(8,128)(2,1)} %get-tuple-element.30.refs_2_, bf16[256,256]{1,0:T(8,128)(2,1)} %refs_3_.3, bf16[256,256]{1,0:T(8,128)(2,1)} %copy-done.4, bf16[512,256]{1,0:T(8,128)(2,1)} %copy-done.8, ...), custom_call_target="tpu_custom_call" | custom-call | flops 30000001024 | bytes 1024 | tf_op jit(solution)/shard_map/pallas_call | solution.py:91
  52.6 4.1 %all-to-all-done.refs_1_ = bf16[64,72,128]{2,1,0:T(8,128)(2,1)S(1)} async-done(((bf16[64,72,128]{2,1,0:T(8,128)(2,1)}), bf16[64,72,128]{2,1,0:T(8,128)(2,1)S(1)}, u32[]{:S(2)}, u32[]{:S(2)}) %all-to-all-start) | async-done | bytes 1179680 | tf_op jit(solution)/shard_map/all_to_all | solution.py:328
  57.7 5.3 %shard_map.132 = (bf16[256,256]{1,0:T(8,128)(2,1)}, bf16[256,256]{1,0:T(8,128)(2,1)}, bf16[256,256]{1,0:T(8,128)(2,1)}, f32[256,256]{1,0:T(8,128)}, bf16[32,32,2...) custom-call(s32[1]{0:T(128)} %bitcast.refs_1_.refs_0_, bf16[64,72,128]{2,1,0:T(8,128)(2,1)} %copy-done.1, ...), custom_call_target="tpu_custom_call" | custom-call | flops 1024 | bytes 1024 | tf_op jit(solution)/shard_map/pallas_call | solution.py:91
  63.0 3.4 %collective-permute-start.4 = (bf16[32,48,256]{2,1,0:T(8,128)(2,1)}, bf16[32,48,256]{2,1,0:T(8,128)(2,1)S(1)}, u32[]{:S(2)}, u32[]{:S(2)}) collective-permute-start(bf16[32,48,256]{2,1,0:T(8,128)(2,1)} %get-tuple-element.40), channel_id=1, source_target_pairs={{0,1},{1,0},{2,3},{3,2},{4,5},{5,4},{6,7},{7,6},{8,9},{9,8},{10,11... | collective-permute-start | bytes 2359304 | tf_op jit(solution)/shard_map/ppermute | solution.py:332
  66.5 2.1 %collective-permute-done.4.refs_2_ = bf16[32,48,256]{2,1,0:T(8,128)(2,1)S(1)} collective-permute-done((bf16[32,48,256]{2,1,0:T(8,128)(2,1)}, bf16[32,48,256]{2,1,0:T(8,128)(2,1)S(1)}, u32[]{:S(2)}, u32[]{:S(2)}) %collective-permute-start.4) | collective-permute-done | bytes 786464 | tf_op jit(solution)/shard_map/ppermute | solution.py:332
  69.5 2.6 %shard_map.133 = bf16[32,80,256]{2,1,0:T(8,128)(2,1)} custom-call(bf16[32,32,256]{2,1,0:T(8,128)(2,1)} %get-tuple-element.38.refs_0_, f32[256,256]{1,0:T(8,128)} %get-tuple-element.39.refs_1_, bf16[32,48,256]{2,1,0:T(8,128)(2,1)} %copy-done.3), custom_call_target="tpu_custom_call" | custom-call | flops 1024 | bytes 1024 | tf_op jit(solution)/shard_map/pallas_call | solution.py:91
  72.1 10.8 %all-to-all-start.1 = ((bf16[32,80,256]{2,1,0:T(8,128)(2,1)}), bf16[32,80,256]{2,1,0:T(8,128)(2,1)S(1)}, u32[]{:S(2)}, u32[]{:S(2)}) async-start(bf16[32,80,256]{2,1,0:T(8,128)(2,1)} %shard_map.133), calls=%async_computation.1 | async-start | bytes 2621440 | tf_op jit(solution)/shard_map/all_to_all | solution.py:328
  82.9 4.1 %shard_map.134.refs_1_ = bf16[8,272,256]{2,1,0:T(8,128)(2,1)} custom-call(s32[32]{0:T(128)} %reshape.37.refs_0_, bf16[256,256]{1,0:T(8,128)(2,1)} %get-tuple-element.42.refs_1_, bf16[8,256,512]{2,1,0:T(8,128)(2,1)} %get-tuple-element.43.refs_2_), custom_call_target="tpu_custom_call" | custom-call | flops 1024 | bytes 1024 | tf_op jit(solution)/shard_map/pallas_call | solution.py:91
  86.9 36.7 %all-to-all-done.1.refs_0_.refs_3_ = bf16[32,80,256]{2,1,0:T(8,128)(2,1)S(1)} async-done(((bf16[32,80,256]{2,1,0:T(8,128)(2,1)}), bf16[32,80,256]{2,1,0:T(8,128)(2,1)S(1)}, u32[]{:S(2)}, u32[]{:S(2)}) %all-to-all-start.1) | async-done | bytes 1310752 | tf_op jit(solution)/shard_map/all_to_all | solution.py:328
  123.7 1.1 copy-done
  124.7 1.6 shard_map.135
  126.4 23.0 %all_to_all.20.refs_0_.refs_4_ = bf16[8,272,256]{2,1,0:T(8,128)(2,1)} all-to-all(bf16[8,272,256]{2,1,0:T(8,128)(2,1)} %shard_map.135), channel_id=1, replica_groups=mesh['y'=2,'x'=4,'far'=32,'core'=2] {'y','x'}, dimensions={0} | all-to-all | bytes 2228224 | tf_op jit(solution)/shard_map/all_to_all | solution.py:328
  149.4 1.6 shard_map.136
  151.0 23.3 %all_to_all.21 = f32[32,8,256]{2,1,0:T(8,128)S(1)} all-to-all(f32[32,8,256]{2,1,0:T(8,128)} %shard_map.136), channel_id=1, replica_groups=mesh['y'=2,'x'=4,'far'=32,'core'=2] {'far'}, dimensions={0} | all-to-all | bytes 524288 | tf_op jit(solution)/shard_map/all_to_all | solution.py:328
  174.2 6.3 %collective-permute-start.5 = (f32[256,256]{1,0:T(8,128)S(1)}, f32[256,256]{1,0:T(8,128)S(1)}, u32[]{:S(2)}, u32[]{:S(2)}) collective-permute-start(f32[256,256]{1,0:T(8,128)S(1)} %bitcast.13), channel_id=1, source_target_pairs={{0,1},{1,0},{2,3},{3,2},{4,5},{5,4},{6,7},{7,6},{8,9},{9,8},{10,11... | collective-permute-start | bytes 786440 | tf_op jit(solution)/shard_map/ppermute | solution.py:332
  180.5 3.0 %shard_map.137 = bf16[256,256]{1,0:T(8,128)(2,1)} custom-call(bf16[256,256]{1,0:T(8,128)(2,1)} %get-tuple-element.44.refs_0_, bf16[256,256]{1,0:T(8,128)(2,1)} %refs_1_.1, bf16[256,2048]{1,0:T(8,128)(2,1)} %get-tuple-element.45.refs_2_, bf16[32,80,256]{2,1,0:T(8,128)(2,1)} %copy-done, bf16[8,272,256]{2,1,0:T(8,128)(2,1)} %all_to_all.20.refs_0_.refs_4_), custom_call_target="tpu_custom_call" | custom-call | flops 1024 | bytes 1024 | tf_op jit(solution)/shard_map/pallas_call | solution.py:91
  (38 shorter events, 6.6 us)
Async XLA Ops:
  0.6 25.0 %collective-permute-start = (bf16[256,256]{1,0:T(8,128)(2,1)}, bf16[256,256]{1,0:T(8,128)(2,1)S(1)}, u32[]{:S(2)}, u32[]{:S(2)}) collective-permute-start(bf16[256,256]{1,0:T(8,128)(2,1)} %refs_3_.3), channel_id=1, source_target_pairs={{0,256},{256,0},{1,257},{257,1},{2,258},{258,2},{3,259},{259,3},{4... | collective-permute-start | bytes 393224 | tf_op jit(solution)/shard_map/ppermute | solution.py:349
  8.4 16.4 %copy-start.5 = (s32[1,64,32]{1,2,0:T(8,128)S(1)}, s32[1,64,32]{1,2,0:T(8,128)}, u32[]{:S(2)}) copy-start(s32[1,64,32]{1,2,0:T(8,128)} %param.19) | copy-start | bytes 24580
  8.4 17.2 %copy-start.2 = (bf16[256,256]{1,0:T(8,128)(2,1)S(1)}, bf16[256,256]{1,0:T(8,128)(2,1)}, u32[]{:S(2)}) copy-start(bf16[256,256]{1,0:T(8,128)(2,1)} %refs_3_.3) | copy-start | bytes 393220
  8.4 48.2 %all-to-all-start = ((bf16[64,72,128]{2,1,0:T(8,128)(2,1)}), bf16[64,72,128]{2,1,0:T(8,128)(2,1)S(1)}, u32[]{:S(2)}, u32[]{:S(2)}) async-start(bf16[64,72,128]{2,1,0:T(8,128)(2,1)} %get-tuple-element.25), calls=%async_computation | async-start | bytes 2359296 | tf_op jit(solution)/shard_map/all_to_all | solution.py:328
  24.8 13.6 %copy-start.6 = (s32[1,8,4]{1,2,0:T(4,128)S(1)}, s32[1,8,4]{1,2,0:T(4,128)}, u32[]{:S(2)}) copy-start(s32[1,8,4]{1,2,0:T(4,128)} %param.15) | copy-start | bytes 388
  24.8 14.3 %copy-start.7 = (s32[1,8,4]{1,2,0:T(4,128)S(1)}, s32[1,8,4]{1,2,0:T(4,128)}, u32[]{:S(2)}) copy-start(s32[1,8,4]{1,2,0:T(4,128)} %param.16) | copy-start | bytes 388
  25.7 21.2 %copy-start.4 = (bf16[256,256]{1,0:T(8,128)(2,1)}, bf16[256,256]{1,0:T(8,128)(2,1)S(1)}, u32[]{:S(2)}) copy-start(bf16[256,256]{1,0:T(8,128)(2,1)S(1)} %collective-permute-done.refs_4_) | copy-start | bytes 393220
  25.7 21.8 %collective-permute-start.1 = (bf16[512,256]{1,0:T(8,128)(2,1)S(1)}, bf16[512,256]{1,0:T(8,128)(2,1)S(1)}, u32[]{:S(2)}, u32[]{:S(2)}) collective-permute-start(bf16[512,256]{1,0:T(8,128)(2,1)S(1)} %pad_maximum_fusion), channel_id=1, source_target_pairs={{0,64},{64,128},{128,192},{192,0},{1,65},{65,129},{129,193},{193,1... | collective-permute-start | bytes 786440 | tf_op jit(solution)/shard_map/ppermute | solution.py:358
  28.8 18.7 %collective-permute-start.2 = (bf16[512,256]{1,0:T(8,128)(2,1)S(1)}, bf16[512,256]{1,0:T(8,128)(2,1)S(1)}, u32[]{:S(2)}, u32[]{:S(2)}) collective-permute-start(bf16[512,256]{1,0:T(8,128)(2,1)S(1)} %pad_maximum_fusion), channel_id=1, source_target_pairs={{0,128},{64,192},{128,0},{192,64},{1,129},{65,193},{129,1},{193,65... | collective-permute-start | bytes 786440 | tf_op jit(solution)/shard_map/ppermute | solution.py:358
  33.2 14.4 %collective-permute-start.3 = (bf16[512,256]{1,0:T(8,128)(2,1)S(1)}, bf16[512,256]{1,0:T(8,128)(2,1)S(1)}, u32[]{:S(2)}, u32[]{:S(2)}) collective-permute-start(bf16[512,256]{1,0:T(8,128)(2,1)S(1)} %pad_maximum_fusion), channel_id=1, source_target_pairs={{0,192},{64,0},{128,64},{192,128},{1,193},{65,1},{129,65},{193,129... | collective-permute-start | bytes 786440 | tf_op jit(solution)/shard_map/ppermute | solution.py:358
  47.5 0.7 copy-start.8
  47.5 0.8 copy-start.9
  47.6 0.9 copy-start.10
  56.7 1.0 copy-start.1
  63.0 5.5 %collective-permute-start.4 = (bf16[32,48,256]{2,1,0:T(8,128)(2,1)}, bf16[32,48,256]{2,1,0:T(8,128)(2,1)S(1)}, u32[]{:S(2)}, u32[]{:S(2)}) collective-permute-start(bf16[32,48,256]{2,1,0:T(8,128)(2,1)} %get-tuple-element.40), channel_id=1, source_target_pairs={{0,1},{1,0},{2,3},{3,2},{4,5},{5,4},{6,7},{7,6},{8,9},{9,8},{10,11... | collective-permute-start | bytes 2359304 | tf_op jit(solution)/shard_map/ppermute | solution.py:332
  68.6 0.9 copy-start.3
  72.1 51.6 %all-to-all-start.1 = ((bf16[32,80,256]{2,1,0:T(8,128)(2,1)}), bf16[32,80,256]{2,1,0:T(8,128)(2,1)S(1)}, u32[]{:S(2)}, u32[]{:S(2)}) async-start(bf16[32,80,256]{2,1,0:T(8,128)(2,1)} %shard_map.133), calls=%async_computation.1 | async-start | bytes 2621440 | tf_op jit(solution)/shard_map/all_to_all | solution.py:328
  123.7 1.1 copy-start
  174.2 9.3 %collective-permute-start.5 = (f32[256,256]{1,0:T(8,128)S(1)}, f32[256,256]{1,0:T(8,128)S(1)}, u32[]{:S(2)}, u32[]{:S(2)}) collective-permute-start(f32[256,256]{1,0:T(8,128)S(1)} %bitcast.13), channel_id=1, source_target_pairs={{0,1},{1,0},{2,3},{3,2},{4,5},{5,4},{6,7},{7,6},{8,9},{9,8},{10,11... | collective-permute-start | bytes 786440 | tf_op jit(solution)/shard_map/ppermute | solution.py:332

commit v4 on v3

v4 whole, which is shorter than its diff:
```python
import jax
import jax.numpy as jnp
from jax import lax
from jax.experimental import pallas as pl
from jax.experimental.pallas import tpu as pltpu
from jax.sharding import Mesh, PartitionSpec as P

F32 = jnp.float32
BF16 = jnp.bfloat16
LANES = 128
EXTRA = 8
PIECES = 4
SMALL = 1 << 10
TILE_COST = 30_000_000_000
NT = (((1,), (1,)), ((), ()))
NN = (((1,), (0,)), ((), ()))
ALL = slice(None)


def dot(a, b, dims=NN):
    return lax.dot_general(a, b, dims, preferred_element_type=F32)


def shape(dims, dtype):
    return jax.ShapeDtypeStruct(dims, dtype)


class Arrival:
    def __init__(self, copy, ref):
        self.copy, self.ref = copy, ref

    def __call__(self):
        if self.copy is not None:
            self.copy.wait()
            self.copy = None
        return self.ref


class Departure:
    def __init__(self, src, dst, sem):
        self.src, self.dst, self.sem = src, dst, sem
        self.ref, self.copies = src, []

    def send(self, piece=0, pieces=1):
        n = self.src.shape[0] // pieces
        rows = pl.ds(piece * n, n)
        copy = pltpu.make_async_copy(self.src.at[rows], self.dst.at[rows], self.sem.at[piece])
        copy.start()
        self.copies.append(copy)


def call(kernel, outs, scalars, arrays, scratch=(), flops=SMALL, into=None, pieces=1):
    def split(x):
        return x if isinstance(x, tuple) else (x, ())

    def window_shape(x, window):
        dims = list(x.shape)
        for i, part in enumerate(window):
            dims[i] = len(range(*part.indices(dims[i])))
        return pltpu.VMEM(tuple(dims), x.dtype)

    def cut(ref, window):
        return ref.at[window] if window else ref

    arrays, windows = zip(*[split(x) for x in arrays])
    outs = [split(x) for x in outs] if into is None else [into]
    n_smem, n_in, n_out = len(scalars), len(arrays), len(outs)

    def body(*refs):
        smem, refs = refs[:n_smem], refs[n_smem:]
        src, refs = refs[:n_in], refs[n_in:]
        if into is not None:
            refs = refs[1:]
        dst, refs = refs[:n_out], refs[n_out:]
        held, refs = refs[:n_in], refs[n_in:]
        made, refs = refs[:n_out], refs[n_out:]
        in_sem, out_sem, refs = refs[0], refs[1], refs[2:]
        ins = []
        for i in range(n_in):
            copy = pltpu.make_async_copy(cut(src[i], windows[i]), held[i], in_sem.at[i])
            copy.start()
            ins.append(Arrival(copy, held[i]))
        leaving = [
            Departure(made[i], cut(dst[i], outs[i][1]), out_sem.at[i]) for i in range(n_out)
        ]
        kernel(*smem, *ins, *leaving, *refs)
        for x in ins:
            x()
        for x in leaving:
            if not x.copies:
                x.send()
        for x in leaving:
            for copy in x.copies:
                copy.wait()

    smem = pl.BlockSpec(memory_space=pltpu.SMEM)
    hbm = pl.BlockSpec(memory_space=pltpu.MemorySpace.HBM)
    extra = [] if into is None else [into[0]]
    result = pl.pallas_call(
        body,
        out_shape=[shape(x.shape, x.dtype) for x, _ in outs],
        in_specs=[smem] * n_smem + [hbm] * (n_in + len(extra)),
        out_specs=[hbm] * n_out,
        scratch_shapes=[window_shape(x, w) for x, w in zip(arrays, windows)]
        + [window_shape(x, w) for x, w in outs]
        + [pltpu.SemaphoreType.DMA((n_in,)), pltpu.SemaphoreType.DMA((n_out, pieces))]
        + list(scratch),
        input_output_aliases={} if into is None else {n_smem + n_in: 0},
        cost_estimate=pl.CostEstimate(flops=flops, bytes_accessed=SMALL, transcendentals=0),
    )(*scalars, *arrays, *extra)
    return result if n_out > 1 else result[0]


def by_source(w, source, nblk):
    return [jnp.where(source == b, w, jnp.zeros_like(w)) for b in range(nblk)]


def hub_send_kernel(src, weights, feat, message, wm_ref):
    w_ref = weights()
    msg_ref = message.ref
    owners, hub, tile = w_ref.shape
    per = LANES // hub
    flat = w_ref[...].reshape(owners * hub, tile)
    weight = dot(jnp.ones((EXTRA, tile), BF16), flat, NT)
    high = weight.astype(BF16).astype(F32)
    row = lax.broadcasted_iota(jnp.int32, weight.shape, 0)
    pair = jnp.where(row < EXTRA // 2, high, weight - high).astype(BF16)
    x_ref = feat()
    rows, width = x_ref.shape
    nblk = rows // tile
    top = (width // LANES) * hub
    n = owners // PIECES
    for p in range(PIECES):
        for o in range(p * n, (p + 1) * n):
            for b, part in enumerate(by_source(w_ref[o], src[o], nblk)):
                wm_ref[o * hub : (o + 1) * hub, b * tile : (b + 1) * tile] = part
        at = slice(p * n * hub, (p + 1) * n * hub)
        part = dot(wm_ref[at, :], x_ref[...]).astype(BF16)
        for c in range(width // LANES):
            msg_ref[p * n : (p + 1) * n, c * hub : (c + 1) * hub, :] = part[
                :, c * LANES : (c + 1) * LANES
            ].reshape(n, hub, LANES)
        for o in range(p * n, (p + 1) * n):
            g = o // per
            msg_ref[o, top : top + EXTRA, :] = pair[:, g * LANES : (g + 1) * LANES]
        message.send(p, PIECES)


def prepare_kernel(
    dest, source, core, hub_source, tiles, feat, row, col, weights, self_weight,
    place, back, onehot, onehot_t, hub_t, feat_t, feat_self, degree, wm_ref,
):
    t_ref = tiles()
    place_ref, back_ref = place.ref, back.ref
    n, tile, _ = t_ref.shape
    rows = place_ref.shape[0]
    nblk = rows // tile
    per = back_ref.shape[2] // tile
    for i in range(n):
        t = t_ref[i]
        d = dest[i]
        s = source[i]
        zero = jnp.zeros_like(t)
        tt = t.T
        q, k = i // per, i % per
        for b in range(nblk):
            place_ref[b * tile : (b + 1) * tile, i * tile : (i + 1) * tile] = jnp.where(d == b, t, zero)
            keep = jnp.logical_and(s == b, d < nblk)
            back_ref[q, b * tile : (b + 1) * tile, k * tile : (k + 1) * tile] = jnp.where(keep, tt, zero)
    place.send()
    back.send()
    degree.ref[...] = dot(place_ref[...], jnp.ones((n * tile, LANES), BF16))
    degree.send()
    slots = onehot.ref.shape[1]
    r = lax.broadcasted_iota(jnp.int32, (rows, slots), 0)
    onehot.ref[...] = jnp.where(r == row()[...], 1.0, 0.0).astype(BF16)
    onehot.send()
    c = lax.broadcasted_iota(jnp.int32, (slots, rows), 1)
    onehot_t.ref[...] = jnp.where(c == col()[...], 1.0, 0.0).astype(BF16)
    onehot_t.send()
    w_ref = weights()
    owners, hub, _ = w_ref.shape
    half = owners // 2
    for i in range(owners):
        o = (i % half) * 2 + (core[0] if i < half else 1 - core[0])
        for b, part in enumerate(by_source(w_ref[o], hub_source[o], nblk)):
            wm_ref[i * hub : (i + 1) * hub, b * tile : (b + 1) * tile] = part
    hub_t.ref[...] = wm_ref[...].T
    hub_t.send()
    x = feat()[...]
    feat_t.ref[...] = x.T
    feat_self.ref[...] = dot(x, self_weight()[...])


def tiles_kernel(source, here, own, beside, *rest):
    pairs, (place, out, halo_ref, rhs_ref) = rest[:-4], rest[-4:]
    tile = LANES
    rows = out.ref.shape[0]
    n = place.ref.shape[1] // tile
    nx = len(pairs) + 1
    per = n // (2 * nx)
    nblk = rows // tile
    halo_ref[:rows, :] = own()[...]
    halo_ref[rows : 2 * rows, :] = beside()[...]
    for i, pair in enumerate(pairs):
        halo_ref[2 * (i + 1) * rows : 2 * (i + 2) * rows, :] = pair()[...]
    for i in range(n):
        y, x = (i // per) // nx, (i // per) % nx
        back = lax.rem(here[1] - x + nx, nx)
        other = jnp.where(here[0] == y, 0, 1)
        at = pl.multiple_of(((back * 2 + other) * nblk + source[i]) * tile, tile)
        rhs_ref[i * tile : (i + 1) * tile, :] = halo_ref[pl.ds(at, tile), :]
    out.ref[...] = dot(place()[...], rhs_ref[...])


def middle_kernel(
    core, me, got, onehot, local, degree, feat_self, neigh_weight, cotangent, feat_t, onehot_t,
    layer_out, dpre_out, gn_out, wkeep, packed, send, rhs_ref,
):
    got_ref = got()
    senders = got_ref.shape[0]
    rows, width = layer_out.ref.shape
    slots = onehot.ref.shape[1]
    hub = slots // senders
    parts = width // LANES
    for c in range(parts):
        rhs_ref[:, c * LANES : (c + 1) * LANES] = got_ref[:, c * hub : (c + 1) * hub, :].reshape(
            slots, LANES
        )
    top = parts * hub
    slot = lax.broadcasted_iota(jnp.int32, (1, hub, LANES), 1)
    lane = lax.broadcasted_iota(jnp.int32, (1, hub, LANES), 2)
    mine = lane == lax.rem(me[0], LANES // hub) * hub + slot
    for h in range(2):
        line = got_ref[:, top + h * (EXTRA // 2) : top + h * (EXTRA // 2) + 1, :].astype(F32)
        spread = jnp.where(mine, jnp.broadcast_to(line, (senders, hub, LANES)), 0.0)
        rhs_ref[:, (parts + h) * LANES : (parts + h + 1) * LANES] = spread.astype(BF16).reshape(
            slots, LANES
        )
    hubs = dot(onehot()[...], rhs_ref[...])
    summed = local()[...] + hubs[:, :width]
    hub_deg = jnp.sum(
        hubs[:, width : width + LANES] + hubs[:, width + LANES : width + 2 * LANES],
        axis=1, keepdims=True,
    )
    scale = lax.rsqrt(degree()[:, :1] + hub_deg + 1.0)
    neigh = (summed * scale).astype(BF16)
    nw = neigh_weight()[...]
    pre = feat_self()[...] + dot(neigh, nw)
    sig = 1.0 / (1.0 + jnp.exp(-pre))
    dpre = (cotangent()[...].astype(F32) * (sig * (1.0 + pre * (1.0 - sig)))).astype(BF16)
    gn = (dot(dpre, nw, NT) * scale).astype(BF16)
    wself = dot(feat_t()[...], dpre)
    wneigh = dot(neigh.T, dpre)
    put_pairs(send.ref, hub, jnp.where(core[0] == 0, wneigh, wself))
    hot = onehot_t()
    send.ref[:, :hub, :] = dot(hot[slots // 2 :, :], gn).astype(BF16).reshape(packed.ref.shape)
    send.send()
    packed.ref[...] = dot(hot[: slots // 2, :], gn).astype(BF16).reshape(packed.ref.shape)
    packed.send()
    wkeep.ref[...] = jnp.where(core[0] == 0, wself, wneigh)
    wkeep.send()
    gn_out.ref[...] = gn
    gn_out.send()
    layer_out.ref[...] = (pre * sig).astype(BF16)
    dpre_out.ref[...] = dpre


def put_pairs(ref, top, total):
    far, _, width = ref.shape
    rows = total.shape[0] // far
    high = total.astype(BF16)
    low = (total - high.astype(F32)).astype(BF16)
    ref[:, top : top + rows, :] = high.reshape(far, rows, width)
    ref[:, top + rows : top + 2 * rows, :] = low.reshape(far, rows, width)


def get_pairs(ref, top):
    far, deep, width = ref.shape
    rows = (deep - top) // 2
    both = ref[:, top:, :].astype(F32)
    return both[:, :rows, :] + both[:, rows:, :]


def assemble_kernel(got, wkeep, out):
    got_ref = got()
    far, deep, width = got_ref.shape
    hub = deep - 2 * (wkeep.ref.shape[0] // far)
    out.ref[:, :hub, :] = got_ref[:, :hub, :]
    total = wkeep()[...] + get_pairs(got_ref, hub).reshape(wkeep.ref.shape)
    put_pairs(out.ref, hub, total)


def sum_pairs_kernel(got, out):
    total = jnp.sum(get_pairs(got(), 0), axis=0)
    out.ref[...] = jnp.broadcast_to(total[None], out.ref.shape)


def sum_kernel(got, out):
    total = jnp.sum(got()[...], axis=0)
    out.ref[...] = jnp.broadcast_to(total[None], out.ref.shape)


def panels_kernel(dest, here, gn, back, *rest):
    outs, rhs_ref = rest[:-1], rest[-1]
    gn_ref, back_ref = gn(), back()
    panels, rows, depth = back_ref.shape
    tile = LANES
    per = depth // tile
    nblk = rows // tile
    nx = panels // 2
    for step in list(range(1, nx)) + [0]:
        out = outs[step]
        x = lax.rem(here[1] + step, nx)
        for other in range(2):
            q = (here[0] if other == 0 else 1 - here[0]) * nx + x
            for k in range(per):
                d = jnp.minimum(dest[q * per + k], nblk - 1)
                at = pl.multiple_of(d * tile, tile)
                rhs_ref[k * tile : (k + 1) * tile, :] = gn_ref[pl.ds(at, tile), :]
            part = dot(back_ref[q], rhs_ref[...])
            out.ref[other * rows : (other + 1) * rows, :] = part.astype(out.ref.dtype)
        out.send()


def sum_panels_kernel(*rest):
    terms, (here, there) = rest[:-2], rest[-2:]
    rows = here.ref.shape[0]
    total = terms[0]()[...].astype(F32)
    for term in terms[1:]:
        total = total + term()[...].astype(F32)
    there.ref[...] = total[rows:]
    there.send()
    here.ref[...] = total[:rows]


def final_kernel(dpre, self_weight, hub_t, back, here, got, out):
    total = dot(dpre()[...], self_weight()[...], NT)
    back_ref, hub_ref = back(), hub_t()
    far, both, width = back_ref.shape
    hub = both // 2
    half = far * hub
    for i in range(2):
        rows = back_ref[:, i * hub : (i + 1) * hub, :].reshape(half, width)
        total = total + dot(hub_ref[:, i * half : (i + 1) * half], rows)
    out.ref[...] = (total + here()[...] + got()[...]).astype(BF16)


def exchange(x, axis):
    return lax.all_to_all(x, axis, split_axis=0, concat_axis=0, tiled=True)


def swap(x, axis):
    return lax.ppermute(x, axis, [(0, 1), (1, 0)])


def along_x(x, step, nx):
    return lax.ppermute(x, "x", [(i, (i + step) % nx) for i in range(nx)])


def after(x, other):
    return lax.optimization_barrier((x, other))[0]


def per_device(
    node_feat, cotangent, self_weight, neigh_weight, tile_weights,
    tile_dest, tile_source, hub_weights, hub_source, hub_slots,
):
    rows, width = node_feat.shape
    _, panels, per, tile, _ = tile_weights.shape
    _, owners, hub, _ = hub_weights.shape
    n = panels * per
    slots = owners * hub
    high = (width // LANES) * hub + EXTRA
    far = lax.axis_size("far")
    nx = lax.axis_size("x")
    chunk = width // far
    core = lax.axis_index("core").astype(jnp.int32)
    core1 = core.reshape(1)
    me = (lax.axis_index("far") * 2 + core).astype(jnp.int32).reshape(1)
    here = jnp.stack([lax.axis_index("y"), lax.axis_index("x")]).astype(jnp.int32)
    square = shape((rows, width), BF16)
    square32 = shape((rows, width), F32)
    beside = swap(node_feat, "y")
    msg = call(
        hub_send_kernel, [shape((owners, high, LANES), BF16)], (hub_source[0],),
        (hub_weights[0], node_feat), [pltpu.VMEM((slots, rows), BF16)], pieces=PIECES,
    )
    got = exchange(msg, ("far", "core"))
    pair = after(jnp.concatenate([node_feat, beside], axis=0), msg)
    pairs = [along_x(pair, k, nx) for k in range(1, nx)]
    dest = tile_dest.reshape(n)
    source = tile_source.reshape(n)
    slot_row = hub_slots.reshape(1, slots)
    order = hub_slots.reshape(far, 2, hub)
    order = jnp.where(core == 0, order, order[:, ::-1])
    slot_col = jnp.swapaxes(order, 0, 1).reshape(slots, 1)
    place, back, onehot, onehot_t, hub_t, feat_t, feat_self, degree = call(
        prepare_kernel,
        [
            shape((rows, n * tile), BF16),
            shape((panels, rows, per * tile), BF16),
            shape((rows, slots), BF16),
            shape((slots, rows), BF16),
            shape((rows, slots), BF16),
            square,
            square32,
            shape((rows, LANES), F32),
        ],
        (dest, source, core1, hub_source[0]),
        (
            tile_weights.reshape(n, tile, tile), after(node_feat, msg), slot_row, slot_col,
            hub_weights[0], self_weight,
        ),
        [pltpu.VMEM((slots, rows), BF16)],
    )
    local = call(
        tiles_kernel, [square32], (source, here), (node_feat, beside, *pairs, place),
        [pltpu.VMEM((panels * rows, width), BF16), pltpu.VMEM((n * tile, width), BF16)],
        TILE_COST,
    )
    deep = 2 * (hub + chunk)
    layer_out, dpre, gn, wkeep, packed, send = call(
        middle_kernel,
        [
            square, square, square, square32,
            (shape((far, deep, width), BF16), (ALL, slice(0, hub))),
            shape((far, hub + 2 * chunk, width), BF16),
        ],
        (core1, me),
        (
            got, onehot, local, degree, feat_self, neigh_weight, cotangent, feat_t, onehot_t,
        ),
        [pltpu.VMEM((slots, width + 2 * LANES), BF16)],
    )
    packed = call(
        assemble_kernel, [], (), (swap(send, "core"), wkeep),
        into=(packed, (ALL, slice(hub, deep))),
    )
    gathered = exchange(packed, "far")
    terms = call(
        panels_kernel, [shape((2 * rows, width), F32)] + [shape((2 * rows, width), BF16)] * (nx - 1),
        (dest, here), (after(gn, packed), back), [pltpu.VMEM((per * tile, width), BF16)],
    )
    terms = terms if nx > 1 else [terms]
    arrived = [along_x(terms[k], k, nx) for k in range(1, nx)]
    panel_here, panel_there = call(sum_panels_kernel, [square32] * 2, (), (terms[0], *arrived))
    panel_got = swap(panel_there, "y")
    part = call(
        sum_pairs_kernel, [shape((panels, chunk, width), F32)], (),
        ((after(gathered, arrived), (ALL, slice(2 * hub, deep))),),
    )
    total = call(
        sum_kernel, [shape((far, chunk, width), F32)], (), (exchange(part, ("y", "x")),)
    )
    mine = exchange(total, "far").reshape(width, width)
    feat_grad = call(
        final_kernel, [square], (),
        (
            after(dpre, total), self_weight, hub_t, (gathered, (ALL, slice(0, 2 * hub))),
            panel_here, panel_got,
        ),
    )
    theirs = swap(after(mine, feat_grad), "core")
    self_grad = jnp.where(core == 0, mine, theirs)
    neigh_grad = jnp.where(core == 0, theirs, mine)
    return layer_out, feat_grad, self_grad, neigh_grad


def solution(mesh):
    nb, nd = mesh.devices.shape
    fine = Mesh(mesh.devices.reshape(2, nb // 2, nd // 2, 2), ("y", "x", "far", "core"))
    split = P(("y", "x", "far", "core"))
    in_specs = (split, split, P(), P(), split, split, split, split, split, split)
    out_specs = (split, split, P(), P())
    return jax.shard_map(
        per_device, mesh=fine, in_specs=in_specs, out_specs=out_specs, check_vma=False
    )
```

time: 185 us -> 175 us (0.946)
  blocking collectives: 46.3 us -> 15.7 us
  starting transfers between devices: 51.4 us -> 73.1 us
    all_to_all x2 -> x1, blocking collectives: 46.3 us -> 15.7 us  [exchange(): return lax.all_to_all(x, axis, split_axis=0, concat_axis=0, tiled=True)]
    all_to_all x2 -> x3, waiting for transfers between devices: 40.8 us -> 23.2 us  [exchange(): return lax.all_to_all(x, axis, split_axis=0, concat_axis=0, tiled=True)]
    ppermute x6 -> x10, waiting for transfers between devices: 2.11 us -> 17.9 us  [the longest x4 9.98 us: swap(): return lax.ppermute(x, axis, [(0, 1), (1, 0)])]
    ppermute x6 -> x10, starting transfers between devices: 24.3 us -> 35.5 us  [the longest x6 21 us: along_x(): return lax.ppermute(x, 'x', [(i, (i + step) % nx) for i in range(nx)])]
    all_to_all x2 -> x3, starting transfers between devices: 27.1 us -> 37.6 us  [exchange(): return lax.all_to_all(x, axis, split_axis=0, concat_axis=0, tiled=True)]
    unnamed x25 -> x33, local copies, waits for them, and re-layouts: 4.09 us -> 4.82 us
    pallas_call x9 -> x10, Pallas kernels: 33.1 us -> 33.2 us  [call(): pl.pallas_call(body, out_shape=[shape(x.shape, x.dtype) for x, _ in outs]...]
  transfers between devices with their start and end apart: 8 -> 13, of which waited for: 3 -> 8; matrix products, arithmetic and copies ran while one was open for 3% -> 3% of each run, Pallas kernels for 12% -> 13%
where the time goes in v4:
time: 175 us; the launch traced here: 174 us
  starting transfers between devices  73.1 us (42%)
  waiting for transfers between devices  41.1 us (23%)
  Pallas kernels  33.2 us (19%)
  blocking collectives  15.7 us (9%)
  local copies, waits for them, and re-layouts  8.79 us (5%)
    all_to_all x3, starting transfers between devices, exchange(): return lax.all_to_all(x, axis, split_axis=0, concat_axis=0, tiled=True)  37.6 us
    pallas_call x10, Pallas kernels, call(): pl.pallas_call(body, out_shape=[shape(x.shape, x.dtype) for x, _ in outs]...  33.2 us
    all_to_all x3, waiting for transfers between devices, exchange(): return lax.all_to_all(x, axis, split_axis=0, concat_axis=0, tiled=True)  23.2 us
    ppermute x6, starting transfers between devices, along_x(): return lax.ppermute(x, 'x', [(i, (i + step) % nx) for i in range(nx)])  21 us
    all_to_all x1, blocking collectives, exchange(): return lax.all_to_all(x, axis, split_axis=0, concat_axis=0, tiled=True)  15.7 us
    ppermute x4, starting transfers between devices, swap(): return lax.ppermute(x, axis, [(0, 1), (1, 0)])  14.5 us
    ppermute x4, waiting for transfers between devices, swap(): return lax.ppermute(x, axis, [(0, 1), (1, 0)])  9.98 us
    ppermute x6, waiting for transfers between devices, along_x(): return lax.ppermute(x, 'x', [(i, (i + step) % nx) for i in range(nx)])  7.89 us
  transfers between devices with their start and end apart: 13, of which 8 were waited for; matrix products, arithmetic and copies ran while one was open for 3% of the time, Pallas kernels for 13%

profile of v4, /device:TPU:1, one launch (start us, length us, event | category | flops | bytes accessed | tf_op | source)
XLA Modules:
  0.0 174.3 jit_solution(6467342343358492849)
XLA Ops:
  0.6 4.0 %collective-permute-start = (bf16[256,256]{1,0:T(8,128)(2,1)}, bf16[256,256]{1,0:T(8,128)(2,1)S(1)}, u32[]{:S(2)}, u32[]{:S(2)}) collective-permute-start(bf16[256,256]{1,0:T(8,128)(2,1)} %refs_2_.3), channel_id=1, source_target_pairs={{0,256},{256,0},{1,257},{257,1},{2,258},{258,2},{3,259},{259,3},{4... | collective-permute-start | bytes 393224 | tf_op jit(solution)/shard_map/ppermute | solution.py:354
  4.7 3.4 %shard_map.129 = bf16[64,72,128]{2,1,0:T(8,128)(2,1)} custom-call(s32[64]{0:T(128)} %bitcast.19, bf16[64,32,128]{2,1,0:T(8,128)(2,1)} %bitcast.13, bf16[256,256]{1,0:T(8,128)(2,1)} %refs_2_.3), custom_call_target="tpu_custom_call" | custom-call | flops 1024 | bytes 1024 | tf_op jit(solution)/shard_map/pallas_call | solution.py:99
  8.1 16.3 %all-to-all-start = ((bf16[64,72,128]{2,1,0:T(8,128)(2,1)}), bf16[64,72,128]{2,1,0:T(8,128)(2,1)S(1)}, u32[]{:S(2)}, u32[]{:S(2)}) async-start(bf16[64,72,128]{2,1,0:T(8,128)(2,1)} %shard_map.129), calls=%async_computation | async-start | bytes 2359296 | tf_op jit(solution)/shard_map/all_to_all | solution.py:350
  25.4 3.1 %collective-permute-start.1 = (bf16[512,256]{1,0:T(8,128)(2,1)S(1)}, bf16[512,256]{1,0:T(8,128)(2,1)S(1)}, u32[]{:S(2)}, u32[]{:S(2)}) collective-permute-start(bf16[512,256]{1,0:T(8,128)(2,1)S(1)} %pad_maximum_fusion), channel_id=1, source_target_pairs={{0,64},{64,128},{128,192},{192,0},{1,65},{65,129},{129,193},{193,1... | collective-permute-start | bytes 786440 | tf_op jit(solution)/shard_map/ppermute | solution.py:358
  28.6 4.4 %collective-permute-start.2 = (bf16[512,256]{1,0:T(8,128)(2,1)S(1)}, bf16[512,256]{1,0:T(8,128)(2,1)S(1)}, u32[]{:S(2)}, u32[]{:S(2)}) collective-permute-start(bf16[512,256]{1,0:T(8,128)(2,1)S(1)} %pad_maximum_fusion), channel_id=1, source_target_pairs={{0,128},{64,192},{128,0},{192,64},{1,129},{65,193},{129,1},{193,65... | collective-permute-start | bytes 786440 | tf_op jit(solution)/shard_map/ppermute | solution.py:358
  32.9 3.1 %collective-permute-start.3 = (bf16[512,256]{1,0:T(8,128)(2,1)S(1)}, bf16[512,256]{1,0:T(8,128)(2,1)S(1)}, u32[]{:S(2)}, u32[]{:S(2)}) collective-permute-start(bf16[512,256]{1,0:T(8,128)(2,1)S(1)} %pad_maximum_fusion), channel_id=1, source_target_pairs={{0,192},{64,0},{128,64},{192,128},{1,193},{65,1},{129,65},{193,129... | collective-permute-start | bytes 786440 | tf_op jit(solution)/shard_map/ppermute | solution.py:358
  39.4 6.1 %shard_map.130 = (bf16[256,4096]{1,0:T(8,128)(2,1)}, bf16[8,256,512]{2,1,0:T(8,128)(2,1)}, bf16[256,2048]{1,0:T(8,128)(2,1)}, bf16[2048,256]{1,0:T(8,128)(2,1)},...) custom-call(s32[32]{0:T(128)} %reshape.37.refs_0_, ...), custom_call_target="tpu_custom_call" | custom-call | flops 1024 | bytes 1024 | tf_op jit(solution)/shard_map/pallas_call | solution.py:99
  47.0 4.1 %shard_map.131.refs_4_ = f32[256,256]{1,0:T(8,128)} custom-call(s32[32]{0:T(128)} %reshape.38.refs_1_.refs_0_, s32[2]{0:T(128)} %pad_add_fusion.refs_1_, bf16[256,256]{1,0:T(8,128)(2,1)} %refs_2_.3, bf16[256,256]{1,0:T(8,128)(2,1)} %copy-done.8, bf16[512,256]{1,0:T(8,128)(2,1)} %copy-done.12, bf16[512,256]{1,0:T(8,128)(2,1)} %copy-done.13, ...), custom_call_target="tpu_custom_call" | custom-call | flops 30000001024 | bytes 1024 | tf_op jit(solution)/shard_map/pallas_call | solution.py:99
  51.1 5.2 %all-to-all-done.refs_2_ = bf16[64,72,128]{2,1,0:T(8,128)(2,1)S(1)} async-done(((bf16[64,72,128]{2,1,0:T(8,128)(2,1)}), bf16[64,72,128]{2,1,0:T(8,128)(2,1)S(1)}, u32[]{:S(2)}, u32[]{:S(2)}) %all-to-all-start) | async-done | bytes 1179680 | tf_op jit(solution)/shard_map/all_to_all | solution.py:350
  57.3 5.1 %shard_map.132 = (bf16[256,256]{1,0:T(8,128)(2,1)}, bf16[256,256]{1,0:T(8,128)(2,1)}, bf16[256,256]{1,0:T(8,128)(2,1)}, f32[256,256]{1,0:T(8,128)}, bf16[32,80,2...) custom-call(s32[1]{0:T(128)} %bitcast.refs_2_.refs_0_, s32[1]{0:T(128)} %bitcast.1.refs_1_, ...), custom_call_target="tpu_custom_call" | custom-call | flops 1024 | bytes 1024 | tf_op jit(solution)/shard_map/pallas_call | solution.py:99
  62.5 3.1 %collective-permute-start.4 = (bf16[32,48,256]{2,1,0:T(8,128)(2,1)}, bf16[32,48,256]{2,1,0:T(8,128)(2,1)S(1)}, u32[]{:S(2)}, u32[]{:S(2)}) collective-permute-start(bf16[32,48,256]{2,1,0:T(8,128)(2,1)} %get-tuple-element.40), channel_id=1, source_target_pairs={{0,1},{1,0},{2,3},{3,2},{4,5},{5,4},{6,7},{7,6},{8,9},{9,8},{10,11... | collective-permute-start | bytes 2359304 | tf_op jit(solution)/shard_map/ppermute | solution.py:354
  70.8 11.2 %all-to-all-start.1 = ((bf16[32,80,256]{2,1,0:T(8,128)(2,1)}), bf16[32,80,256]{2,1,0:T(8,128)(2,1)S(1)}, u32[]{:S(2)}, u32[]{:S(2)}) async-start(bf16[32,80,256]{2,1,0:T(8,128)(2,1)} %shard_map.133), calls=%async_computation.1 | async-start | bytes 2621440 | tf_op jit(solution)/shard_map/all_to_all | solution.py:350
  82.0 3.9 %shard_map.134 = (f32[512,256]{1,0:T(8,128)}, bf16[512,256]{1,0:T(8,128)(2,1)}, bf16[512,256]{1,0:T(8,128)(2,1)}, bf16[512,256]{1,0:T(8,128)(2,1)}) custom-call(s32[32]{0:T(128)} %reshape.37.refs_0_, s32[2]{0:T(128)} %pad_add_fusion.refs_1_, bf16[256,256]{1,0:T(8,128)(2,1)} %get-tuple-element.44.refs_2_, bf16[8,256,512]{2,1,0:T(8,128)(2,1)} %get-tuple-element.45.refs_3_), custom_call_target="tpu_custom_call" | custom-call | flops 1024 | bytes 1024 | tf_op jit(solution)/shard_map/pallas_call | solution.py:99
  85.9 2.7 %collective-permute-start.5 = (bf16[512,256]{1,0:T(8,128)(2,1)}, bf16[512,256]{1,0:T(8,128)(2,1)S(1)}, u32[]{:S(2)}, u32[]{:S(2)}) collective-permute-start(bf16[512,256]{1,0:T(8,128)(2,1)} %get-tuple-element.46), channel_id=1, source_target_pairs={{0,64},{64,128},{128,192},{192,0},{1,65},{65,129},{129,193},{193,1... | collective-permute-start | bytes 786440 | tf_op jit(solution)/shard_map/ppermute | solution.py:358
  88.6 4.6 %collective-permute-start.6 = (bf16[512,256]{1,0:T(8,128)(2,1)}, bf16[512,256]{1,0:T(8,128)(2,1)S(1)}, u32[]{:S(2)}, u32[]{:S(2)}) collective-permute-start(bf16[512,256]{1,0:T(8,128)(2,1)} %get-tuple-element.47), channel_id=1, source_target_pairs={{0,128},{64,192},{128,0},{192,64},{1,129},{65,193},{129,1},{193,65... | collective-permute-start | bytes 786440 | tf_op jit(solution)/shard_map/ppermute | solution.py:358
  93.3 3.1 %collective-permute-start.7 = (bf16[512,256]{1,0:T(8,128)(2,1)}, bf16[512,256]{1,0:T(8,128)(2,1)S(1)}, u32[]{:S(2)}, u32[]{:S(2)}) collective-permute-start(bf16[512,256]{1,0:T(8,128)(2,1)} %get-tuple-element.48), channel_id=1, source_target_pairs={{0,192},{64,0},{128,64},{192,128},{1,193},{65,1},{129,65},{193,129... | collective-permute-start | bytes 786440 | tf_op jit(solution)/shard_map/ppermute | solution.py:358
  96.4 6.5 %collective-permute-done.6.refs_2_ = bf16[512,256]{1,0:T(8,128)(2,1)S(1)} collective-permute-done((bf16[512,256]{1,0:T(8,128)(2,1)}, bf16[512,256]{1,0:T(8,128)(2,1)S(1)}, u32[]{:S(2)}, u32[]{:S(2)}) %collective-permute-start.6) | collective-permute-done | bytes 262176 | tf_op jit(solution)/shard_map/ppermute | solution.py:358
  104.2 18.0 %all-to-all-done.1.refs_0_.refs_3_ = bf16[32,80,256]{2,1,0:T(8,128)(2,1)S(1)} async-done(((bf16[32,80,256]{2,1,0:T(8,128)(2,1)}), bf16[32,80,256]{2,1,0:T(8,128)(2,1)S(1)}, u32[]{:S(2)}, u32[]{:S(2)}) %all-to-all-start.1) | async-done | bytes 1310752 | tf_op jit(solution)/shard_map/all_to_all | solution.py:350
  124.9 15.7 %all_to_all.20.refs_0_ = f32[8,8,256]{2,1,0:T(8,128)} all-to-all(f32[8,8,256]{2,1,0:T(8,128)} %shard_map.135), channel_id=1, replica_groups=mesh['y'=2,'x'=4,'far'=32,'core'=2] {'y','x'}, dimensions={0} | all-to-all | bytes 131072 | tf_op jit(solution)/shard_map/all_to_all | solution.py:350
  142.2 10.1 %all-to-all-start.3 = ((f32[32,8,256]{2,1,0:T(8,128)}), f32[32,8,256]{2,1,0:T(8,128)S(1)}, u32[]{:S(2)}, u32[]{:S(2)}) async-start(f32[32,8,256]{2,1,0:T(8,128)} %shard_map.136), calls=%async_computation.3 | async-start | bytes 524288 | tf_op jit(solution)/shard_map/all_to_all | solution.py:350
  154.6 2.3 %collective-permute-start.8 = (f32[256,256]{1,0:T(8,128)}, f32[256,256]{1,0:T(8,128)S(1)}, u32[]{:S(2)}, u32[]{:S(2)}) collective-permute-start(f32[256,256]{1,0:T(8,128)} %get-tuple-element.54), channel_id=1, source_target_pairs={{0,256},{256,0},{1,257},{257,1},{2,258},{258,2},{3,259},{259,3},{4... | collective-permute-start | bytes 786440 | tf_op jit(solution)/shard_map/ppermute | solution.py:354
  156.8 6.7 %collective-permute-done.8.refs_5_ = f32[256,256]{1,0:T(8,128)S(1)} collective-permute-done((f32[256,256]{1,0:T(8,128)}, f32[256,256]{1,0:T(8,128)S(1)}, u32[]{:S(2)}, u32[]{:S(2)}) %collective-permute-start.8) | collective-permute-done | bytes 262176 | tf_op jit(solution)/shard_map/ppermute | solution.py:354
  164.3 2.9 %shard_map.138 = bf16[256,256]{1,0:T(8,128)(2,1)} custom-call(bf16[256,256]{1,0:T(8,128)(2,1)} %get-tuple-element.50.refs_0_, bf16[256,256]{1,0:T(8,128)(2,1)} %refs_1_.1, bf16[256,2048]{1,0:T(8,128)(2,1)} %get-tuple-element.51.refs_2_, bf16[32,80,256]{2,1,0:T(8,128)(2,1)} %copy-done, f32[256,256]{1,0:T(8,128)} %get-tuple-element.53.refs_4_, ...), custom_call_target="tpu_custom_call" | custom-call | flops 1024 | bytes 1024 | tf_op jit(solution)/shard_map/pallas_call | solution.py:99
  167.2 5.1 %collective-permute-start.9 = (f32[256,256]{1,0:T(8,128)S(1)}, f32[256,256]{1,0:T(8,128)S(1)}, u32[]{:S(2)}, u32[]{:S(2)}) collective-permute-start(f32[256,256]{1,0:T(8,128)S(1)} %bitcast.16), channel_id=1, source_target_pairs={{0,1},{1,0},{2,3},{3,2},{4,5},{5,4},{6,7},{7,6},{8,9},{9,8},{10,11... | collective-permute-start | bytes 786440 | tf_op jit(solution)/shard_map/ppermute | solution.py:354
  (56 shorter events, 22.5 us)
Async XLA Ops:
  0.6 24.7 %collective-permute-start = (bf16[256,256]{1,0:T(8,128)(2,1)}, bf16[256,256]{1,0:T(8,128)(2,1)S(1)}, u32[]{:S(2)}, u32[]{:S(2)}) collective-permute-start(bf16[256,256]{1,0:T(8,128)(2,1)} %refs_2_.3), channel_id=1, source_target_pairs={{0,256},{256,0},{1,257},{257,1},{2,258},{258,2},{3,259},{259,3},{4... | collective-permute-start | bytes 393224 | tf_op jit(solution)/shard_map/ppermute | solution.py:354
  8.1 16.4 %copy-start.9 = (s32[1,64,32]{1,2,0:T(8,128)S(1)}, s32[1,64,32]{1,2,0:T(8,128)}, u32[]{:S(2)}) copy-start(s32[1,64,32]{1,2,0:T(8,128)} %param.19) | copy-start | bytes 24580
  8.1 17.3 %copy-start.2 = (bf16[256,256]{1,0:T(8,128)(2,1)S(1)}, bf16[256,256]{1,0:T(8,128)(2,1)}, u32[]{:S(2)}) copy-start(bf16[256,256]{1,0:T(8,128)(2,1)} %refs_2_.3) | copy-start | bytes 393220
  8.1 48.2 %all-to-all-start = ((bf16[64,72,128]{2,1,0:T(8,128)(2,1)}), bf16[64,72,128]{2,1,0:T(8,128)(2,1)S(1)}, u32[]{:S(2)}, u32[]{:S(2)}) async-start(bf16[64,72,128]{2,1,0:T(8,128)(2,1)} %shard_map.129), calls=%async_computation | async-start | bytes 2359296 | tf_op jit(solution)/shard_map/all_to_all | solution.py:350
  24.5 13.6 %copy-start.10 = (s32[1,8,4]{1,2,0:T(4,128)S(1)}, s32[1,8,4]{1,2,0:T(4,128)}, u32[]{:S(2)}) copy-start(s32[1,8,4]{1,2,0:T(4,128)} %param.15) | copy-start | bytes 388
  24.5 14.3 %copy-start.11 = (s32[1,8,4]{1,2,0:T(4,128)S(1)}, s32[1,8,4]{1,2,0:T(4,128)}, u32[]{:S(2)}) copy-start(s32[1,8,4]{1,2,0:T(4,128)} %param.16) | copy-start | bytes 388
  25.4 20.1 %copy-start.8 = (bf16[256,256]{1,0:T(8,128)(2,1)}, bf16[256,256]{1,0:T(8,128)(2,1)S(1)}, u32[]{:S(2)}) copy-start(bf16[256,256]{1,0:T(8,128)(2,1)S(1)} %collective-permute-done.refs_3_) | copy-start | bytes 393220
  25.4 20.7 %collective-permute-start.1 = (bf16[512,256]{1,0:T(8,128)(2,1)S(1)}, bf16[512,256]{1,0:T(8,128)(2,1)S(1)}, u32[]{:S(2)}, u32[]{:S(2)}) collective-permute-start(bf16[512,256]{1,0:T(8,128)(2,1)S(1)} %pad_maximum_fusion), channel_id=1, source_target_pairs={{0,64},{64,128},{128,192},{192,0},{1,65},{65,129},{129,193},{193,1... | collective-permute-start | bytes 786440 | tf_op jit(solution)/shard_map/ppermute | solution.py:358
  28.6 17.5 %collective-permute-start.2 = (bf16[512,256]{1,0:T(8,128)(2,1)S(1)}, bf16[512,256]{1,0:T(8,128)(2,1)S(1)}, u32[]{:S(2)}, u32[]{:S(2)}) collective-permute-start(bf16[512,256]{1,0:T(8,128)(2,1)S(1)} %pad_maximum_fusion), channel_id=1, source_target_pairs={{0,128},{64,192},{128,0},{192,64},{1,129},{65,193},{129,1},{193,65... | collective-permute-start | bytes 786440 | tf_op jit(solution)/shard_map/ppermute | solution.py:358
  32.9 13.2 %collective-permute-start.3 = (bf16[512,256]{1,0:T(8,128)(2,1)S(1)}, bf16[512,256]{1,0:T(8,128)(2,1)S(1)}, u32[]{:S(2)}, u32[]{:S(2)}) collective-permute-start(bf16[512,256]{1,0:T(8,128)(2,1)S(1)} %pad_maximum_fusion), channel_id=1, source_target_pairs={{0,192},{64,0},{128,64},{192,128},{1,193},{65,1},{129,65},{193,129... | collective-permute-start | bytes 786440 | tf_op jit(solution)/shard_map/ppermute | solution.py:358
  56.3 1.0 copy-start.1
  62.5 5.2 %collective-permute-start.4 = (bf16[32,48,256]{2,1,0:T(8,128)(2,1)}, bf16[32,48,256]{2,1,0:T(8,128)(2,1)S(1)}, u32[]{:S(2)}, u32[]{:S(2)}) collective-permute-start(bf16[32,48,256]{2,1,0:T(8,128)(2,1)} %get-tuple-element.40), channel_id=1, source_target_pairs={{0,1},{1,0},{2,3},{3,2},{4,5},{5,4},{6,7},{7,6},{8,9},{9,8},{10,11... | collective-permute-start | bytes 2359304 | tf_op jit(solution)/shard_map/ppermute | solution.py:354
  67.7 0.9 copy-start.3
  70.8 51.4 %all-to-all-start.1 = ((bf16[32,80,256]{2,1,0:T(8,128)(2,1)}), bf16[32,80,256]{2,1,0:T(8,128)(2,1)S(1)}, u32[]{:S(2)}, u32[]{:S(2)}) async-start(bf16[32,80,256]{2,1,0:T(8,128)(2,1)} %shard_map.133), calls=%async_computation.1 | async-start | bytes 2621440 | tf_op jit(solution)/shard_map/all_to_all | solution.py:350
  85.9 10.5 %collective-permute-start.5 = (bf16[512,256]{1,0:T(8,128)(2,1)}, bf16[512,256]{1,0:T(8,128)(2,1)S(1)}, u32[]{:S(2)}, u32[]{:S(2)}) collective-permute-start(bf16[512,256]{1,0:T(8,128)(2,1)} %get-tuple-element.46), channel_id=1, source_target_pairs={{0,64},{64,128},{128,192},{192,0},{1,65},{65,129},{129,193},{193,1... | collective-permute-start | bytes 786440 | tf_op jit(solution)/shard_map/ppermute | solution.py:358
  88.6 14.3 %collective-permute-start.6 = (bf16[512,256]{1,0:T(8,128)(2,1)}, bf16[512,256]{1,0:T(8,128)(2,1)S(1)}, u32[]{:S(2)}, u32[]{:S(2)}) collective-permute-start(bf16[512,256]{1,0:T(8,128)(2,1)} %get-tuple-element.47), channel_id=1, source_target_pairs={{0,128},{64,192},{128,0},{192,64},{1,129},{65,193},{129,1},{193,65... | collective-permute-start | bytes 786440 | tf_op jit(solution)/shard_map/ppermute | solution.py:358
  93.3 11.0 %collective-permute-start.7 = (bf16[512,256]{1,0:T(8,128)(2,1)}, bf16[512,256]{1,0:T(8,128)(2,1)S(1)}, u32[]{:S(2)}, u32[]{:S(2)}) collective-permute-start(bf16[512,256]{1,0:T(8,128)(2,1)} %get-tuple-element.48), channel_id=1, source_target_pairs={{0,192},{64,0},{128,64},{192,128},{1,193},{65,1},{129,65},{193,129... | collective-permute-start | bytes 786440 | tf_op jit(solution)/shard_map/ppermute | solution.py:358
  96.4 55.9 %copy-start.4 = (bf16[512,256]{1,0:T(8,128)(2,1)}, bf16[512,256]{1,0:T(8,128)(2,1)S(1)}, u32[]{:S(2)}) copy-start(bf16[512,256]{1,0:T(8,128)(2,1)S(1)} %collective-permute-done.5.refs_1_) | copy-start | bytes 786436
  102.9 49.5 %copy-start.5 = (bf16[512,256]{1,0:T(8,128)(2,1)}, bf16[512,256]{1,0:T(8,128)(2,1)S(1)}, u32[]{:S(2)}) copy-start(bf16[512,256]{1,0:T(8,128)(2,1)S(1)} %collective-permute-done.6.refs_2_) | copy-start | bytes 786436
  104.2 48.2 %copy-start.6 = (bf16[512,256]{1,0:T(8,128)(2,1)}, bf16[512,256]{1,0:T(8,128)(2,1)S(1)}, u32[]{:S(2)}) copy-start(bf16[512,256]{1,0:T(8,128)(2,1)S(1)} %collective-permute-done.7.refs_3_) | copy-start | bytes 786436
  122.2 1.1 copy-start
  142.2 25.0 %all-to-all-start.3 = ((f32[32,8,256]{2,1,0:T(8,128)}), f32[32,8,256]{2,1,0:T(8,128)S(1)}, u32[]{:S(2)}, u32[]{:S(2)}) async-start(f32[32,8,256]{2,1,0:T(8,128)} %shard_map.136), calls=%async_computation.3 | async-start | bytes 524288 | tf_op jit(solution)/shard_map/all_to_all | solution.py:350
  154.6 9.0 %collective-permute-start.8 = (f32[256,256]{1,0:T(8,128)}, f32[256,256]{1,0:T(8,128)S(1)}, u32[]{:S(2)}, u32[]{:S(2)}) collective-permute-start(f32[256,256]{1,0:T(8,128)} %get-tuple-element.54), channel_id=1, source_target_pairs={{0,256},{256,0},{1,257},{257,1},{2,258},{258,2},{3,259},{259,3},{4... | collective-permute-start | bytes 786440 | tf_op jit(solution)/shard_map/ppermute | solution.py:354
  167.2 6.3 %collective-permute-start.9 = (f32[256,256]{1,0:T(8,128)S(1)}, f32[256,256]{1,0:T(8,128)S(1)}, u32[]{:S(2)}, u32[]{:S(2)}) collective-permute-start(f32[256,256]{1,0:T(8,128)S(1)} %bitcast.16), channel_id=1, source_target_pairs={{0,1},{1,0},{2,3},{3,2},{4,5},{5,4},{6,7},{7,6},{8,9},{9,8},{10,11... | collective-permute-start | bytes 786440 | tf_op jit(solution)/shard_map/ppermute | solution.py:354
  (4 other events, 3.0 us)

commit v5 on v4

--- a/solution.py
+++ b/solution.py
@@ -49,7 +49,7 @@
         self.copies.append(copy)
 
 
-def call(kernel, outs, scalars, arrays, scratch=(), flops=SMALL, into=None, pieces=1):
+def call(kernel, outs, scalars, arrays, scratch=(), flops=SMALL, into=(), pieces=1):
     def split(x):
         return x if isinstance(x, tuple) else (x, ())
 
@@ -63,14 +63,13 @@
         return ref.at[window] if window else ref
 
     arrays, windows = zip(*[split(x) for x in arrays])
-    outs = [split(x) for x in outs] if into is None else [into]
+    outs = [split(x) for x in outs] + list(into)
     n_smem, n_in, n_out = len(scalars), len(arrays), len(outs)
 
     def body(*refs):
         smem, refs = refs[:n_smem], refs[n_smem:]
         src, refs = refs[:n_in], refs[n_in:]
-        if into is not None:
-            refs = refs[1:]
+        refs = refs[len(into) :]
         dst, refs = refs[:n_out], refs[n_out:]
         held, refs = refs[:n_in], refs[n_in:]
         made, refs = refs[:n_out], refs[n_out:]
@@ -95,7 +94,8 @@
 
     smem = pl.BlockSpec(memory_space=pltpu.SMEM)
     hbm = pl.BlockSpec(memory_space=pltpu.MemorySpace.HBM)
-    extra = [] if into is None else [into[0]]
+    extra = [x for x, _ in into]
+    first = n_out - len(into)
     result = pl.pallas_call(
         body,
         out_shape=[shape(x.shape, x.dtype) for x, _ in outs],
@@ -105,7 +105,7 @@
         + [window_shape(x, w) for x, w in outs]
         + [pltpu.SemaphoreType.DMA((n_in,)), pltpu.SemaphoreType.DMA((n_out, pieces))]
         + list(scratch),
-        input_output_aliases={} if into is None else {n_smem + n_in: 0},
+        input_output_aliases={n_smem + n_in + i: first + i for i in range(len(into))},
         cost_estimate=pl.CostEstimate(flops=flops, bytes_accessed=SMALL, transcendentals=0),
     )(*scalars, *arrays, *extra)
     return result if n_out > 1 else result[0]
@@ -215,7 +215,7 @@
 
 def middle_kernel(
     core, me, got, onehot, local, degree, feat_self, neigh_weight, cotangent, feat_t, onehot_t,
-    layer_out, dpre_out, gn_out, wkeep, packed, send, rhs_ref,
+    layer_out, dpre_out, gn_out, wkeep, wsend, packed, hsend, rhs_ref,
 ):
     got_ref = got()
     senders = got_ref.shape[0]
@@ -252,53 +252,28 @@
     gn = (dot(dpre, nw, NT) * scale).astype(BF16)
     wself = dot(feat_t()[...], dpre)
     wneigh = dot(neigh.T, dpre)
-    put_pairs(send.ref, hub, jnp.where(core[0] == 0, wneigh, wself))
-    hot = onehot_t()
-    send.ref[:, :hub, :] = dot(hot[slots // 2 :, :], gn).astype(BF16).reshape(packed.ref.shape)
-    send.send()
-    packed.ref[...] = dot(hot[: slots // 2, :], gn).astype(BF16).reshape(packed.ref.shape)
-    packed.send()
+    wsend.ref[...] = jnp.where(core[0] == 0, wneigh, wself)
+    wsend.send()
     wkeep.ref[...] = jnp.where(core[0] == 0, wself, wneigh)
     wkeep.send()
     gn_out.ref[...] = gn
     gn_out.send()
+    hot = onehot_t()
+    hsend.ref[...] = dot(hot[slots // 2 :, :], gn).astype(BF16).reshape(hsend.ref.shape)
+    hsend.send()
+    packed.ref[...] = dot(hot[: slots // 2, :], gn).astype(BF16).reshape(packed.ref.shape)
+    packed.send()
     layer_out.ref[...] = (pre * sig).astype(BF16)
     dpre_out.ref[...] = dpre
 
 
-def put_pairs(ref, top, total):
-    far, _, width = ref.shape
-    rows = total.shape[0] // far
-    high = total.astype(BF16)
-    low = (total - high.astype(F32)).astype(BF16)
-    ref[:, top : top + rows, :] = high.reshape(far, rows, width)
-    ref[:, top + rows : top + 2 * rows, :] = low.reshape(far, rows, width)
-
-
-def get_pairs(ref, top):
-    far, deep, width = ref.shape
-    rows = (deep - top) // 2
-    both = ref[:, top:, :].astype(F32)
-    return both[:, :rows, :] + both[:, rows:, :]
-
-
-def assemble_kernel(got, wkeep, out):
-    got_ref = got()
-    far, deep, width = got_ref.shape
-    hub = deep - 2 * (wkeep.ref.shape[0] // far)
-    out.ref[:, :hub, :] = got_ref[:, :hub, :]
-    total = wkeep()[...] + get_pairs(got_ref, hub).reshape(wkeep.ref.shape)
-    put_pairs(out.ref, hub, total)
-
-
-def sum_pairs_kernel(got, out):
-    total = jnp.sum(get_pairs(got(), 0), axis=0)
-    out.ref[...] = jnp.broadcast_to(total[None], out.ref.shape)
-
-
-def sum_kernel(got, out):
-    total = jnp.sum(got()[...], axis=0)
-    out.ref[...] = jnp.broadcast_to(total[None], out.ref.shape)
+def add_kernel(got, keep, out):
+    total = keep()[...] + got()[...]
+    out.ref[...] = total.reshape(out.ref.shape)
+
+
+def assemble_kernel(got, out):
+    out.ref[...] = got()[...]
 
 
 def panels_kernel(dest, here, gn, back, *rest):
@@ -323,15 +298,38 @@
         out.send()
 
 
-def sum_panels_kernel(*rest):
-    terms, (here, there) = rest[:-2], rest[-2:]
-    rows = here.ref.shape[0]
-    total = terms[0]()[...].astype(F32)
-    for term in terms[1:]:
-        total = total + term()[...].astype(F32)
-    there.ref[...] = total[rows:]
-    there.send()
+def sum_far_kernel(got, out, *rest):
+    total = jnp.sum(got()[...], axis=0)
+    rows = total.shape[0]
+    high = total.astype(BF16)
+    low = (total - high.astype(F32)).astype(BF16)
+    for behind in rest:
+        behind.ref[:rows, :] = high
+        behind.ref[rows:, :] = low
+        behind.send()
+    out.ref[...] = total
+
+
+def sum_x_kernel(own, chunk, *rest):
+    terms, (here, keep, message) = rest[:-3], rest[-3:]
+    rows, small = here.ref.shape[0], keep.ref.shape[0]
+    total = own()[...]
+    part = chunk()[...]
+    for term in terms:
+        ref = term()
+        total = total + ref[: 2 * rows, :].astype(F32)
+        both = ref[2 * rows :, :].astype(F32)
+        part = part + (both[:small] + both[small:])
+    message.ref[:rows, :] = total[rows:]
+    message.ref[rows:, :] = part
+    message.send()
+    keep.ref[...] = part
     here.ref[...] = total[:rows]
+
+
+def sum_y_kernel(keep, got, out):
+    total = keep()[...] + got()[...]
+    out.ref[...] = jnp.broadcast_to(total[None], out.ref.shape)
 
 
 def final_kernel(dpre, self_weight, hub_t, back, here, got, out):
@@ -344,6 +342,14 @@
         rows = back_ref[:, i * hub : (i + 1) * hub, :].reshape(half, width)
         total = total + dot(hub_ref[:, i * half : (i + 1) * half], rows)
     out.ref[...] = (total + here()[...] + got()[...]).astype(BF16)
+
+
+def square32_pair(rows, width):
+    return shape((2 * rows, width), F32)
+
+
+def as_list(x):
+    return list(x) if isinstance(x, (list, tuple)) else [x]
 
 
 def exchange(x, axis):
@@ -419,13 +425,12 @@
         [pltpu.VMEM((panels * rows, width), BF16), pltpu.VMEM((n * tile, width), BF16)],
         TILE_COST,
     )
-    deep = 2 * (hub + chunk)
-    layer_out, dpre, gn, wkeep, packed, send = call(
+    layer_out, dpre, gn, wkeep, wsend, packed, hsend = call(
         middle_kernel,
         [
-            square, square, square, square32,
-            (shape((far, deep, width), BF16), (ALL, slice(0, hub))),
-            shape((far, hub + 2 * chunk, width), BF16),
+            square, square, square, square32, square32,
+            (shape((far, 2 * hub, width), BF16), (ALL, slice(0, hub))),
+            shape((far, hub, width), BF16),
         ],
         (core1, me),
         (
@@ -433,32 +438,47 @@
         ),
         [pltpu.VMEM((slots, width + 2 * LANES), BF16)],
     )
+    both = call(add_kernel, [shape((far, chunk, width), F32)], (), (swap(wsend, "core"), wkeep))
+    scattered = exchange(both, "far")
+    tall = 2 * rows + 2 * chunk
+    terms = call(
+        panels_kernel,
+        [square32_pair(rows, width)]
+        + [(shape((tall, width), BF16), (slice(0, 2 * rows),))] * (nx - 1),
+        (dest, here), (after(gn, both), back), [pltpu.VMEM((per * tile, width), BF16)],
+    )
+    terms = terms if nx > 1 else [terms]
+    hsend = after(hsend, both)
     packed = call(
-        assemble_kernel, [], (), (swap(send, "core"), wkeep),
-        into=(packed, (ALL, slice(hub, deep))),
-    )
-    gathered = exchange(packed, "far")
-    terms = call(
-        panels_kernel, [shape((2 * rows, width), F32)] + [shape((2 * rows, width), BF16)] * (nx - 1),
-        (dest, here), (after(gn, packed), back), [pltpu.VMEM((per * tile, width), BF16)],
-    )
-    terms = terms if nx > 1 else [terms]
-    arrived = [along_x(terms[k], k, nx) for k in range(1, nx)]
-    panel_here, panel_there = call(sum_panels_kernel, [square32] * 2, (), (terms[0], *arrived))
-    panel_got = swap(panel_there, "y")
-    part = call(
-        sum_pairs_kernel, [shape((panels, chunk, width), F32)], (),
-        ((after(gathered, arrived), (ALL, slice(2 * hub, deep))),),
-    )
+        assemble_kernel, [], (), (swap(hsend, "core"),),
+        into=[(packed, (ALL, slice(hub, 2 * hub)))],
+    )
+    scattered = after(scattered, (terms, packed))
+    tail = (slice(2 * rows, tall),)
+    part, *behind = as_list(
+        call(
+            sum_far_kernel, [shape((chunk, width), F32)], (), (scattered,),
+            into=[(x, tail) for x in terms[1:]],
+        )
+    )
+    gathered = exchange(after(packed, part), "far")
+    arrived = [along_x(behind[k - 1], k, nx) for k in range(1, nx)]
+    panel_here, keep, message = call(
+        sum_x_kernel, [square32, shape((chunk, width), F32), shape((rows + chunk, width), F32)],
+        (), (terms[0], part, *arrived),
+    )
+    message = swap(message, "y")
     total = call(
-        sum_kernel, [shape((far, chunk, width), F32)], (), (exchange(part, ("y", "x")),)
-    )
+        sum_y_kernel, [shape((far, chunk, width), F32)], (),
+        (keep, (message, (slice(rows, rows + chunk),))),
+    )
+    total = after(total, gathered)
     mine = exchange(total, "far").reshape(width, width)
     feat_grad = call(
         final_kernel, [square], (),
         (
-            after(dpre, total), self_weight, hub_t, (gathered, (ALL, slice(0, 2 * hub))),
-            panel_here, panel_got,
+            after(dpre, total), self_weight, hub_t, gathered, panel_here,
+            (message, (slice(0, rows),)),
         ),
     )
     theirs = swap(after(mine, feat_grad), "core")

time: 175 us -> 179 us (1.023); the launches traced: 174 us -> 176 us
  starting transfers between devices: 73.1 us -> 93.3 us
  blocking collectives: 15.7 us -> 0 us
  waiting for transfers between devices: 41.1 us -> 35.6 us
    all_to_all x1 -> x0, blocking collectives: 15.7 us -> none  [exchange(): return lax.all_to_all(x, axis, split_axis=0, concat_axis=0, tiled=True)]
    ppermute x4 -> x5, starting transfers between devices: 14.5 us -> 25.9 us  [swap(): return lax.ppermute(x, axis, [(0, 1), (1, 0)])]
    all_to_all x3 -> x4, starting transfers between devices: 37.6 us -> 46.3 us  [exchange(): return lax.all_to_all(x, axis, split_axis=0, concat_axis=0, tiled=True)]
    all_to_all x3 -> x4, waiting for transfers between devices: 23.2 us -> 19.7 us  [exchange(): return lax.all_to_all(x, axis, split_axis=0, concat_axis=0, tiled=True)]
    ppermute x4 -> x5, waiting for transfers between devices: 9.98 us -> 8.2 us  [swap(): return lax.ppermute(x, axis, [(0, 1), (1, 0)])]
    pallas_call x10 -> x11, Pallas kernels: 33.2 us -> 34.5 us  [call(): pl.pallas_call(body, out_shape=[shape(x.shape, x.dtype) for x, _ in outs]...]
    unnamed x33 -> x43, local copies, waits for them, and re-layouts: 4.82 us -> 5.81 us
  transfers between devices with their start and end apart: 13 -> 15, of which waited for: 8 -> 8; matrix products, arithmetic and copies ran while one was open for 3% -> 3% of each run, Pallas kernels for 13% -> 15%
where the time goes in v5:
time: 179 us; the launch traced here: 176 us
  starting transfers between devices  93.3 us (52%)
  waiting for transfers between devices  35.6 us (20%)
  Pallas kernels  34.5 us (19%)
  local copies, waits for them, and re-layouts  9.89 us (6%)
    all_to_all x4, starting transfers between devices, exchange(): return lax.all_to_all(x, axis, split_axis=0, concat_axis=0, tiled=True)  46.3 us
    pallas_call x11, Pallas kernels, call(): pl.pallas_call(body, out_shape=[shape(x.shape, x.dtype) for x, _ in outs]...  34.5 us
    ppermute x5, starting transfers between devices, swap(): return lax.ppermute(x, axis, [(0, 1), (1, 0)])  25.9 us
    ppermute x6, starting transfers between devices, along_x(): return lax.ppermute(x, 'x', [(i, (i + step) % nx) for i in range(nx)])  21.1 us
    all_to_all x4, waiting for transfers between devices, exchange(): return lax.all_to_all(x, axis, split_axis=0, concat_axis=0, tiled=True)  19.7 us
    ppermute x5, waiting for transfers between devices, swap(): return lax.ppermute(x, axis, [(0, 1), (1, 0)])  8.2 us
    ppermute x6, waiting for transfers between devices, along_x(): return lax.ppermute(x, 'x', [(i, (i + step) % nx) for i in range(nx)])  7.69 us
    unnamed x43, local copies, waits for them, and re-layouts  5.81 us
  transfers between devices with their start and end apart: 15, of which 8 were waited for; matrix products, arithmetic and copies ran while one was open for 3% of the time, Pallas kernels for 15%

profile of v5, /device:TPU:1, one launch (start us, length us, event | category | flops | bytes accessed | tf_op | source)
XLA Modules:
  0.0 175.9 jit_solution(738431416733889704)
XLA Ops:
  0.6 4.0 %collective-permute-start = (bf16[256,256]{1,0:T(8,128)(2,1)}, bf16[256,256]{1,0:T(8,128)(2,1)S(1)}, u32[]{:S(2)}, u32[]{:S(2)}) collective-permute-start(bf16[256,256]{1,0:T(8,128)(2,1)} %refs_2_.3), channel_id=1, source_target_pairs={{0,256},{256,0},{1,257},{257,1},{2,258},{258,2},{3,259},{259,3},{4... | collective-permute-start | bytes 393224 | tf_op jit(solution)/shard_map/ppermute | solution.py:360
  4.7 3.6 %shard_map.129 = bf16[64,72,128]{2,1,0:T(8,128)(2,1)} custom-call(s32[64]{0:T(128)} %bitcast.19, bf16[64,32,128]{2,1,0:T(8,128)(2,1)} %bitcast.13, bf16[256,256]{1,0:T(8,128)(2,1)} %refs_2_.3), custom_call_target="tpu_custom_call" | custom-call | flops 1024 | bytes 1024 | tf_op jit(solution)/shard_map/pallas_call | solution.py:99
  8.3 16.2 %all-to-all-start = ((bf16[64,72,128]{2,1,0:T(8,128)(2,1)}), bf16[64,72,128]{2,1,0:T(8,128)(2,1)S(1)}, u32[]{:S(2)}, u32[]{:S(2)}) async-start(bf16[64,72,128]{2,1,0:T(8,128)(2,1)} %shard_map.129), calls=%async_computation | async-start | bytes 2359296 | tf_op jit(solution)/shard_map/all_to_all | solution.py:356
  25.4 3.1 %collective-permute-start.1 = (bf16[512,256]{1,0:T(8,128)(2,1)S(1)}, bf16[512,256]{1,0:T(8,128)(2,1)S(1)}, u32[]{:S(2)}, u32[]{:S(2)}) collective-permute-start(bf16[512,256]{1,0:T(8,128)(2,1)S(1)} %pad_maximum_fusion), channel_id=1, source_target_pairs={{0,64},{64,128},{128,192},{192,0},{1,65},{65,129},{129,193},{193,1... | collective-permute-start | bytes 786440 | tf_op jit(solution)/shard_map/ppermute | solution.py:364
  28.6 4.4 %collective-permute-start.2 = (bf16[512,256]{1,0:T(8,128)(2,1)S(1)}, bf16[512,256]{1,0:T(8,128)(2,1)S(1)}, u32[]{:S(2)}, u32[]{:S(2)}) collective-permute-start(bf16[512,256]{1,0:T(8,128)(2,1)S(1)} %pad_maximum_fusion), channel_id=1, source_target_pairs={{0,128},{64,192},{128,0},{192,64},{1,129},{65,193},{129,1},{193,65... | collective-permute-start | bytes 786440 | tf_op jit(solution)/shard_map/ppermute | solution.py:364
  32.9 3.1 %collective-permute-start.3 = (bf16[512,256]{1,0:T(8,128)(2,1)S(1)}, bf16[512,256]{1,0:T(8,128)(2,1)S(1)}, u32[]{:S(2)}, u32[]{:S(2)}) collective-permute-start(bf16[512,256]{1,0:T(8,128)(2,1)S(1)} %pad_maximum_fusion), channel_id=1, source_target_pairs={{0,192},{64,0},{128,64},{192,128},{1,193},{65,1},{129,65},{193,129... | collective-permute-start | bytes 786440 | tf_op jit(solution)/shard_map/ppermute | solution.py:364
  39.5 6.1 %shard_map.130 = (bf16[256,4096]{1,0:T(8,128)(2,1)}, bf16[8,256,512]{2,1,0:T(8,128)(2,1)}, bf16[256,2048]{1,0:T(8,128)(2,1)}, bf16[2048,256]{1,0:T(8,128)(2,1)},...) custom-call(s32[32]{0:T(128)} %reshape.37.refs_0_, ...), custom_call_target="tpu_custom_call" | custom-call | flops 1024 | bytes 1024 | tf_op jit(solution)/shard_map/pallas_call | solution.py:99
  47.1 4.1 %shard_map.131.refs_4_ = f32[256,256]{1,0:T(8,128)} custom-call(s32[32]{0:T(128)} %reshape.38.refs_1_.refs_0_, s32[2]{0:T(128)} %pad_add_fusion.refs_1_, bf16[256,256]{1,0:T(8,128)(2,1)} %refs_2_.3, bf16[256,256]{1,0:T(8,128)(2,1)} %copy-done.13, bf16[512,256]{1,0:T(8,128)(2,1)} %copy-done.17, bf16[512,256]{1,0:T(8,128)(2,1)} %copy-done.18, ...), custom_call_target="tpu_custom_call" | custom-call | flops 30000001024 | bytes 1024 | tf_op jit(solution)/shard_map/pallas_call | solution.py:99
  51.3 5.0 %all-to-all-done.refs_2_ = bf16[64,72,128]{2,1,0:T(8,128)(2,1)S(1)} async-done(((bf16[64,72,128]{2,1,0:T(8,128)(2,1)}), bf16[64,72,128]{2,1,0:T(8,128)(2,1)S(1)}, u32[]{:S(2)}, u32[]{:S(2)}) %all-to-all-start) | async-done | bytes 1179680 | tf_op jit(solution)/shard_map/all_to_all | solution.py:356
  57.3 4.9 %shard_map.132 = (bf16[256,256]{1,0:T(8,128)(2,1)}, bf16[256,256]{1,0:T(8,128)(2,1)}, bf16[256,256]{1,0:T(8,128)(2,1)}, f32[256,256]{1,0:T(8,128)}, f32[256,256]...) custom-call(s32[1]{0:T(128)} %bitcast.refs_2_.refs_0_, s32[1]{0:T(128)} %bitcast.1.refs_1_, ...), custom_call_target="tpu_custom_call" | custom-call | flops 1024 | bytes 1024 | tf_op jit(solution)/shard_map/pallas_call | solution.py:99
  70.4 12.2 %all-to-all-start.1 = ((f32[32,8,256]{2,1,0:T(8,128)}), f32[32,8,256]{2,1,0:T(8,128)S(1)}, u32[]{:S(2)}, u32[]{:S(2)}) async-start(f32[32,8,256]{2,1,0:T(8,128)} %shard_map.133), calls=%async_computation.1 | async-start | bytes 524288 | tf_op jit(solution)/shard_map/all_to_all | solution.py:356
  82.7 3.9 %shard_map.134 = (f32[512,256]{1,0:T(8,128)}, bf16[528,256]{1,0:T(8,128)(2,1)}, bf16[528,256]{1,0:T(8,128)(2,1)}, bf16[528,256]{1,0:T(8,128)(2,1)}) custom-call(s32[32]{0:T(128)} %reshape.37.refs_0_, s32[2]{0:T(128)} %pad_add_fusion.refs_1_, bf16[256,256]{1,0:T(8,128)(2,1)} %get-tuple-element.52.refs_2_, bf16[8,256,512]{2,1,0:T(8,128)(2,1)} %get-tuple-element.53.refs_3_), custom_call_target="tpu_custom_call" | custom-call | flops 1024 | bytes 1024 | tf_op jit(solution)/shard_map/pallas_call | solution.py:99
  89.4 5.3 %all-to-all-done.1.refs_0_ = f32[32,8,256]{2,1,0:T(8,128)S(1)} async-done(((f32[32,8,256]{2,1,0:T(8,128)}), f32[32,8,256]{2,1,0:T(8,128)S(1)}, u32[]{:S(2)}, u32[]{:S(2)}) %all-to-all-start.1) | async-done | bytes 262176 | tf_op jit(solution)/shard_map/all_to_all | solution.py:356
  97.0 6.9 %all-to-all-start.2 = ((bf16[32,64,256]{2,1,0:T(8,128)(2,1)}), bf16[32,64,256]{2,1,0:T(8,128)(2,1)S(1)}, u32[]{:S(2)}, u32[]{:S(2)}) async-start(bf16[32,64,256]{2,1,0:T(8,128)(2,1)} %shard_map.135), calls=%async_computation.2 | async-start | bytes 2097152 | tf_op jit(solution)/shard_map/all_to_all | solution.py:356
  103.9 2.7 %collective-permute-start.6 = (bf16[528,256]{1,0:T(8,128)(2,1)S(1)}, bf16[528,256]{1,0:T(8,128)(2,1)S(1)}, u32[]{:S(2)}, u32[]{:S(2)}) collective-permute-start(bf16[528,256]{1,0:T(8,128)(2,1)S(1)} %copy-done.7), channel_id=1, source_target_pairs={{0,64},{64,128},{128,192},{192,0},{1,65},{65,129},{129,193},{193,1... | collective-permute-start | bytes 811016 | tf_op jit(solution)/shard_map/ppermute | solution.py:364
  106.7 4.7 %collective-permute-start.7 = (bf16[528,256]{1,0:T(8,128)(2,1)S(1)}, bf16[528,256]{1,0:T(8,128)(2,1)S(1)}, u32[]{:S(2)}, u32[]{:S(2)}) collective-permute-start(bf16[528,256]{1,0:T(8,128)(2,1)S(1)} %copy-done.8), channel_id=1, source_target_pairs={{0,128},{64,192},{128,0},{192,64},{1,129},{65,193},{129,1},{193,65... | collective-permute-start | bytes 811016 | tf_op jit(solution)/shard_map/ppermute | solution.py:364
  111.4 3.1 %collective-permute-start.8 = (bf16[528,256]{1,0:T(8,128)(2,1)S(1)}, bf16[528,256]{1,0:T(8,128)(2,1)S(1)}, u32[]{:S(2)}, u32[]{:S(2)}) collective-permute-start(bf16[528,256]{1,0:T(8,128)(2,1)S(1)} %copy-done.9), channel_id=1, source_target_pairs={{0,192},{64,0},{128,64},{192,128},{1,193},{65,1},{129,65},{193,129... | collective-permute-start | bytes 811016 | tf_op jit(solution)/shard_map/ppermute | solution.py:364
  114.5 6.4 %collective-permute-done.7.refs_3_ = bf16[528,256]{1,0:T(8,128)(2,1)S(1)} collective-permute-done((bf16[528,256]{1,0:T(8,128)(2,1)S(1)}, bf16[528,256]{1,0:T(8,128)(2,1)S(1)}, u32[]{:S(2)}, u32[]{:S(2)}) %collective-permute-start.7) | collective-permute-done | bytes 270368 | tf_op jit(solution)/shard_map/ppermute | solution.py:364
  125.1 12.1 %collective-permute-start.9 = (f32[264,256]{1,0:T(8,128)}, f32[264,256]{1,0:T(8,128)S(1)}, u32[]{:S(2)}, u32[]{:S(2)}) collective-permute-start(f32[264,256]{1,0:T(8,128)} %get-tuple-element.67), channel_id=1, source_target_pairs={{0,256},{256,0},{1,257},{257,1},{2,258},{258,2},{3,259},{259,3},{4... | collective-permute-start | bytes 811016 | tf_op jit(solution)/shard_map/ppermute | solution.py:360
  137.2 5.3 %collective-permute-done.9.refs_1_.refs_5_ = f32[264,256]{1,0:T(8,128)S(1)} collective-permute-done((f32[264,256]{1,0:T(8,128)}, f32[264,256]{1,0:T(8,128)S(1)}, u32[]{:S(2)}, u32[]{:S(2)}) %collective-permute-start.9) | collective-permute-done | bytes 270368 | tf_op jit(solution)/shard_map/ppermute | solution.py:360
  144.7 11.0 %all-to-all-start.3 = ((f32[32,8,256]{2,1,0:T(8,128)}), f32[32,8,256]{2,1,0:T(8,128)S(1)}, u32[]{:S(2)}, u32[]{:S(2)}) async-start(f32[32,8,256]{2,1,0:T(8,128)} %shard_map.138), calls=%async_computation.3 | async-start | bytes 524288 | tf_op jit(solution)/shard_map/all_to_all | solution.py:356
  155.7 2.9 %shard_map.139 = bf16[256,256]{1,0:T(8,128)(2,1)} custom-call(bf16[256,256]{1,0:T(8,128)(2,1)} %get-tuple-element.70.refs_0_, bf16[256,256]{1,0:T(8,128)(2,1)} %refs_1_.1, bf16[256,2048]{1,0:T(8,128)(2,1)} %get-tuple-element.71.refs_2_, bf16[32,64,256]{2,1,0:T(8,128)(2,1)} %copy-done.1, f32[256,256]{1,0:T(8,128)} %get-tuple-element.72.refs_4_, ...), custom_call_target="tpu_custom_call" | custom-call | flops 1024 | bytes 1024 | tf_op jit(solution)/shard_map/pallas_call | solution.py:99
  158.7 9.4 %all-to-all-done.3 = f32[32,8,256]{2,1,0:T(8,128)S(1)} async-done(((f32[32,8,256]{2,1,0:T(8,128)}), f32[32,8,256]{2,1,0:T(8,128)S(1)}, u32[]{:S(2)}, u32[]{:S(2)}) %all-to-all-start.3) | async-done | bytes 262176 | tf_op jit(solution)/shard_map/all_to_all | solution.py:356
  168.1 5.8 %collective-permute-start.10 = (f32[256,256]{1,0:T(8,128)S(1)}, f32[256,256]{1,0:T(8,128)S(1)}, u32[]{:S(2)}, u32[]{:S(2)}) collective-permute-start(f32[256,256]{1,0:T(8,128)S(1)} %bitcast.16), channel_id=1, source_target_pairs={{0,1},{1,0},{2,3},{3,2},{4,5},{5,4},{6,7},{7,6},{8,9},{9,8},{10,11... | collective-permute-start | bytes 786440 | tf_op jit(solution)/shard_map/ppermute | solution.py:360
  (70 shorter events, 28.5 us)
Async XLA Ops:
  0.6 24.7 %collective-permute-start = (bf16[256,256]{1,0:T(8,128)(2,1)}, bf16[256,256]{1,0:T(8,128)(2,1)S(1)}, u32[]{:S(2)}, u32[]{:S(2)}) collective-permute-start(bf16[256,256]{1,0:T(8,128)(2,1)} %refs_2_.3), channel_id=1, source_target_pairs={{0,256},{256,0},{1,257},{257,1},{2,258},{258,2},{3,259},{259,3},{4... | collective-permute-start | bytes 393224 | tf_op jit(solution)/shard_map/ppermute | solution.py:360
  4.7 19.8 %copy-start.14 = (s32[1,64,32]{1,2,0:T(8,128)S(1)}, s32[1,64,32]{1,2,0:T(8,128)}, u32[]{:S(2)}) copy-start(s32[1,64,32]{1,2,0:T(8,128)} %param.19) | copy-start | bytes 24580
  4.7 20.7 %copy-start.2 = (bf16[256,256]{1,0:T(8,128)(2,1)S(1)}, bf16[256,256]{1,0:T(8,128)(2,1)}, u32[]{:S(2)}) copy-start(bf16[256,256]{1,0:T(8,128)(2,1)} %refs_2_.3) | copy-start | bytes 393220
  8.3 29.8 %copy-start.15 = (s32[1,8,4]{1,2,0:T(4,128)S(1)}, s32[1,8,4]{1,2,0:T(4,128)}, u32[]{:S(2)}) copy-start(s32[1,8,4]{1,2,0:T(4,128)} %param.15) | copy-start | bytes 388
  8.3 30.5 %copy-start.16 = (s32[1,8,4]{1,2,0:T(4,128)S(1)}, s32[1,8,4]{1,2,0:T(4,128)}, u32[]{:S(2)}) copy-start(s32[1,8,4]{1,2,0:T(4,128)} %param.16) | copy-start | bytes 388
  8.3 48.0 %all-to-all-start = ((bf16[64,72,128]{2,1,0:T(8,128)(2,1)}), bf16[64,72,128]{2,1,0:T(8,128)(2,1)S(1)}, u32[]{:S(2)}, u32[]{:S(2)}) async-start(bf16[64,72,128]{2,1,0:T(8,128)(2,1)} %shard_map.129), calls=%async_computation | async-start | bytes 2359296 | tf_op jit(solution)/shard_map/all_to_all | solution.py:356
  25.4 20.2 %copy-start.13 = (bf16[256,256]{1,0:T(8,128)(2,1)}, bf16[256,256]{1,0:T(8,128)(2,1)S(1)}, u32[]{:S(2)}) copy-start(bf16[256,256]{1,0:T(8,128)(2,1)S(1)} %collective-permute-done.refs_3_) | copy-start | bytes 393220
  25.4 20.8 %collective-permute-start.1 = (bf16[512,256]{1,0:T(8,128)(2,1)S(1)}, bf16[512,256]{1,0:T(8,128)(2,1)S(1)}, u32[]{:S(2)}, u32[]{:S(2)}) collective-permute-start(bf16[512,256]{1,0:T(8,128)(2,1)S(1)} %pad_maximum_fusion), channel_id=1, source_target_pairs={{0,64},{64,128},{128,192},{192,0},{1,65},{65,129},{129,193},{193,1... | collective-permute-start | bytes 786440 | tf_op jit(solution)/shard_map/ppermute | solution.py:364
  28.6 17.7 %collective-permute-start.2 = (bf16[512,256]{1,0:T(8,128)(2,1)S(1)}, bf16[512,256]{1,0:T(8,128)(2,1)S(1)}, u32[]{:S(2)}, u32[]{:S(2)}) collective-permute-start(bf16[512,256]{1,0:T(8,128)(2,1)S(1)} %pad_maximum_fusion), channel_id=1, source_target_pairs={{0,128},{64,192},{128,0},{192,64},{1,129},{65,193},{129,1},{193,65... | collective-permute-start | bytes 786440 | tf_op jit(solution)/shard_map/ppermute | solution.py:364
  32.9 13.3 %collective-permute-start.3 = (bf16[512,256]{1,0:T(8,128)(2,1)S(1)}, bf16[512,256]{1,0:T(8,128)(2,1)S(1)}, u32[]{:S(2)}, u32[]{:S(2)}) collective-permute-start(bf16[512,256]{1,0:T(8,128)(2,1)S(1)} %pad_maximum_fusion), channel_id=1, source_target_pairs={{0,192},{64,0},{128,64},{192,128},{1,193},{65,1},{129,65},{193,129... | collective-permute-start | bytes 786440 | tf_op jit(solution)/shard_map/ppermute | solution.py:364
  62.2 3.6 %collective-permute-start.4 = (f32[256,256]{1,0:T(8,128)}, f32[256,256]{1,0:T(8,128)S(1)}, u32[]{:S(2)}, u32[]{:S(2)}) collective-permute-start(f32[256,256]{1,0:T(8,128)} %get-tuple-element.50), channel_id=1, source_target_pairs={{0,1},{1,0},{2,3},{3,2},{4,5},{5,4},{6,7},{7,6},{8,9},{9,8},{10,11... | collective-permute-start | bytes 786440 | tf_op jit(solution)/shard_map/ppermute | solution.py:360
  68.4 18.2 %collective-permute-start.5 = (bf16[32,32,256]{2,1,0:T(8,128)(2,1)}, bf16[32,32,256]{2,1,0:T(8,128)(2,1)S(1)}, u32[]{:S(2)}, u32[]{:S(2)}) collective-permute-start(bf16[32,32,256]{2,1,0:T(8,128)(2,1)} %get-tuple-element.59), channel_id=1, source_target_pairs={{0,1},{1,0},{2,3},{3,2},{4,5},{5,4},{6,7},{7,6},{8,9},{9,8},{10,11... | collective-permute-start | bytes 1572872 | tf_op jit(solution)/shard_map/ppermute | solution.py:360
  70.4 24.2 %all-to-all-start.1 = ((f32[32,8,256]{2,1,0:T(8,128)}), f32[32,8,256]{2,1,0:T(8,128)S(1)}, u32[]{:S(2)}, u32[]{:S(2)}) async-start(f32[32,8,256]{2,1,0:T(8,128)} %shard_map.133), calls=%async_computation.1 | async-start | bytes 524288 | tf_op jit(solution)/shard_map/all_to_all | solution.py:356
  97.0 9.7 %copy-start.8 = (bf16[528,256]{1,0:T(8,128)(2,1)S(1)}, bf16[528,256]{1,0:T(8,128)(2,1)}, u32[]{:S(2)}) copy-start(bf16[528,256]{1,0:T(8,128)(2,1)} %get-tuple-element.64) | copy-start | bytes 811012
  97.0 14.4 %copy-start.9 = (bf16[528,256]{1,0:T(8,128)(2,1)S(1)}, bf16[528,256]{1,0:T(8,128)(2,1)}, u32[]{:S(2)}) copy-start(bf16[528,256]{1,0:T(8,128)(2,1)} %get-tuple-element.65) | copy-start | bytes 811012
  97.0 47.7 %all-to-all-start.2 = ((bf16[32,64,256]{2,1,0:T(8,128)(2,1)}), bf16[32,64,256]{2,1,0:T(8,128)(2,1)S(1)}, u32[]{:S(2)}, u32[]{:S(2)}) async-start(bf16[32,64,256]{2,1,0:T(8,128)(2,1)} %shard_map.135), calls=%async_computation.2 | async-start | bytes 2097152 | tf_op jit(solution)/shard_map/all_to_all | solution.py:356
  103.9 10.6 %collective-permute-start.6 = (bf16[528,256]{1,0:T(8,128)(2,1)S(1)}, bf16[528,256]{1,0:T(8,128)(2,1)S(1)}, u32[]{:S(2)}, u32[]{:S(2)}) collective-permute-start(bf16[528,256]{1,0:T(8,128)(2,1)S(1)} %copy-done.7), channel_id=1, source_target_pairs={{0,64},{64,128},{128,192},{192,0},{1,65},{65,129},{129,193},{193,1... | collective-permute-start | bytes 811016 | tf_op jit(solution)/shard_map/ppermute | solution.py:364
  106.7 14.3 %collective-permute-start.7 = (bf16[528,256]{1,0:T(8,128)(2,1)S(1)}, bf16[528,256]{1,0:T(8,128)(2,1)S(1)}, u32[]{:S(2)}, u32[]{:S(2)}) collective-permute-start(bf16[528,256]{1,0:T(8,128)(2,1)S(1)} %copy-done.8), channel_id=1, source_target_pairs={{0,128},{64,192},{128,0},{192,64},{1,129},{65,193},{129,1},{193,65... | collective-permute-start | bytes 811016 | tf_op jit(solution)/shard_map/ppermute | solution.py:364
  111.4 10.8 %collective-permute-start.8 = (bf16[528,256]{1,0:T(8,128)(2,1)S(1)}, bf16[528,256]{1,0:T(8,128)(2,1)S(1)}, u32[]{:S(2)}, u32[]{:S(2)}) collective-permute-start(bf16[528,256]{1,0:T(8,128)(2,1)S(1)} %copy-done.9), channel_id=1, source_target_pairs={{0,192},{64,0},{128,64},{192,128},{1,193},{65,1},{129,65},{193,129... | collective-permute-start | bytes 811016 | tf_op jit(solution)/shard_map/ppermute | solution.py:364
  114.5 7.7 %copy-start.6 = (bf16[528,256]{1,0:T(8,128)(2,1)}, bf16[528,256]{1,0:T(8,128)(2,1)S(1)}, u32[]{:S(2)}) copy-start(bf16[528,256]{1,0:T(8,128)(2,1)S(1)} %collective-permute-done.6.refs_2_) | copy-start | bytes 811012
  125.1 17.4 %collective-permute-start.9 = (f32[264,256]{1,0:T(8,128)}, f32[264,256]{1,0:T(8,128)S(1)}, u32[]{:S(2)}, u32[]{:S(2)}) collective-permute-start(f32[264,256]{1,0:T(8,128)} %get-tuple-element.67), channel_id=1, source_target_pairs={{0,256},{256,0},{1,257},{257,1},{2,258},{258,2},{3,259},{259,3},{4... | collective-permute-start | bytes 811016 | tf_op jit(solution)/shard_map/ppermute | solution.py:360
  144.7 11.0 %copy-start.1 = (bf16[32,64,256]{2,1,0:T(8,128)(2,1)}, bf16[32,64,256]{2,1,0:T(8,128)(2,1)S(1)}, u32[]{:S(2)}) copy-start(bf16[32,64,256]{2,1,0:T(8,128)(2,1)S(1)} %all-to-all-done.2.refs_3_) | copy-start | bytes 3145732
  144.7 23.4 %all-to-all-start.3 = ((f32[32,8,256]{2,1,0:T(8,128)}), f32[32,8,256]{2,1,0:T(8,128)S(1)}, u32[]{:S(2)}, u32[]{:S(2)}) async-start(f32[32,8,256]{2,1,0:T(8,128)} %shard_map.138), calls=%async_computation.3 | async-start | bytes 524288 | tf_op jit(solution)/shard_map/all_to_all | solution.py:356
  168.1 7.0 %collective-permute-start.10 = (f32[256,256]{1,0:T(8,128)S(1)}, f32[256,256]{1,0:T(8,128)S(1)}, u32[]{:S(2)}, u32[]{:S(2)}) collective-permute-start(f32[256,256]{1,0:T(8,128)S(1)} %bitcast.16), channel_id=1, source_target_pairs={{0,1},{1,0},{2,3},{3,2},{4,5},{5,4},{6,7},{7,6},{8,9},{9,8},{10,11... | collective-permute-start | bytes 786440 | tf_op jit(solution)/shard_map/ppermute | solution.py:360
  (11 other events, 15.2 us)

commit v6 on v5

--- a/solution.py
+++ b/solution.py
@@ -269,7 +269,13 @@
 
 def add_kernel(got, keep, out):
     total = keep()[...] + got()[...]
-    out.ref[...] = total.reshape(out.ref.shape)
+    wide = total.shape[1] // LANES
+    per = out.ref.shape[1] // 8
+    for i in range(out.ref.shape[0] * per):
+        r, c, k = i // wide, i % wide, i % per
+        out.ref[i // per, 8 * k : 8 * (k + 1), :] = total[
+            8 * r : 8 * (r + 1), c * LANES : (c + 1) * LANES
+        ]
 
 
 def assemble_kernel(got, out):
@@ -300,36 +306,30 @@
 
 def sum_far_kernel(got, out, *rest):
     total = jnp.sum(got()[...], axis=0)
-    rows = total.shape[0]
     high = total.astype(BF16)
     low = (total - high.astype(F32)).astype(BF16)
     for behind in rest:
-        behind.ref[:rows, :] = high
-        behind.ref[rows:, :] = low
+        behind.ref[:, :LANES] = high
+        behind.ref[:, LANES:] = low
         behind.send()
     out.ref[...] = total
 
 
-def sum_x_kernel(own, chunk, *rest):
-    terms, (here, keep, message) = rest[:-3], rest[-3:]
-    rows, small = here.ref.shape[0], keep.ref.shape[0]
+def sum_x_kernel(own, part, *rest):
+    messages, (tiles, there, here) = rest[:-3], rest[-3:]
+    rows = here.ref.shape[0]
+    small = part()[...]
     total = own()[...]
-    part = chunk()[...]
-    for term in terms:
-        ref = term()
+    for message in messages:
+        ref = message()
+        both = ref[2 * rows :, :].astype(F32)
+        small = small + (both[:, :LANES] + both[:, LANES:])
         total = total + ref[: 2 * rows, :].astype(F32)
-        both = ref[2 * rows :, :].astype(F32)
-        part = part + (both[:small] + both[small:])
-    message.ref[:rows, :] = total[rows:]
-    message.ref[rows:, :] = part
-    message.send()
-    keep.ref[...] = part
+    tiles.ref[...] = jnp.broadcast_to(small[None], tiles.ref.shape)
+    tiles.send()
+    there.ref[...] = total[rows:]
+    there.send()
     here.ref[...] = total[:rows]
-
-
-def sum_y_kernel(keep, got, out):
-    total = keep()[...] + got()[...]
-    out.ref[...] = jnp.broadcast_to(total[None], out.ref.shape)
 
 
 def final_kernel(dpre, self_weight, hub_t, back, here, got, out):
@@ -342,10 +342,6 @@
         rows = back_ref[:, i * hub : (i + 1) * hub, :].reshape(half, width)
         total = total + dot(hub_ref[:, i * half : (i + 1) * half], rows)
     out.ref[...] = (total + here()[...] + got()[...]).astype(BF16)
-
-
-def square32_pair(rows, width):
-    return shape((2 * rows, width), F32)
 
 
 def as_list(x):
@@ -380,7 +376,6 @@
     high = (width // LANES) * hub + EXTRA
     far = lax.axis_size("far")
     nx = lax.axis_size("x")
-    chunk = width // far
     core = lax.axis_index("core").astype(jnp.int32)
     core1 = core.reshape(1)
     me = (lax.axis_index("far") * 2 + core).astype(jnp.int32).reshape(1)
@@ -438,48 +433,42 @@
         ),
         [pltpu.VMEM((slots, width + 2 * LANES), BF16)],
     )
-    both = call(add_kernel, [shape((far, chunk, width), F32)], (), (swap(wsend, "core"), wkeep))
-    scattered = exchange(both, "far")
-    tall = 2 * rows + 2 * chunk
+    deep = width * width // (2 * far * LANES)
+    tiles = shape((2 * far, deep, LANES), F32)
+    both = call(add_kernel, [tiles], (), (swap(wsend, "core"), wkeep))
+    scattered = exchange(both, ("y", "far"))
+    packed = call(
+        assemble_kernel, [], (), (swap(after(hsend, both), "core"),),
+        into=[(packed, (ALL, slice(hub, 2 * hub)))],
+    )
+    tall = 2 * rows + deep
     terms = call(
         panels_kernel,
-        [square32_pair(rows, width)]
+        [shape((2 * rows, width), F32)]
         + [(shape((tall, width), BF16), (slice(0, 2 * rows),))] * (nx - 1),
         (dest, here), (after(gn, both), back), [pltpu.VMEM((per * tile, width), BF16)],
     )
-    terms = terms if nx > 1 else [terms]
-    hsend = after(hsend, both)
-    packed = call(
-        assemble_kernel, [], (), (swap(hsend, "core"),),
-        into=[(packed, (ALL, slice(hub, 2 * hub)))],
-    )
+    terms = [terms] if nx == 1 else terms
     scattered = after(scattered, (terms, packed))
+    gathered = exchange(after(packed, scattered), "far")
     tail = (slice(2 * rows, tall),)
-    part, *behind = as_list(
+    part, *messages = as_list(
         call(
-            sum_far_kernel, [shape((chunk, width), F32)], (), (scattered,),
+            sum_far_kernel, [shape((deep, LANES), F32)], (), (scattered,),
             into=[(x, tail) for x in terms[1:]],
         )
     )
-    gathered = exchange(after(packed, part), "far")
-    arrived = [along_x(behind[k - 1], k, nx) for k in range(1, nx)]
-    panel_here, keep, message = call(
-        sum_x_kernel, [square32, shape((chunk, width), F32), shape((rows + chunk, width), F32)],
-        (), (terms[0], part, *arrived),
-    )
-    message = swap(message, "y")
-    total = call(
-        sum_y_kernel, [shape((far, chunk, width), F32)], (),
-        (keep, (message, (slice(rows, rows + chunk),))),
+    arrived = [along_x(messages[k - 1], k, nx) for k in range(1, nx)]
+    total, panel_there, panel_here = call(
+        sum_x_kernel, [tiles, square32, square32], (), (terms[0], part, *arrived)
     )
     total = after(total, gathered)
-    mine = exchange(total, "far").reshape(width, width)
+    panel_got = swap(after(panel_there, gathered), "y")
+    mine = exchange(total, ("y", "far")).reshape(width // 8, width // LANES, 8, LANES)
+    mine = jnp.swapaxes(mine, 1, 2).reshape(width, width)
     feat_grad = call(
         final_kernel, [square], (),
-        (
-            after(dpre, total), self_weight, hub_t, gathered, panel_here,
-            (message, (slice(0, rows),)),
-        ),
+        (after(dpre, total), self_weight, hub_t, gathered, panel_here, panel_got),
     )
     theirs = swap(after(mine, feat_grad), "core")
     self_grad = jnp.where(core == 0, mine, theirs)

time: 179 us -> 170 us (0.950)
  starting transfers between devices: 93.3 us -> 90.7 us
  waiting for transfers between devices: 35.6 us -> 33.1 us
    ppermute x5, starting transfers between devices: 25.9 us -> 15.3 us  [swap(): return lax.ppermute(x, axis, [(0, 1), (1, 0)])]
    all_to_all x4, starting transfers between devices: 46.3 us -> 53.5 us  [exchange(): return lax.all_to_all(x, axis, split_axis=0, concat_axis=0, tiled=True)]
    all_to_all x4, waiting for transfers between devices: 19.7 us -> 12.9 us  [exchange(): return lax.all_to_all(x, axis, split_axis=0, concat_axis=0, tiled=True)]
    ppermute x5, waiting for transfers between devices: 8.2 us -> 12 us  [swap(): return lax.ppermute(x, axis, [(0, 1), (1, 0)])]
    pallas_call x11 -> x10, Pallas kernels: 34.5 us -> 33.2 us  [call(): pl.pallas_call(body, out_shape=[shape(x.shape, x.dtype) for x, _ in outs]...]
    unnamed x43 -> x37, local copies, waits for them, and re-layouts: 5.81 us -> 5.08 us
  transfers between devices with their start and end apart: 15 -> 15, of which waited for: 8 -> 8; matrix products, arithmetic and copies ran while one was open for 3% -> 3% of each run, Pallas kernels for 15% -> 16%
where the time goes in v6:
time: 170 us; the launch traced here: 169 us
  starting transfers between devices  90.7 us (53%)
  Pallas kernels  33.2 us (20%)
  waiting for transfers between devices  33.1 us (19%)
  local copies, waits for them, and re-layouts  9.11 us (5%)
    all_to_all x4, starting transfers between devices, exchange(): return lax.all_to_all(x, axis, split_axis=0, concat_axis=0, tiled=True)  53.5 us
    pallas_call x10, Pallas kernels, call(): pl.pallas_call(body, out_shape=[shape(x.shape, x.dtype) for x, _ in outs]...  33.2 us
    ppermute x6, starting transfers between devices, along_x(): return lax.ppermute(x, 'x', [(i, (i + step) % nx) for i in range(nx)])  21.8 us
    ppermute x5, starting transfers between devices, swap(): return lax.ppermute(x, axis, [(0, 1), (1, 0)])  15.3 us
    all_to_all x4, waiting for transfers between devices, exchange(): return lax.all_to_all(x, axis, split_axis=0, concat_axis=0, tiled=True)  12.9 us
    ppermute x5, waiting for transfers between devices, swap(): return lax.ppermute(x, axis, [(0, 1), (1, 0)])  12 us
    ppermute x6, waiting for transfers between devices, along_x(): return lax.ppermute(x, 'x', [(i, (i + step) % nx) for i in range(nx)])  8.2 us
    unnamed x37, local copies, waits for them, and re-layouts  5.08 us
  transfers between devices with their start and end apart: 15, of which 8 were waited for; matrix products, arithmetic and copies ran while one was open for 3% of the time, Pallas kernels for 16%

profile of v6, /device:TPU:1, one launch (start us, length us, event | category | flops | bytes accessed | tf_op | source)
XLA Modules:
  0.0 168.6 jit_solution(4351207886021056676)
XLA Ops:
  0.6 4.0 %collective-permute-start = (bf16[256,256]{1,0:T(8,128)(2,1)}, bf16[256,256]{1,0:T(8,128)(2,1)S(1)}, u32[]{:S(2)}, u32[]{:S(2)}) collective-permute-start(bf16[256,256]{1,0:T(8,128)(2,1)} %refs_2_.3), channel_id=1, source_target_pairs={{0,256},{256,0},{1,257},{257,1},{2,258},{258,2},{3,259},{259,3},{4... | collective-permute-start | bytes 393224 | tf_op jit(solution)/shard_map/ppermute | solution.py:356
  4.7 3.6 %shard_map.129 = bf16[64,72,128]{2,1,0:T(8,128)(2,1)} custom-call(s32[64]{0:T(128)} %bitcast.22, bf16[64,32,128]{2,1,0:T(8,128)(2,1)} %bitcast.15, bf16[256,256]{1,0:T(8,128)(2,1)} %refs_2_.3), custom_call_target="tpu_custom_call" | custom-call | flops 1024 | bytes 1024 | tf_op jit(solution)/shard_map/pallas_call | solution.py:99
  8.3 16.2 %all-to-all-start = ((bf16[64,72,128]{2,1,0:T(8,128)(2,1)}), bf16[64,72,128]{2,1,0:T(8,128)(2,1)S(1)}, u32[]{:S(2)}, u32[]{:S(2)}) async-start(bf16[64,72,128]{2,1,0:T(8,128)(2,1)} %shard_map.129), calls=%async_computation | async-start | bytes 2359296 | tf_op jit(solution)/shard_map/all_to_all | solution.py:352
  25.4 3.1 %collective-permute-start.1 = (bf16[512,256]{1,0:T(8,128)(2,1)S(1)}, bf16[512,256]{1,0:T(8,128)(2,1)S(1)}, u32[]{:S(2)}, u32[]{:S(2)}) collective-permute-start(bf16[512,256]{1,0:T(8,128)(2,1)S(1)} %pad_maximum_fusion), channel_id=1, source_target_pairs={{0,64},{64,128},{128,192},{192,0},{1,65},{65,129},{129,193},{193,1... | collective-permute-start | bytes 786440 | tf_op jit(solution)/shard_map/ppermute | solution.py:360
  28.6 4.4 %collective-permute-start.2 = (bf16[512,256]{1,0:T(8,128)(2,1)S(1)}, bf16[512,256]{1,0:T(8,128)(2,1)S(1)}, u32[]{:S(2)}, u32[]{:S(2)}) collective-permute-start(bf16[512,256]{1,0:T(8,128)(2,1)S(1)} %pad_maximum_fusion), channel_id=1, source_target_pairs={{0,128},{64,192},{128,0},{192,64},{1,129},{65,193},{129,1},{193,65... | collective-permute-start | bytes 786440 | tf_op jit(solution)/shard_map/ppermute | solution.py:360
  32.9 3.1 %collective-permute-start.3 = (bf16[512,256]{1,0:T(8,128)(2,1)S(1)}, bf16[512,256]{1,0:T(8,128)(2,1)S(1)}, u32[]{:S(2)}, u32[]{:S(2)}) collective-permute-start(bf16[512,256]{1,0:T(8,128)(2,1)S(1)} %pad_maximum_fusion), channel_id=1, source_target_pairs={{0,192},{64,0},{128,64},{192,128},{1,193},{65,1},{129,65},{193,129... | collective-permute-start | bytes 786440 | tf_op jit(solution)/shard_map/ppermute | solution.py:360
  39.5 6.1 %shard_map.130 = (bf16[256,4096]{1,0:T(8,128)(2,1)}, bf16[8,256,512]{2,1,0:T(8,128)(2,1)}, bf16[256,2048]{1,0:T(8,128)(2,1)}, bf16[2048,256]{1,0:T(8,128)(2,1)},...) custom-call(s32[32]{0:T(128)} %reshape.40.refs_0_, ...), custom_call_target="tpu_custom_call" | custom-call | flops 1024 | bytes 1024 | tf_op jit(solution)/shard_map/pallas_call | solution.py:99
  47.1 4.1 %shard_map.131.refs_4_ = f32[256,256]{1,0:T(8,128)} custom-call(s32[32]{0:T(128)} %reshape.41.refs_1_.refs_0_, s32[2]{0:T(128)} %pad_add_fusion.refs_1_, bf16[256,256]{1,0:T(8,128)(2,1)} %refs_2_.3, bf16[256,256]{1,0:T(8,128)(2,1)} %copy-done.10, bf16[512,256]{1,0:T(8,128)(2,1)} %copy-done.14, bf16[512,256]{1,0:T(8,128)(2,1)} %copy-done.15, ...), custom_call_target="tpu_custom_call" | custom-call | flops 30000001024 | bytes 1024 | tf_op jit(solution)/shard_map/pallas_call | solution.py:99
  51.3 5.1 %all-to-all-done.refs_2_ = bf16[64,72,128]{2,1,0:T(8,128)(2,1)S(1)} async-done(((bf16[64,72,128]{2,1,0:T(8,128)(2,1)}), bf16[64,72,128]{2,1,0:T(8,128)(2,1)S(1)}, u32[]{:S(2)}, u32[]{:S(2)}) %all-to-all-start) | async-done | bytes 1179680 | tf_op jit(solution)/shard_map/all_to_all | solution.py:352
  57.3 4.9 %shard_map.132 = (bf16[256,256]{1,0:T(8,128)(2,1)}, bf16[256,256]{1,0:T(8,128)(2,1)}, bf16[256,256]{1,0:T(8,128)(2,1)}, f32[256,256]{1,0:T(8,128)}, f32[256,256]...) custom-call(s32[1]{0:T(128)} %bitcast.refs_2_.refs_0_, s32[1]{0:T(128)} %bitcast.1.refs_1_, ...), custom_call_target="tpu_custom_call" | custom-call | flops 1024 | bytes 1024 | tf_op jit(solution)/shard_map/pallas_call | solution.py:99
  70.5 21.4 %all-to-all-start.1 = ((f32[64,8,128]{2,1,0:T(8,128)}), f32[64,8,128]{2,1,0:T(8,128)S(1)}, u32[]{:S(2)}, u32[]{:S(2)}) async-start(f32[64,8,128]{2,1,0:T(8,128)} %shard_map.133), calls=%async_computation.1 | async-start | bytes 524288 | tf_op jit(solution)/shard_map/all_to_all | solution.py:352
  91.9 3.9 %shard_map.134 = (f32[512,256]{1,0:T(8,128)}, bf16[520,256]{1,0:T(8,128)(2,1)}, bf16[520,256]{1,0:T(8,128)(2,1)}, bf16[520,256]{1,0:T(8,128)(2,1)}) custom-call(s32[32]{0:T(128)} %reshape.40.refs_0_, s32[2]{0:T(128)} %pad_add_fusion.refs_1_, bf16[256,256]{1,0:T(8,128)(2,1)} %get-tuple-element.53.refs_2_, bf16[8,256,512]{2,1,0:T(8,128)(2,1)} %get-tuple-element.54.refs_3_), custom_call_target="tpu_custom_call" | custom-call | flops 1024 | bytes 1024 | tf_op jit(solution)/shard_map/pallas_call | solution.py:99
  98.6 7.5 %all-to-all-done.1.refs_0_ = f32[64,8,128]{2,1,0:T(8,128)S(1)} async-done(((f32[64,8,128]{2,1,0:T(8,128)}), f32[64,8,128]{2,1,0:T(8,128)S(1)}, u32[]{:S(2)}, u32[]{:S(2)}) %all-to-all-start.1) | async-done | bytes 262176 | tf_op jit(solution)/shard_map/all_to_all | solution.py:352
  106.1 4.0 %all-to-all-start.2 = ((bf16[32,64,256]{2,1,0:T(8,128)(2,1)}), bf16[32,64,256]{2,1,0:T(8,128)(2,1)S(1)}, u32[]{:S(2)}, u32[]{:S(2)}) async-start(bf16[32,64,256]{2,1,0:T(8,128)(2,1)} %shard_map.135), calls=%async_computation.2 | async-start | bytes 2097152 | tf_op jit(solution)/shard_map/all_to_all | solution.py:352
  111.8 3.2 %collective-permute-start.6 = (bf16[520,256]{1,0:T(8,128)(2,1)}, bf16[520,256]{1,0:T(8,128)(2,1)S(1)}, u32[]{:S(2)}, u32[]{:S(2)}) collective-permute-start(bf16[520,256]{1,0:T(8,128)(2,1)} %get-tuple-element.64), channel_id=1, source_target_pairs={{0,64},{64,128},{128,192},{192,0},{1,65},{65,129},{129,193},{193,1... | collective-permute-start | bytes 798728 | tf_op jit(solution)/shard_map/ppermute | solution.py:360
  114.9 5.8 %collective-permute-start.7 = (bf16[520,256]{1,0:T(8,128)(2,1)}, bf16[520,256]{1,0:T(8,128)(2,1)S(1)}, u32[]{:S(2)}, u32[]{:S(2)}) collective-permute-start(bf16[520,256]{1,0:T(8,128)(2,1)} %get-tuple-element.65), channel_id=1, source_target_pairs={{0,128},{64,192},{128,0},{192,64},{1,129},{65,193},{129,1},{193,65... | collective-permute-start | bytes 798728 | tf_op jit(solution)/shard_map/ppermute | solution.py:360
  120.7 2.4 %collective-permute-start.8 = (bf16[520,256]{1,0:T(8,128)(2,1)}, bf16[520,256]{1,0:T(8,128)(2,1)S(1)}, u32[]{:S(2)}, u32[]{:S(2)}) collective-permute-start(bf16[520,256]{1,0:T(8,128)(2,1)} %get-tuple-element.66), channel_id=1, source_target_pairs={{0,192},{64,0},{128,64},{192,128},{1,193},{65,1},{129,65},{193,129... | collective-permute-start | bytes 798728 | tf_op jit(solution)/shard_map/ppermute | solution.py:360
  123.1 6.2 %collective-permute-done.7.refs_3_ = bf16[520,256]{1,0:T(8,128)(2,1)S(1)} collective-permute-done((bf16[520,256]{1,0:T(8,128)(2,1)}, bf16[520,256]{1,0:T(8,128)(2,1)S(1)}, u32[]{:S(2)}, u32[]{:S(2)}) %collective-permute-start.7) | collective-permute-done | bytes 266272 | tf_op jit(solution)/shard_map/ppermute | solution.py:360
  132.0 2.2 %shard_map.137 = (f32[64,8,128]{2,1,0:T(8,128)}, f32[256,256]{1,0:T(8,128)}, f32[256,256]{1,0:T(8,128)}) custom-call(f32[512,256]{1,0:T(8,128)} %get-tuple-element.55.refs_0_, f32[8,128]{1,0:T(8,128)} %get-tuple-element.63.refs_1_, bf16[520,256]{1,0:T(8,128)(2,1)} %copy-done.5, bf16[520,256]{1,0:T(8,128)(2,1)} %copy-done.6, bf16[520,256]{1,0:T(8,128)(2,1)} %copy-done.7), custom_call_target="tpu_custom_call" | custom-call | flops 1024 | bytes 1024 | tf_op jit(solution)/shard_map/pallas_call | solution.py:99
  134.6 11.9 %all-to-all-start.3 = ((f32[64,8,128]{2,1,0:T(8,128)}), f32[64,8,128]{2,1,0:T(8,128)S(1)}, u32[]{:S(2)}, u32[]{:S(2)}) async-start(f32[64,8,128]{2,1,0:T(8,128)} %get-tuple-element.69), calls=%async_computation.3 | async-start | bytes 524288 | tf_op jit(solution)/shard_map/all_to_all | solution.py:352
  146.5 3.0 %collective-permute-start.9 = (f32[256,256]{1,0:T(8,128)}, f32[256,256]{1,0:T(8,128)S(1)}, u32[]{:S(2)}, u32[]{:S(2)}) collective-permute-start(f32[256,256]{1,0:T(8,128)} %get-tuple-element.74), channel_id=1, source_target_pairs={{0,256},{256,0},{1,257},{257,1},{2,258},{258,2},{3,259},{259,3},{4... | collective-permute-start | bytes 786440 | tf_op jit(solution)/shard_map/ppermute | solution.py:356
  149.5 9.2 %collective-permute-done.9.refs_5_ = f32[256,256]{1,0:T(8,128)S(1)} collective-permute-done((f32[256,256]{1,0:T(8,128)}, f32[256,256]{1,0:T(8,128)S(1)}, u32[]{:S(2)}, u32[]{:S(2)}) %collective-permute-start.9) | collective-permute-done | bytes 262176 | tf_op jit(solution)/shard_map/ppermute | solution.py:356
  159.4 2.9 %shard_map.138 = bf16[256,256]{1,0:T(8,128)(2,1)} custom-call(bf16[256,256]{1,0:T(8,128)(2,1)} %get-tuple-element.70.refs_0_, bf16[256,256]{1,0:T(8,128)(2,1)} %refs_1_.1, bf16[256,2048]{1,0:T(8,128)(2,1)} %get-tuple-element.71.refs_2_, bf16[32,64,256]{2,1,0:T(8,128)(2,1)} %copy-done.1, f32[256,256]{1,0:T(8,128)} %get-tuple-element.72.refs_4_, ...), custom_call_target="tpu_custom_call" | custom-call | flops 1024 | bytes 1024 | tf_op jit(solution)/shard_map/pallas_call | solution.py:99
  162.3 4.3 %collective-permute-start.10 = (f32[256,256]{1,0:T(8,128)S(1)}, f32[256,256]{1,0:T(8,128)S(1)}, u32[]{:S(2)}, u32[]{:S(2)}) collective-permute-start(f32[256,256]{1,0:T(8,128)S(1)} %bitcast.18), channel_id=1, source_target_pairs={{0,1},{1,0},{2,3},{3,2},{4,5},{5,4},{6,7},{7,6},{8,9},{9,8},{10,11... | collective-permute-start | bytes 786440 | tf_op jit(solution)/shard_map/ppermute | solution.py:356
  (63 shorter events, 25.3 us)
Async XLA Ops:
  0.6 24.7 %collective-permute-start = (bf16[256,256]{1,0:T(8,128)(2,1)}, bf16[256,256]{1,0:T(8,128)(2,1)S(1)}, u32[]{:S(2)}, u32[]{:S(2)}) collective-permute-start(bf16[256,256]{1,0:T(8,128)(2,1)} %refs_2_.3), channel_id=1, source_target_pairs={{0,256},{256,0},{1,257},{257,1},{2,258},{258,2},{3,259},{259,3},{4... | collective-permute-start | bytes 393224 | tf_op jit(solution)/shard_map/ppermute | solution.py:356
  4.7 19.8 %copy-start.11 = (s32[1,64,32]{1,2,0:T(8,128)S(1)}, s32[1,64,32]{1,2,0:T(8,128)}, u32[]{:S(2)}) copy-start(s32[1,64,32]{1,2,0:T(8,128)} %param.19) | copy-start | bytes 24580
  4.7 20.7 %copy-start.2 = (bf16[256,256]{1,0:T(8,128)(2,1)S(1)}, bf16[256,256]{1,0:T(8,128)(2,1)}, u32[]{:S(2)}) copy-start(bf16[256,256]{1,0:T(8,128)(2,1)} %refs_2_.3) | copy-start | bytes 393220
  8.3 29.8 %copy-start.12 = (s32[1,8,4]{1,2,0:T(4,128)S(1)}, s32[1,8,4]{1,2,0:T(4,128)}, u32[]{:S(2)}) copy-start(s32[1,8,4]{1,2,0:T(4,128)} %param.15) | copy-start | bytes 388
  8.3 30.5 %copy-start.13 = (s32[1,8,4]{1,2,0:T(4,128)S(1)}, s32[1,8,4]{1,2,0:T(4,128)}, u32[]{:S(2)}) copy-start(s32[1,8,4]{1,2,0:T(4,128)} %param.16) | copy-start | bytes 388
  8.3 48.0 %all-to-all-start = ((bf16[64,72,128]{2,1,0:T(8,128)(2,1)}), bf16[64,72,128]{2,1,0:T(8,128)(2,1)S(1)}, u32[]{:S(2)}, u32[]{:S(2)}) async-start(bf16[64,72,128]{2,1,0:T(8,128)(2,1)} %shard_map.129), calls=%async_computation | async-start | bytes 2359296 | tf_op jit(solution)/shard_map/all_to_all | solution.py:352
  25.4 20.1 %copy-start.10 = (bf16[256,256]{1,0:T(8,128)(2,1)}, bf16[256,256]{1,0:T(8,128)(2,1)S(1)}, u32[]{:S(2)}) copy-start(bf16[256,256]{1,0:T(8,128)(2,1)S(1)} %collective-permute-done.refs_3_) | copy-start | bytes 393220
  25.4 20.8 %collective-permute-start.1 = (bf16[512,256]{1,0:T(8,128)(2,1)S(1)}, bf16[512,256]{1,0:T(8,128)(2,1)S(1)}, u32[]{:S(2)}, u32[]{:S(2)}) collective-permute-start(bf16[512,256]{1,0:T(8,128)(2,1)S(1)} %pad_maximum_fusion), channel_id=1, source_target_pairs={{0,64},{64,128},{128,192},{192,0},{1,65},{65,129},{129,193},{193,1... | collective-permute-start | bytes 786440 | tf_op jit(solution)/shard_map/ppermute | solution.py:360
  28.6 17.7 %collective-permute-start.2 = (bf16[512,256]{1,0:T(8,128)(2,1)S(1)}, bf16[512,256]{1,0:T(8,128)(2,1)S(1)}, u32[]{:S(2)}, u32[]{:S(2)}) collective-permute-start(bf16[512,256]{1,0:T(8,128)(2,1)S(1)} %pad_maximum_fusion), channel_id=1, source_target_pairs={{0,128},{64,192},{128,0},{192,64},{1,129},{65,193},{129,1},{193,65... | collective-permute-start | bytes 786440 | tf_op jit(solution)/shard_map/ppermute | solution.py:360
  32.9 13.3 %collective-permute-start.3 = (bf16[512,256]{1,0:T(8,128)(2,1)S(1)}, bf16[512,256]{1,0:T(8,128)(2,1)S(1)}, u32[]{:S(2)}, u32[]{:S(2)}) collective-permute-start(bf16[512,256]{1,0:T(8,128)(2,1)S(1)} %pad_maximum_fusion), channel_id=1, source_target_pairs={{0,192},{64,0},{128,64},{192,128},{1,193},{65,1},{129,65},{193,129... | collective-permute-start | bytes 786440 | tf_op jit(solution)/shard_map/ppermute | solution.py:360
  62.3 3.6 %collective-permute-start.4 = (f32[256,256]{1,0:T(8,128)}, f32[256,256]{1,0:T(8,128)S(1)}, u32[]{:S(2)}, u32[]{:S(2)}) collective-permute-start(f32[256,256]{1,0:T(8,128)} %get-tuple-element.51), channel_id=1, source_target_pairs={{0,1},{1,0},{2,3},{3,2},{4,5},{5,4},{6,7},{7,6},{8,9},{9,8},{10,11... | collective-permute-start | bytes 786440 | tf_op jit(solution)/shard_map/ppermute | solution.py:356
  68.4 27.4 %collective-permute-start.5 = (bf16[32,32,256]{2,1,0:T(8,128)(2,1)}, bf16[32,32,256]{2,1,0:T(8,128)(2,1)S(1)}, u32[]{:S(2)}, u32[]{:S(2)}) collective-permute-start(bf16[32,32,256]{2,1,0:T(8,128)(2,1)} %get-tuple-element.60), channel_id=1, source_target_pairs={{0,1},{1,0},{2,3},{3,2},{4,5},{5,4},{6,7},{7,6},{8,9},{9,8},{10,11... | collective-permute-start | bytes 1572872 | tf_op jit(solution)/shard_map/ppermute | solution.py:356
  70.5 35.6 %all-to-all-start.1 = ((f32[64,8,128]{2,1,0:T(8,128)}), f32[64,8,128]{2,1,0:T(8,128)S(1)}, u32[]{:S(2)}, u32[]{:S(2)}) async-start(f32[64,8,128]{2,1,0:T(8,128)} %shard_map.133), calls=%async_computation.1 | async-start | bytes 524288 | tf_op jit(solution)/shard_map/all_to_all | solution.py:352
  106.1 4.0 %copy-start.3 = (f32[64,8,128]{2,1,0:T(8,128)}, f32[64,8,128]{2,1,0:T(8,128)S(1)}, u32[]{:S(2)}) copy-start(f32[64,8,128]{2,1,0:T(8,128)S(1)} %all-to-all-done.1.refs_0_) | copy-start | bytes 786436
  106.1 28.5 %all-to-all-start.2 = ((bf16[32,64,256]{2,1,0:T(8,128)(2,1)}), bf16[32,64,256]{2,1,0:T(8,128)(2,1)S(1)}, u32[]{:S(2)}, u32[]{:S(2)}) async-start(bf16[32,64,256]{2,1,0:T(8,128)(2,1)} %shard_map.135), calls=%async_computation.2 | async-start | bytes 2097152 | tf_op jit(solution)/shard_map/all_to_all | solution.py:352
  111.8 11.3 %collective-permute-start.6 = (bf16[520,256]{1,0:T(8,128)(2,1)}, bf16[520,256]{1,0:T(8,128)(2,1)S(1)}, u32[]{:S(2)}, u32[]{:S(2)}) collective-permute-start(bf16[520,256]{1,0:T(8,128)(2,1)} %get-tuple-element.64), channel_id=1, source_target_pairs={{0,64},{64,128},{128,192},{192,0},{1,65},{65,129},{129,193},{193,1... | collective-permute-start | bytes 798728 | tf_op jit(solution)/shard_map/ppermute | solution.py:360
  114.9 14.3 %collective-permute-start.7 = (bf16[520,256]{1,0:T(8,128)(2,1)}, bf16[520,256]{1,0:T(8,128)(2,1)S(1)}, u32[]{:S(2)}, u32[]{:S(2)}) collective-permute-start(bf16[520,256]{1,0:T(8,128)(2,1)} %get-tuple-element.65), channel_id=1, source_target_pairs={{0,128},{64,192},{128,0},{192,64},{1,129},{65,193},{129,1},{193,65... | collective-permute-start | bytes 798728 | tf_op jit(solution)/shard_map/ppermute | solution.py:360
  120.7 10.6 %collective-permute-start.8 = (bf16[520,256]{1,0:T(8,128)(2,1)}, bf16[520,256]{1,0:T(8,128)(2,1)S(1)}, u32[]{:S(2)}, u32[]{:S(2)}) collective-permute-start(bf16[520,256]{1,0:T(8,128)(2,1)} %get-tuple-element.66), channel_id=1, source_target_pairs={{0,192},{64,0},{128,64},{192,128},{1,193},{65,1},{129,65},{193,129... | collective-permute-start | bytes 798728 | tf_op jit(solution)/shard_map/ppermute | solution.py:360
  123.1 8.2 %copy-start.5 = (bf16[520,256]{1,0:T(8,128)(2,1)}, bf16[520,256]{1,0:T(8,128)(2,1)S(1)}, u32[]{:S(2)}) copy-start(bf16[520,256]{1,0:T(8,128)(2,1)S(1)} %collective-permute-done.6.refs_2_) | copy-start | bytes 798724
  129.3 2.0 %copy-start.6 = (bf16[520,256]{1,0:T(8,128)(2,1)}, bf16[520,256]{1,0:T(8,128)(2,1)S(1)}, u32[]{:S(2)}) copy-start(bf16[520,256]{1,0:T(8,128)(2,1)S(1)} %collective-permute-done.7.refs_3_) | copy-start | bytes 798724
  134.6 24.1 %copy-start.1 = (bf16[32,64,256]{2,1,0:T(8,128)(2,1)}, bf16[32,64,256]{2,1,0:T(8,128)(2,1)S(1)}, u32[]{:S(2)}) copy-start(bf16[32,64,256]{2,1,0:T(8,128)(2,1)S(1)} %all-to-all-done.2.refs_3_) | copy-start | bytes 3145732
  134.6 27.7 %all-to-all-start.3 = ((f32[64,8,128]{2,1,0:T(8,128)}), f32[64,8,128]{2,1,0:T(8,128)S(1)}, u32[]{:S(2)}, u32[]{:S(2)}) async-start(f32[64,8,128]{2,1,0:T(8,128)} %get-tuple-element.69), calls=%async_computation.3 | async-start | bytes 524288 | tf_op jit(solution)/shard_map/all_to_all | solution.py:352
  146.5 12.2 %collective-permute-start.9 = (f32[256,256]{1,0:T(8,128)}, f32[256,256]{1,0:T(8,128)S(1)}, u32[]{:S(2)}, u32[]{:S(2)}) collective-permute-start(f32[256,256]{1,0:T(8,128)} %get-tuple-element.74), channel_id=1, source_target_pairs={{0,256},{256,0},{1,257},{257,1},{2,258},{258,2},{3,259},{259,3},{4... | collective-permute-start | bytes 786440 | tf_op jit(solution)/shard_map/ppermute | solution.py:356
  162.3 5.5 %collective-permute-start.10 = (f32[256,256]{1,0:T(8,128)S(1)}, f32[256,256]{1,0:T(8,128)S(1)}, u32[]{:S(2)}, u32[]{:S(2)}) collective-permute-start(f32[256,256]{1,0:T(8,128)S(1)} %bitcast.18), channel_id=1, source_target_pairs={{0,1},{1,0},{2,3},{3,2},{4,5},{5,4},{6,7},{7,6},{8,9},{9,8},{10,11... | collective-permute-start | bytes 786440 | tf_op jit(solution)/shard_map/ppermute | solution.py:356
  (8 other events, 6.3 us)

commit v7 on v6

--- a/solution.py
+++ b/solution.py
@@ -12,6 +12,8 @@
 PIECES = 4
 SMALL = 1 << 10
 TILE_COST = 30_000_000_000
+PANEL_COST = 20_000_000_000
+FINAL_COST = 20_000_000_000
 NT = (((1,), (1,)), ((), ()))
 NN = (((1,), (0,)), ((), ()))
 ALL = slice(None)
@@ -447,6 +449,7 @@
         [shape((2 * rows, width), F32)]
         + [(shape((tall, width), BF16), (slice(0, 2 * rows),))] * (nx - 1),
         (dest, here), (after(gn, both), back), [pltpu.VMEM((per * tile, width), BF16)],
+        PANEL_COST,
     )
     terms = [terms] if nx == 1 else terms
     scattered = after(scattered, (terms, packed))
@@ -469,6 +472,7 @@
     feat_grad = call(
         final_kernel, [square], (),
         (after(dpre, total), self_weight, hub_t, gathered, panel_here, panel_got),
+        flops=FINAL_COST,
     )
     theirs = swap(after(mine, feat_grad), "core")
     self_grad = jnp.where(core == 0, mine, theirs)

time: 170 us -> 173 us (1.018)
  waiting for transfers between devices: 33.1 us -> 36.9 us
    all_to_all x4, waiting for transfers between devices: 12.9 us -> 25.3 us  [exchange(): return lax.all_to_all(x, axis, split_axis=0, concat_axis=0, tiled=True)]
    ppermute x5, waiting for transfers between devices: 12 us -> 2.86 us  [swap(): return lax.ppermute(x, axis, [(0, 1), (1, 0)])]
  transfers between devices with their start and end apart: 15 -> 15, of which waited for: 8 -> 9; matrix products, arithmetic and copies ran while one was open for 3% -> 3% of each run, Pallas kernels for 16% -> 15%
where the time goes in v7:
time: 173 us; the launch traced here: 171 us
  starting transfers between devices  89.7 us (52%)
  waiting for transfers between devices  36.9 us (21%)
  Pallas kernels  33.2 us (19%)
  local copies, waits for them, and re-layouts  9.1 us (5%)
    all_to_all x4, starting transfers between devices, exchange(): return lax.all_to_all(x, axis, split_axis=0, concat_axis=0, tiled=True)  52.4 us
    pallas_call x10, Pallas kernels, call(): pl.pallas_call(body, out_shape=[shape(x.shape, x.dtype) for x, _ in outs]...  33.2 us
    all_to_all x4, waiting for transfers between devices, exchange(): return lax.all_to_all(x, axis, split_axis=0, concat_axis=0, tiled=True)  25.3 us
    ppermute x6, starting transfers between devices, along_x(): return lax.ppermute(x, 'x', [(i, (i + step) % nx) for i in range(nx)])  21.8 us
    ppermute x5, starting transfers between devices, swap(): return lax.ppermute(x, axis, [(0, 1), (1, 0)])  15.4 us
    ppermute x6, waiting for transfers between devices, along_x(): return lax.ppermute(x, 'x', [(i, (i + step) % nx) for i in range(nx)])  8.71 us
    unnamed x37, local copies, waits for them, and re-layouts  5.07 us
  transfers between devices with their start and end apart: 15, of which 9 were waited for; matrix products, arithmetic and copies ran while one was open for 3% of the time, Pallas kernels for 15%

profile of v7, /device:TPU:1, one launch (start us, length us, event | category | flops | bytes accessed | tf_op | source)
XLA Modules:
  0.0 171.3 jit_solution(7852346007541323214)
XLA Ops:
  0.6 4.0 %collective-permute-start = (bf16[256,256]{1,0:T(8,128)(2,1)}, bf16[256,256]{1,0:T(8,128)(2,1)S(1)}, u32[]{:S(2)}, u32[]{:S(2)}) collective-permute-start(bf16[256,256]{1,0:T(8,128)(2,1)} %refs_2_.3), channel_id=1, source_target_pairs={{0,256},{256,0},{1,257},{257,1},{2,258},{258,2},{3,259},{259,3},{4... | collective-permute-start | bytes 393224 | tf_op jit(solution)/shard_map/ppermute | solution.py:358
  4.7 3.6 %shard_map.129 = bf16[64,72,128]{2,1,0:T(8,128)(2,1)} custom-call(s32[64]{0:T(128)} %bitcast.22, bf16[64,32,128]{2,1,0:T(8,128)(2,1)} %bitcast.15, bf16[256,256]{1,0:T(8,128)(2,1)} %refs_2_.3), custom_call_target="tpu_custom_call" | custom-call | flops 1024 | bytes 1024 | tf_op jit(solution)/shard_map/pallas_call | solution.py:101
  8.3 16.2 %all-to-all-start = ((bf16[64,72,128]{2,1,0:T(8,128)(2,1)}), bf16[64,72,128]{2,1,0:T(8,128)(2,1)S(1)}, u32[]{:S(2)}, u32[]{:S(2)}) async-start(bf16[64,72,128]{2,1,0:T(8,128)(2,1)} %shard_map.129), calls=%async_computation | async-start | bytes 2359296 | tf_op jit(solution)/shard_map/all_to_all | solution.py:354
  25.4 3.1 %collective-permute-start.1 = (bf16[512,256]{1,0:T(8,128)(2,1)S(1)}, bf16[512,256]{1,0:T(8,128)(2,1)S(1)}, u32[]{:S(2)}, u32[]{:S(2)}) collective-permute-start(bf16[512,256]{1,0:T(8,128)(2,1)S(1)} %pad_maximum_fusion), channel_id=1, source_target_pairs={{0,64},{64,128},{128,192},{192,0},{1,65},{65,129},{129,193},{193,1... | collective-permute-start | bytes 786440 | tf_op jit(solution)/shard_map/ppermute | solution.py:362
  28.6 4.4 %collective-permute-start.2 = (bf16[512,256]{1,0:T(8,128)(2,1)S(1)}, bf16[512,256]{1,0:T(8,128)(2,1)S(1)}, u32[]{:S(2)}, u32[]{:S(2)}) collective-permute-start(bf16[512,256]{1,0:T(8,128)(2,1)S(1)} %pad_maximum_fusion), channel_id=1, source_target_pairs={{0,128},{64,192},{128,0},{192,64},{1,129},{65,193},{129,1},{193,65... | collective-permute-start | bytes 786440 | tf_op jit(solution)/shard_map/ppermute | solution.py:362
  32.9 3.1 %collective-permute-start.3 = (bf16[512,256]{1,0:T(8,128)(2,1)S(1)}, bf16[512,256]{1,0:T(8,128)(2,1)S(1)}, u32[]{:S(2)}, u32[]{:S(2)}) collective-permute-start(bf16[512,256]{1,0:T(8,128)(2,1)S(1)} %pad_maximum_fusion), channel_id=1, source_target_pairs={{0,192},{64,0},{128,64},{192,128},{1,193},{65,1},{129,65},{193,129... | collective-permute-start | bytes 786440 | tf_op jit(solution)/shard_map/ppermute | solution.py:362
  39.5 6.1 %shard_map.130 = (bf16[256,4096]{1,0:T(8,128)(2,1)}, bf16[8,256,512]{2,1,0:T(8,128)(2,1)}, bf16[256,2048]{1,0:T(8,128)(2,1)}, bf16[2048,256]{1,0:T(8,128)(2,1)},...) custom-call(s32[32]{0:T(128)} %reshape.40.refs_0_, ...), custom_call_target="tpu_custom_call" | custom-call | flops 1024 | bytes 1024 | tf_op jit(solution)/shard_map/pallas_call | solution.py:101
  47.1 4.1 %shard_map.131.refs_4_ = f32[256,256]{1,0:T(8,128)} custom-call(s32[32]{0:T(128)} %reshape.41.refs_1_.refs_0_, s32[2]{0:T(128)} %pad_add_fusion.refs_1_, bf16[256,256]{1,0:T(8,128)(2,1)} %refs_2_.3, bf16[256,256]{1,0:T(8,128)(2,1)} %copy-done.9, bf16[512,256]{1,0:T(8,128)(2,1)} %copy-done.13, bf16[512,256]{1,0:T(8,128)(2,1)} %copy-done.14, ...), custom_call_target="tpu_custom_call" | custom-call | flops 30000001024 | bytes 1024 | tf_op jit(solution)/shard_map/pallas_call | solution.py:101
  51.3 5.1 %all-to-all-done.refs_2_ = bf16[64,72,128]{2,1,0:T(8,128)(2,1)S(1)} async-done(((bf16[64,72,128]{2,1,0:T(8,128)(2,1)}), bf16[64,72,128]{2,1,0:T(8,128)(2,1)S(1)}, u32[]{:S(2)}, u32[]{:S(2)}) %all-to-all-start) | async-done | bytes 1179680 | tf_op jit(solution)/shard_map/all_to_all | solution.py:354
  57.3 4.9 %shard_map.132 = (bf16[256,256]{1,0:T(8,128)(2,1)}, bf16[256,256]{1,0:T(8,128)(2,1)}, bf16[256,256]{1,0:T(8,128)(2,1)}, f32[256,256]{1,0:T(8,128)}, f32[256,256]...) custom-call(s32[1]{0:T(128)} %bitcast.refs_2_.refs_0_, s32[1]{0:T(128)} %bitcast.1.refs_1_, ...), custom_call_target="tpu_custom_call" | custom-call | flops 1024 | bytes 1024 | tf_op jit(solution)/shard_map/pallas_call | solution.py:101
  68.4 21.4 %all-to-all-start.1 = ((f32[64,8,128]{2,1,0:T(8,128)}), f32[64,8,128]{2,1,0:T(8,128)S(1)}, u32[]{:S(2)}, u32[]{:S(2)}) async-start(f32[64,8,128]{2,1,0:T(8,128)} %shard_map.133), calls=%async_computation.1 | async-start | bytes 524288 | tf_op jit(solution)/shard_map/all_to_all | solution.py:354
  89.8 2.3 %collective-permute-start.5 = (bf16[32,32,256]{2,1,0:T(8,128)(2,1)}, bf16[32,32,256]{2,1,0:T(8,128)(2,1)S(1)}, u32[]{:S(2)}, u32[]{:S(2)}) collective-permute-start(bf16[32,32,256]{2,1,0:T(8,128)(2,1)} %get-tuple-element.60), channel_id=1, source_target_pairs={{0,1},{1,0},{2,3},{3,2},{4,5},{5,4},{6,7},{7,6},{8,9},{9,8},{10,11... | collective-permute-start | bytes 1572872 | tf_op jit(solution)/shard_map/ppermute | solution.py:358
  92.2 3.9 %shard_map.134 = (f32[512,256]{1,0:T(8,128)}, bf16[520,256]{1,0:T(8,128)(2,1)}, bf16[520,256]{1,0:T(8,128)(2,1)}, bf16[520,256]{1,0:T(8,128)(2,1)}) custom-call(s32[32]{0:T(128)} %reshape.40.refs_0_, s32[2]{0:T(128)} %pad_add_fusion.refs_1_, bf16[256,256]{1,0:T(8,128)(2,1)} %get-tuple-element.53.refs_2_, bf16[8,256,512]{2,1,0:T(8,128)(2,1)} %get-tuple-element.54.refs_3_), custom_call_target="tpu_custom_call" | custom-call | flops 20000000000 | bytes 1024 | tf_op jit(solution)/shard_map/pallas_call | solution.py:101
  98.9 5.6 %all-to-all-done.1.refs_0_ = f32[64,8,128]{2,1,0:T(8,128)S(1)} async-done(((f32[64,8,128]{2,1,0:T(8,128)}), f32[64,8,128]{2,1,0:T(8,128)S(1)}, u32[]{:S(2)}, u32[]{:S(2)}) %all-to-all-start.1) | async-done | bytes 262176 | tf_op jit(solution)/shard_map/all_to_all | solution.py:354
  104.5 6.1 %all-to-all-start.2 = ((bf16[32,64,256]{2,1,0:T(8,128)(2,1)}), bf16[32,64,256]{2,1,0:T(8,128)(2,1)S(1)}, u32[]{:S(2)}, u32[]{:S(2)}) async-start(bf16[32,64,256]{2,1,0:T(8,128)(2,1)} %shard_map.135), calls=%async_computation.2 | async-start | bytes 2097152 | tf_op jit(solution)/shard_map/all_to_all | solution.py:354
  112.3 2.8 %collective-permute-start.6 = (bf16[520,256]{1,0:T(8,128)(2,1)}, bf16[520,256]{1,0:T(8,128)(2,1)S(1)}, u32[]{:S(2)}, u32[]{:S(2)}) collective-permute-start(bf16[520,256]{1,0:T(8,128)(2,1)} %get-tuple-element.64), channel_id=1, source_target_pairs={{0,64},{64,128},{128,192},{192,0},{1,65},{65,129},{129,193},{193,1... | collective-permute-start | bytes 798728 | tf_op jit(solution)/shard_map/ppermute | solution.py:362
  115.1 5.7 %collective-permute-start.7 = (bf16[520,256]{1,0:T(8,128)(2,1)}, bf16[520,256]{1,0:T(8,128)(2,1)S(1)}, u32[]{:S(2)}, u32[]{:S(2)}) collective-permute-start(bf16[520,256]{1,0:T(8,128)(2,1)} %get-tuple-element.65), channel_id=1, source_target_pairs={{0,128},{64,192},{128,0},{192,64},{1,129},{65,193},{129,1},{193,65... | collective-permute-start | bytes 798728 | tf_op jit(solution)/shard_map/ppermute | solution.py:362
  120.8 2.8 %collective-permute-start.8 = (bf16[520,256]{1,0:T(8,128)(2,1)}, bf16[520,256]{1,0:T(8,128)(2,1)S(1)}, u32[]{:S(2)}, u32[]{:S(2)}) collective-permute-start(bf16[520,256]{1,0:T(8,128)(2,1)} %get-tuple-element.66), channel_id=1, source_target_pairs={{0,192},{64,0},{128,64},{192,128},{1,193},{65,1},{129,65},{193,129... | collective-permute-start | bytes 798728 | tf_op jit(solution)/shard_map/ppermute | solution.py:362
  124.5 6.6 %collective-permute-done.7.refs_3_ = bf16[520,256]{1,0:T(8,128)(2,1)S(1)} collective-permute-done((bf16[520,256]{1,0:T(8,128)(2,1)}, bf16[520,256]{1,0:T(8,128)(2,1)S(1)}, u32[]{:S(2)}, u32[]{:S(2)}) %collective-permute-start.7) | collective-permute-done | bytes 266272 | tf_op jit(solution)/shard_map/ppermute | solution.py:362
  135.3 5.0 %all-to-all-done.2.refs_3_ = bf16[32,64,256]{2,1,0:T(8,128)(2,1)S(1)} async-done(((bf16[32,64,256]{2,1,0:T(8,128)(2,1)}), bf16[32,64,256]{2,1,0:T(8,128)(2,1)S(1)}, u32[]{:S(2)}, u32[]{:S(2)}) %all-to-all-start.2) | async-done | bytes 1048608 | tf_op jit(solution)/shard_map/all_to_all | solution.py:354
  142.2 8.7 %all-to-all-start.3 = ((f32[64,8,128]{2,1,0:T(8,128)}), f32[64,8,128]{2,1,0:T(8,128)S(1)}, u32[]{:S(2)}, u32[]{:S(2)}) async-start(f32[64,8,128]{2,1,0:T(8,128)} %get-tuple-element.69), calls=%async_computation.3 | async-start | bytes 524288 | tf_op jit(solution)/shard_map/all_to_all | solution.py:354
  151.7 2.9 %shard_map.138 = bf16[256,256]{1,0:T(8,128)(2,1)} custom-call(bf16[256,256]{1,0:T(8,128)(2,1)} %get-tuple-element.70.refs_0_, bf16[256,256]{1,0:T(8,128)(2,1)} %refs_1_.1, bf16[256,2048]{1,0:T(8,128)(2,1)} %get-tuple-element.71.refs_2_, bf16[32,64,256]{2,1,0:T(8,128)(2,1)} %copy-done.2, f32[256,256]{1,0:T(8,128)} %get-tuple-element.72.refs_4_, ...), custom_call_target="tpu_custom_call" | custom-call | flops 20000000000 | bytes 1024 | tf_op jit(solution)/shard_map/pallas_call | solution.py:101
  154.6 9.6 %all-to-all-done.3 = f32[64,8,128]{2,1,0:T(8,128)S(1)} async-done(((f32[64,8,128]{2,1,0:T(8,128)}), f32[64,8,128]{2,1,0:T(8,128)S(1)}, u32[]{:S(2)}, u32[]{:S(2)}) %all-to-all-start.3) | async-done | bytes 262176 | tf_op jit(solution)/shard_map/all_to_all | solution.py:354
  164.2 5.2 %collective-permute-start.10 = (f32[256,256]{1,0:T(8,128)S(1)}, f32[256,256]{1,0:T(8,128)S(1)}, u32[]{:S(2)}, u32[]{:S(2)}) collective-permute-start(f32[256,256]{1,0:T(8,128)S(1)} %bitcast.18), channel_id=1, source_target_pairs={{0,1},{1,0},{2,3},{3,2},{4,5},{5,4},{6,7},{7,6},{8,9},{9,8},{10,11... | collective-permute-start | bytes 786440 | tf_op jit(solution)/shard_map/ppermute | solution.py:358
  (63 shorter events, 27.1 us)
Async XLA Ops:
  0.6 24.7 %collective-permute-start = (bf16[256,256]{1,0:T(8,128)(2,1)}, bf16[256,256]{1,0:T(8,128)(2,1)S(1)}, u32[]{:S(2)}, u32[]{:S(2)}) collective-permute-start(bf16[256,256]{1,0:T(8,128)(2,1)} %refs_2_.3), channel_id=1, source_target_pairs={{0,256},{256,0},{1,257},{257,1},{2,258},{258,2},{3,259},{259,3},{4... | collective-permute-start | bytes 393224 | tf_op jit(solution)/shard_map/ppermute | solution.py:358
  4.7 19.8 %copy-start.10 = (s32[1,64,32]{1,2,0:T(8,128)S(1)}, s32[1,64,32]{1,2,0:T(8,128)}, u32[]{:S(2)}) copy-start(s32[1,64,32]{1,2,0:T(8,128)} %param.19) | copy-start | bytes 24580
  4.7 20.7 %copy-start.1 = (bf16[256,256]{1,0:T(8,128)(2,1)S(1)}, bf16[256,256]{1,0:T(8,128)(2,1)}, u32[]{:S(2)}) copy-start(bf16[256,256]{1,0:T(8,128)(2,1)} %refs_2_.3) | copy-start | bytes 393220
  8.3 29.8 %copy-start.11 = (s32[1,8,4]{1,2,0:T(4,128)S(1)}, s32[1,8,4]{1,2,0:T(4,128)}, u32[]{:S(2)}) copy-start(s32[1,8,4]{1,2,0:T(4,128)} %param.15) | copy-start | bytes 388
  8.3 30.5 %copy-start.12 = (s32[1,8,4]{1,2,0:T(4,128)S(1)}, s32[1,8,4]{1,2,0:T(4,128)}, u32[]{:S(2)}) copy-start(s32[1,8,4]{1,2,0:T(4,128)} %param.16) | copy-start | bytes 388
  8.3 48.0 %all-to-all-start = ((bf16[64,72,128]{2,1,0:T(8,128)(2,1)}), bf16[64,72,128]{2,1,0:T(8,128)(2,1)S(1)}, u32[]{:S(2)}, u32[]{:S(2)}) async-start(bf16[64,72,128]{2,1,0:T(8,128)(2,1)} %shard_map.129), calls=%async_computation | async-start | bytes 2359296 | tf_op jit(solution)/shard_map/all_to_all | solution.py:354
  25.4 20.1 %copy-start.9 = (bf16[256,256]{1,0:T(8,128)(2,1)}, bf16[256,256]{1,0:T(8,128)(2,1)S(1)}, u32[]{:S(2)}) copy-start(bf16[256,256]{1,0:T(8,128)(2,1)S(1)} %collective-permute-done.refs_3_) | copy-start | bytes 393220
  25.4 20.8 %collective-permute-start.1 = (bf16[512,256]{1,0:T(8,128)(2,1)S(1)}, bf16[512,256]{1,0:T(8,128)(2,1)S(1)}, u32[]{:S(2)}, u32[]{:S(2)}) collective-permute-start(bf16[512,256]{1,0:T(8,128)(2,1)S(1)} %pad_maximum_fusion), channel_id=1, source_target_pairs={{0,64},{64,128},{128,192},{192,0},{1,65},{65,129},{129,193},{193,1... | collective-permute-start | bytes 786440 | tf_op jit(solution)/shard_map/ppermute | solution.py:362
  28.6 17.7 %collective-permute-start.2 = (bf16[512,256]{1,0:T(8,128)(2,1)S(1)}, bf16[512,256]{1,0:T(8,128)(2,1)S(1)}, u32[]{:S(2)}, u32[]{:S(2)}) collective-permute-start(bf16[512,256]{1,0:T(8,128)(2,1)S(1)} %pad_maximum_fusion), channel_id=1, source_target_pairs={{0,128},{64,192},{128,0},{192,64},{1,129},{65,193},{129,1},{193,65... | collective-permute-start | bytes 786440 | tf_op jit(solution)/shard_map/ppermute | solution.py:362
  32.9 13.3 %collective-permute-start.3 = (bf16[512,256]{1,0:T(8,128)(2,1)S(1)}, bf16[512,256]{1,0:T(8,128)(2,1)S(1)}, u32[]{:S(2)}, u32[]{:S(2)}) collective-permute-start(bf16[512,256]{1,0:T(8,128)(2,1)S(1)} %pad_maximum_fusion), channel_id=1, source_target_pairs={{0,192},{64,0},{128,64},{192,128},{1,193},{65,1},{129,65},{193,129... | collective-permute-start | bytes 786440 | tf_op jit(solution)/shard_map/ppermute | solution.py:362
  62.3 3.6 %collective-permute-start.4 = (f32[256,256]{1,0:T(8,128)}, f32[256,256]{1,0:T(8,128)S(1)}, u32[]{:S(2)}, u32[]{:S(2)}) collective-permute-start(f32[256,256]{1,0:T(8,128)} %get-tuple-element.51), channel_id=1, source_target_pairs={{0,1},{1,0},{2,3},{3,2},{4,5},{5,4},{6,7},{7,6},{8,9},{9,8},{10,11... | collective-permute-start | bytes 786440 | tf_op jit(solution)/shard_map/ppermute | solution.py:358
  68.4 36.1 %all-to-all-start.1 = ((f32[64,8,128]{2,1,0:T(8,128)}), f32[64,8,128]{2,1,0:T(8,128)S(1)}, u32[]{:S(2)}, u32[]{:S(2)}) async-start(f32[64,8,128]{2,1,0:T(8,128)} %shard_map.133), calls=%async_computation.1 | async-start | bytes 524288 | tf_op jit(solution)/shard_map/all_to_all | solution.py:354
  89.8 6.3 %collective-permute-start.5 = (bf16[32,32,256]{2,1,0:T(8,128)(2,1)}, bf16[32,32,256]{2,1,0:T(8,128)(2,1)S(1)}, u32[]{:S(2)}, u32[]{:S(2)}) collective-permute-start(bf16[32,32,256]{2,1,0:T(8,128)(2,1)} %get-tuple-element.60), channel_id=1, source_target_pairs={{0,1},{1,0},{2,3},{3,2},{4,5},{5,4},{6,7},{7,6},{8,9},{9,8},{10,11... | collective-permute-start | bytes 1572872 | tf_op jit(solution)/shard_map/ppermute | solution.py:358
  104.5 6.1 %copy-start.3 = (f32[64,8,128]{2,1,0:T(8,128)}, f32[64,8,128]{2,1,0:T(8,128)S(1)}, u32[]{:S(2)}) copy-start(f32[64,8,128]{2,1,0:T(8,128)S(1)} %all-to-all-done.1.refs_0_) | copy-start | bytes 786436
  104.5 35.8 %all-to-all-start.2 = ((bf16[32,64,256]{2,1,0:T(8,128)(2,1)}), bf16[32,64,256]{2,1,0:T(8,128)(2,1)S(1)}, u32[]{:S(2)}, u32[]{:S(2)}) async-start(bf16[32,64,256]{2,1,0:T(8,128)(2,1)} %shard_map.135), calls=%async_computation.2 | async-start | bytes 2097152 | tf_op jit(solution)/shard_map/all_to_all | solution.py:354
  112.3 12.2 %collective-permute-start.6 = (bf16[520,256]{1,0:T(8,128)(2,1)}, bf16[520,256]{1,0:T(8,128)(2,1)S(1)}, u32[]{:S(2)}, u32[]{:S(2)}) collective-permute-start(bf16[520,256]{1,0:T(8,128)(2,1)} %get-tuple-element.64), channel_id=1, source_target_pairs={{0,64},{64,128},{128,192},{192,0},{1,65},{65,129},{129,193},{193,1... | collective-permute-start | bytes 798728 | tf_op jit(solution)/shard_map/ppermute | solution.py:362
  115.1 16.0 %collective-permute-start.7 = (bf16[520,256]{1,0:T(8,128)(2,1)}, bf16[520,256]{1,0:T(8,128)(2,1)S(1)}, u32[]{:S(2)}, u32[]{:S(2)}) collective-permute-start(bf16[520,256]{1,0:T(8,128)(2,1)} %get-tuple-element.65), channel_id=1, source_target_pairs={{0,128},{64,192},{128,0},{192,64},{1,129},{65,193},{129,1},{193,65... | collective-permute-start | bytes 798728 | tf_op jit(solution)/shard_map/ppermute | solution.py:362
  120.8 11.5 %collective-permute-start.8 = (bf16[520,256]{1,0:T(8,128)(2,1)}, bf16[520,256]{1,0:T(8,128)(2,1)S(1)}, u32[]{:S(2)}, u32[]{:S(2)}) collective-permute-start(bf16[520,256]{1,0:T(8,128)(2,1)} %get-tuple-element.66), channel_id=1, source_target_pairs={{0,192},{64,0},{128,64},{192,128},{1,193},{65,1},{129,65},{193,129... | collective-permute-start | bytes 798728 | tf_op jit(solution)/shard_map/ppermute | solution.py:362
  124.5 7.9 %copy-start.5 = (bf16[520,256]{1,0:T(8,128)(2,1)}, bf16[520,256]{1,0:T(8,128)(2,1)S(1)}, u32[]{:S(2)}) copy-start(bf16[520,256]{1,0:T(8,128)(2,1)S(1)} %collective-permute-done.6.refs_2_) | copy-start | bytes 798724
  131.0 1.3 copy-start.6
  140.3 10.7 %copy-start.2 = (bf16[32,64,256]{2,1,0:T(8,128)(2,1)}, bf16[32,64,256]{2,1,0:T(8,128)(2,1)S(1)}, u32[]{:S(2)}) copy-start(bf16[32,64,256]{2,1,0:T(8,128)(2,1)S(1)} %all-to-all-done.2.refs_3_) | copy-start | bytes 3145732
  140.3 10.7 %collective-permute-start.9 = (f32[256,256]{1,0:T(8,128)}, f32[256,256]{1,0:T(8,128)S(1)}, u32[]{:S(2)}, u32[]{:S(2)}) collective-permute-start(f32[256,256]{1,0:T(8,128)} %get-tuple-element.74), channel_id=1, source_target_pairs={{0,256},{256,0},{1,257},{257,1},{2,258},{258,2},{3,259},{259,3},{4... | collective-permute-start | bytes 786440 | tf_op jit(solution)/shard_map/ppermute | solution.py:358
  142.2 22.0 %all-to-all-start.3 = ((f32[64,8,128]{2,1,0:T(8,128)}), f32[64,8,128]{2,1,0:T(8,128)S(1)}, u32[]{:S(2)}, u32[]{:S(2)}) async-start(f32[64,8,128]{2,1,0:T(8,128)} %get-tuple-element.69), calls=%async_computation.3 | async-start | bytes 524288 | tf_op jit(solution)/shard_map/all_to_all | solution.py:354
  164.2 6.3 %collective-permute-start.10 = (f32[256,256]{1,0:T(8,128)S(1)}, f32[256,256]{1,0:T(8,128)S(1)}, u32[]{:S(2)}, u32[]{:S(2)}) collective-permute-start(f32[256,256]{1,0:T(8,128)S(1)} %bitcast.18), channel_id=1, source_target_pairs={{0,1},{1,0},{2,3},{3,2},{4,5},{5,4},{6,7},{7,6},{8,9},{9,8},{10,11... | collective-permute-start | bytes 786440 | tf_op jit(solution)/shard_map/ppermute | solution.py:358
  (8 other events, 6.3 us)

commit v8 on v7

--- a/solution.py
+++ b/solution.py
@@ -9,9 +9,10 @@
 BF16 = jnp.bfloat16
 LANES = 128
 EXTRA = 8
-PIECES = 4
+PIECES = 2
 SMALL = 1 << 10
-TILE_COST = 30_000_000_000
+TILE_COST = 1 << 10
+PREPARE_COST = 20_000_000_000
 PANEL_COST = 20_000_000_000
 FINAL_COST = 20_000_000_000
 NT = (((1,), (1,)), ((), ()))
@@ -117,9 +118,8 @@
     return [jnp.where(source == b, w, jnp.zeros_like(w)) for b in range(nblk)]
 
 
-def hub_send_kernel(src, weights, feat, message, wm_ref):
+def hub_send_kernel(src, core, weights, feat, packed, send, wm_ref):
     w_ref = weights()
-    msg_ref = message.ref
     owners, hub, tile = w_ref.shape
     per = LANES // hub
     flat = w_ref[...].reshape(owners * hub, tile)
@@ -131,21 +131,23 @@
     rows, width = x_ref.shape
     nblk = rows // tile
     top = (width // LANES) * hub
-    n = owners // PIECES
-    for p in range(PIECES):
-        for o in range(p * n, (p + 1) * n):
-            for b, part in enumerate(by_source(w_ref[o], src[o], nblk)):
-                wm_ref[o * hub : (o + 1) * hub, b * tile : (b + 1) * tile] = part
-        at = slice(p * n * hub, (p + 1) * n * hub)
-        part = dot(wm_ref[at, :], x_ref[...]).astype(BF16)
-        for c in range(width // LANES):
-            msg_ref[p * n : (p + 1) * n, c * hub : (c + 1) * hub, :] = part[
-                :, c * LANES : (c + 1) * LANES
-            ].reshape(n, hub, LANES)
-        for o in range(p * n, (p + 1) * n):
-            g = o // per
-            msg_ref[o, top : top + EXTRA, :] = pair[:, g * LANES : (g + 1) * LANES]
-        message.send(p, PIECES)
+    n = owners // 2 // PIECES
+    for message, other in ((send, 1 - core[0]), (packed, core[0])):
+        msg_ref = message.ref
+        for p in range(PIECES):
+            for i in range(n):
+                o = (p * n + i) * 2 + other
+                for b, part in enumerate(by_source(w_ref[o], src[o], nblk)):
+                    wm_ref[i * hub : (i + 1) * hub, b * tile : (b + 1) * tile] = part
+            part = dot(wm_ref[...], x_ref[...]).astype(BF16)
+            for c in range(width // LANES):
+                msg_ref[p * n : (p + 1) * n, c * hub : (c + 1) * hub, :] = part[
+                    :, c * LANES : (c + 1) * LANES
+                ].reshape(n, hub, LANES)
+            for i in range(p * n, (p + 1) * n):
+                g = 2 * i // per
+                msg_ref[i, top : top + EXTRA, :] = pair[:, g * LANES : (g + 1) * LANES]
+            message.send(p, PIECES)
 
 
 def prepare_kernel(
@@ -220,25 +222,29 @@
     layer_out, dpre_out, gn_out, wkeep, wsend, packed, hsend, rhs_ref,
 ):
     got_ref = got()
-    senders = got_ref.shape[0]
+    far, both, _ = got_ref.shape
     rows, width = layer_out.ref.shape
     slots = onehot.ref.shape[1]
-    hub = slots // senders
+    half = slots // 2
+    hub = half // far
     parts = width // LANES
-    for c in range(parts):
-        rhs_ref[:, c * LANES : (c + 1) * LANES] = got_ref[:, c * hub : (c + 1) * hub, :].reshape(
-            slots, LANES
-        )
     top = parts * hub
     slot = lax.broadcasted_iota(jnp.int32, (1, hub, LANES), 1)
     lane = lax.broadcasted_iota(jnp.int32, (1, hub, LANES), 2)
     mine = lane == lax.rem(me[0], LANES // hub) * hub + slot
-    for h in range(2):
-        line = got_ref[:, top + h * (EXTRA // 2) : top + h * (EXTRA // 2) + 1, :].astype(F32)
-        spread = jnp.where(mine, jnp.broadcast_to(line, (senders, hub, LANES)), 0.0)
-        rhs_ref[:, (parts + h) * LANES : (parts + h + 1) * LANES] = spread.astype(BF16).reshape(
-            slots, LANES
-        )
+    for r in range(2):
+        at, base = slice(r * half, (r + 1) * half), r * (both // 2)
+        for c in range(parts):
+            rhs_ref[at, c * LANES : (c + 1) * LANES] = got_ref[
+                :, base + c * hub : base + (c + 1) * hub, :
+            ].reshape(half, LANES)
+        for h in range(2):
+            first = base + top + h * (EXTRA // 2)
+            line = got_ref[:, first : first + 1, :].astype(F32)
+            spread = jnp.where(mine, jnp.broadcast_to(line, (far, hub, LANES)), 0.0)
+            rhs_ref[at, (parts + h) * LANES : (parts + h + 1) * LANES] = spread.astype(
+                BF16
+            ).reshape(half, LANES)
     hubs = dot(onehot()[...], rhs_ref[...])
     summed = local()[...] + hubs[:, :width]
     hub_deg = jnp.sum(
@@ -385,19 +391,28 @@
     square = shape((rows, width), BF16)
     square32 = shape((rows, width), F32)
     beside = swap(node_feat, "y")
+    msg, send = call(
+        hub_send_kernel,
+        [
+            (shape((far, 2 * high, LANES), BF16), (ALL, slice(0, high))),
+            shape((far, high, LANES), BF16),
+        ],
+        (hub_source[0], core1), (hub_weights[0], node_feat),
+        [pltpu.VMEM((slots // 2 // PIECES, rows), BF16)], pieces=PIECES,
+    )
     msg = call(
-        hub_send_kernel, [shape((owners, high, LANES), BF16)], (hub_source[0],),
-        (hub_weights[0], node_feat), [pltpu.VMEM((slots, rows), BF16)], pieces=PIECES,
-    )
-    got = exchange(msg, ("far", "core"))
+        assemble_kernel, [], (), (swap(send, "core"),),
+        into=[(msg, (ALL, slice(high, 2 * high)))],
+    )
+    got = exchange(msg, "far")
     pair = after(jnp.concatenate([node_feat, beside], axis=0), msg)
     pairs = [along_x(pair, k, nx) for k in range(1, nx)]
     dest = tile_dest.reshape(n)
     source = tile_source.reshape(n)
-    slot_row = hub_slots.reshape(1, slots)
     order = hub_slots.reshape(far, 2, hub)
     order = jnp.where(core == 0, order, order[:, ::-1])
-    slot_col = jnp.swapaxes(order, 0, 1).reshape(slots, 1)
+    order = jnp.swapaxes(order, 0, 1)
+    slot_row, slot_col = order.reshape(1, slots), order.reshape(slots, 1)
     place, back, onehot, onehot_t, hub_t, feat_t, feat_self, degree = call(
         prepare_kernel,
         [
@@ -415,7 +430,7 @@
             tile_weights.reshape(n, tile, tile), after(node_feat, msg), slot_row, slot_col,
             hub_weights[0], self_weight,
         ),
-        [pltpu.VMEM((slots, rows), BF16)],
+        [pltpu.VMEM((slots, rows), BF16)], PREPARE_COST,
     )
     local = call(
         tiles_kernel, [square32], (source, here), (node_feat, beside, *pairs, place),

time: 173 us -> 168 us (0.971)
  starting transfers between devices: 89.7 us -> 84 us
  waiting for transfers between devices: 36.9 us -> 34.8 us
  Pallas kernels: 33.2 us -> 35.1 us
    all_to_all x4, starting transfers between devices: 52.4 us -> 38.1 us  [exchange(): return lax.all_to_all(x, axis, split_axis=0, concat_axis=0, tiled=True)]
    ppermute x5 -> x6, starting transfers between devices: 15.4 us -> 24.8 us  [swap(): return lax.ppermute(x, axis, [(0, 1), (1, 0)])]
    all_to_all x4, waiting for transfers between devices: 25.3 us -> 22.5 us  [exchange(): return lax.all_to_all(x, axis, split_axis=0, concat_axis=0, tiled=True)]
    pallas_call x10 -> x11, Pallas kernels: 33.2 us -> 35.1 us  [call(): pl.pallas_call(body, out_shape=[shape(x.shape, x.dtype) for x, _ in outs]...]
    unnamed x37 -> x39, local copies, waits for them, and re-layouts: 5.07 us -> 6.41 us
  transfers between devices with their start and end apart: 15 -> 16, of which waited for: 9 -> 11; matrix products, arithmetic and copies ran while one was open for 3% -> 3% of each run, Pallas kernels for 15% -> 15%
where the time goes in v8:
time: 168 us; the launch traced here: 167 us
  starting transfers between devices  84 us (50%)
  Pallas kernels  35.1 us (21%)
  waiting for transfers between devices  34.8 us (21%)
  local copies, waits for them, and re-layouts  10.4 us (6%)
    all_to_all x4, starting transfers between devices, exchange(): return lax.all_to_all(x, axis, split_axis=0, concat_axis=0, tiled=True)  38.1 us
    pallas_call x11, Pallas kernels, call(): pl.pallas_call(body, out_shape=[shape(x.shape, x.dtype) for x, _ in outs]...  35.1 us
    ppermute x6, starting transfers between devices, swap(): return lax.ppermute(x, axis, [(0, 1), (1, 0)])  24.8 us
    all_to_all x4, waiting for transfers between devices, exchange(): return lax.all_to_all(x, axis, split_axis=0, concat_axis=0, tiled=True)  22.5 us
    ppermute x6, starting transfers between devices, along_x(): return lax.ppermute(x, 'x', [(i, (i + step) % nx) for i in range(nx)])  21 us
    ppermute x6, waiting for transfers between devices, along_x(): return lax.ppermute(x, 'x', [(i, (i + step) % nx) for i in range(nx)])  9.86 us
    unnamed x39, local copies, waits for them, and re-layouts  6.41 us
  transfers between devices with their start and end apart: 16, of which 11 were waited for; matrix products, arithmetic and copies ran while one was open for 3% of the time, Pallas kernels for 15%

profile of v8, /device:TPU:1, one launch (start us, length us, event | category | flops | bytes accessed | tf_op | source)
XLA Modules:
  0.0 166.8 jit_solution(8993477673500928507)
XLA Ops:
  0.6 3.5 %shard_map.129 = (bf16[32,144,128]{2,1,0:T(8,128)(2,1)}, bf16[32,72,128]{2,1,0:T(8,128)(2,1)}) custom-call(s32[64]{0:T(128)} %bitcast.21, s32[1]{0:T(128)} %bitcast.refs_1_.refs_2_.refs_0_, bf16[64,32,128]{2,1,0:T(8,128)(2,1)} %bitcast.17, bf16[256,256]{1,0:T(8,128)(2,1)} %refs_2_.1), custom_call_target="tpu_custom_call" | custom-call | flops 1024 | bytes 1024 | tf_op jit(solution)/shard_map/pallas_call | solution.py:102
  4.2 8.8 %collective-permute-start = (bf16[32,72,128]{2,1,0:T(8,128)(2,1)}, bf16[32,72,128]{2,1,0:T(8,128)(2,1)S(1)}, u32[]{:S(2)}, u32[]{:S(2)}) collective-permute-start(bf16[32,72,128]{2,1,0:T(8,128)(2,1)} %get-tuple-element.42), channel_id=1, source_target_pairs={{0,1},{1,0},{2,3},{3,2},{4,5},{5,4},{6,7},{7,6},{8,9},{9,8},{10,11... | collective-permute-start | bytes 1769480 | tf_op jit(solution)/shard_map/ppermute | solution.py:364
  18.6 10.7 %all-to-all-start = ((bf16[32,144,128]{2,1,0:T(8,128)(2,1)}), bf16[32,144,128]{2,1,0:T(8,128)(2,1)S(1)}, u32[]{:S(2)}, u32[]{:S(2)}) async-start(bf16[32,144,128]{2,1,0:T(8,128)(2,1)} %shard_map.130), calls=%async_computation | async-start | bytes 2359296 | tf_op jit(solution)/shard_map/all_to_all | solution.py:360
  34.1 3.1 %collective-permute-start.2 = (bf16[512,256]{1,0:T(8,128)(2,1)S(1)}, bf16[512,256]{1,0:T(8,128)(2,1)S(1)}, u32[]{:S(2)}, u32[]{:S(2)}) collective-permute-start(bf16[512,256]{1,0:T(8,128)(2,1)S(1)} %pad_maximum_fusion), channel_id=1, source_target_pairs={{0,64},{64,128},{128,192},{192,0},{1,65},{65,129},{129,193},{193,1... | collective-permute-start | bytes 786440 | tf_op jit(solution)/shard_map/ppermute | solution.py:368
  37.3 4.4 %collective-permute-start.3 = (bf16[512,256]{1,0:T(8,128)(2,1)S(1)}, bf16[512,256]{1,0:T(8,128)(2,1)S(1)}, u32[]{:S(2)}, u32[]{:S(2)}) collective-permute-start(bf16[512,256]{1,0:T(8,128)(2,1)S(1)} %pad_maximum_fusion), channel_id=1, source_target_pairs={{0,128},{64,192},{128,0},{192,64},{1,129},{65,193},{129,1},{193,65... | collective-permute-start | bytes 786440 | tf_op jit(solution)/shard_map/ppermute | solution.py:368
  41.6 3.1 %collective-permute-start.4 = (bf16[512,256]{1,0:T(8,128)(2,1)S(1)}, bf16[512,256]{1,0:T(8,128)(2,1)S(1)}, u32[]{:S(2)}, u32[]{:S(2)}) collective-permute-start(bf16[512,256]{1,0:T(8,128)(2,1)S(1)} %pad_maximum_fusion), channel_id=1, source_target_pairs={{0,192},{64,0},{128,64},{192,128},{1,193},{65,1},{129,65},{193,129... | collective-permute-start | bytes 786440 | tf_op jit(solution)/shard_map/ppermute | solution.py:368
  44.7 6.1 %shard_map.131 = (bf16[256,4096]{1,0:T(8,128)(2,1)}, bf16[8,256,512]{2,1,0:T(8,128)(2,1)}, bf16[256,2048]{1,0:T(8,128)(2,1)}, bf16[2048,256]{1,0:T(8,128)(2,1)},...) custom-call(s32[32]{0:T(128)} %reshape.40.refs_0_, ...), custom_call_target="tpu_custom_call" | custom-call | flops 20000000000 | bytes 1024 | tf_op jit(solution)/shard_map/pallas_call | solution.py:102
  53.0 4.1 %shard_map.132.refs_4_ = f32[256,256]{1,0:T(8,128)} custom-call(s32[32]{0:T(128)} %reshape.41.refs_1_.refs_0_, s32[2]{0:T(128)} %pad_add_fusion.refs_1_, bf16[256,256]{1,0:T(8,128)(2,1)} %refs_2_.1, bf16[256,256]{1,0:T(8,128)(2,1)} %copy-done.6, bf16[512,256]{1,0:T(8,128)(2,1)} %copy-done.10, bf16[512,256]{1,0:T(8,128)(2,1)} %copy-done.11, ...), custom_call_target="tpu_custom_call" | custom-call | flops 1024 | bytes 1024 | tf_op jit(solution)/shard_map/pallas_call | solution.py:102
  60.0 4.9 %shard_map.133 = (bf16[256,256]{1,0:T(8,128)(2,1)}, bf16[256,256]{1,0:T(8,128)(2,1)}, bf16[256,256]{1,0:T(8,128)(2,1)}, f32[256,256]{1,0:T(8,128)}, f32[256,256]...) custom-call(s32[1]{0:T(128)} %bitcast.refs_1_.refs_2_.refs_0_, s32[1]{0:T(128)} %bitcast.1.refs_1_, ...), custom_call_target="tpu_custom_call" | custom-call | flops 1024 | bytes 1024 | tf_op jit(solution)/shard_map/pallas_call | solution.py:102
  64.9 4.5 %collective-permute-start.5 = (f32[256,256]{1,0:T(8,128)}, f32[256,256]{1,0:T(8,128)S(1)}, u32[]{:S(2)}, u32[]{:S(2)}) collective-permute-start(f32[256,256]{1,0:T(8,128)} %get-tuple-element.55), channel_id=1, source_target_pairs={{0,1},{1,0},{2,3},{3,2},{4,5},{5,4},{6,7},{7,6},{8,9},{9,8},{10,11... | collective-permute-start | bytes 786440 | tf_op jit(solution)/shard_map/ppermute | solution.py:364
  73.2 11.9 %all-to-all-start.1 = ((f32[64,8,128]{2,1,0:T(8,128)}), f32[64,8,128]{2,1,0:T(8,128)S(1)}, u32[]{:S(2)}, u32[]{:S(2)}) async-start(f32[64,8,128]{2,1,0:T(8,128)} %shard_map.134), calls=%async_computation.1 | async-start | bytes 524288 | tf_op jit(solution)/shard_map/all_to_all | solution.py:360
  85.1 2.6 %collective-permute-start.6 = (bf16[32,32,256]{2,1,0:T(8,128)(2,1)S(1)}, bf16[32,32,256]{2,1,0:T(8,128)(2,1)S(1)}, u32[]{:S(2)}, u32[]{:S(2)}) collective-permute-start(bf16[32,32,256]{2,1,0:T(8,128)(2,1)S(1)} %copy-done.16), channel_id=1, source_target_pairs={{0,1},{1,0},{2,3},{3,2},{4,5},{5,4},{6,7},{7,6},{8,9},{9,8},{10,11... | collective-permute-start | bytes 1572872 | tf_op jit(solution)/shard_map/ppermute | solution.py:364
  87.7 3.9 %shard_map.135 = (f32[512,256]{1,0:T(8,128)}, bf16[520,256]{1,0:T(8,128)(2,1)}, bf16[520,256]{1,0:T(8,128)(2,1)}, bf16[520,256]{1,0:T(8,128)(2,1)}) custom-call(s32[32]{0:T(128)} %reshape.40.refs_0_, s32[2]{0:T(128)} %pad_add_fusion.refs_1_, bf16[256,256]{1,0:T(8,128)(2,1)} %get-tuple-element.57.refs_2_, bf16[8,256,512]{2,1,0:T(8,128)(2,1)} %get-tuple-element.58.refs_3_), custom_call_target="tpu_custom_call" | custom-call | flops 20000000000 | bytes 1024 | tf_op jit(solution)/shard_map/pallas_call | solution.py:102
  94.4 4.9 %all-to-all-done.1.refs_0_ = f32[64,8,128]{2,1,0:T(8,128)S(1)} async-done(((f32[64,8,128]{2,1,0:T(8,128)}), f32[64,8,128]{2,1,0:T(8,128)S(1)}, u32[]{:S(2)}, u32[]{:S(2)}) %all-to-all-start.1) | async-done | bytes 262176 | tf_op jit(solution)/shard_map/all_to_all | solution.py:360
  99.3 6.8 %all-to-all-start.2 = ((bf16[32,64,256]{2,1,0:T(8,128)(2,1)}), bf16[32,64,256]{2,1,0:T(8,128)(2,1)S(1)}, u32[]{:S(2)}, u32[]{:S(2)}) async-start(bf16[32,64,256]{2,1,0:T(8,128)(2,1)} %shard_map.136), calls=%async_computation.2 | async-start | bytes 2097152 | tf_op jit(solution)/shard_map/all_to_all | solution.py:360
  107.8 3.0 %collective-permute-start.7 = (bf16[520,256]{1,0:T(8,128)(2,1)}, bf16[520,256]{1,0:T(8,128)(2,1)S(1)}, u32[]{:S(2)}, u32[]{:S(2)}) collective-permute-start(bf16[520,256]{1,0:T(8,128)(2,1)} %get-tuple-element.68), channel_id=1, source_target_pairs={{0,64},{64,128},{128,192},{192,0},{1,65},{65,129},{129,193},{193,1... | collective-permute-start | bytes 798728 | tf_op jit(solution)/shard_map/ppermute | solution.py:368
  110.8 4.4 %collective-permute-start.8 = (bf16[520,256]{1,0:T(8,128)(2,1)}, bf16[520,256]{1,0:T(8,128)(2,1)S(1)}, u32[]{:S(2)}, u32[]{:S(2)}) collective-permute-start(bf16[520,256]{1,0:T(8,128)(2,1)} %get-tuple-element.69), channel_id=1, source_target_pairs={{0,128},{64,192},{128,0},{192,64},{1,129},{65,193},{129,1},{193,65... | collective-permute-start | bytes 798728 | tf_op jit(solution)/shard_map/ppermute | solution.py:368
  115.1 3.2 %collective-permute-start.9 = (bf16[520,256]{1,0:T(8,128)(2,1)}, bf16[520,256]{1,0:T(8,128)(2,1)S(1)}, u32[]{:S(2)}, u32[]{:S(2)}) collective-permute-start(bf16[520,256]{1,0:T(8,128)(2,1)} %get-tuple-element.70), channel_id=1, source_target_pairs={{0,192},{64,0},{128,64},{192,128},{1,193},{65,1},{129,65},{193,129... | collective-permute-start | bytes 798728 | tf_op jit(solution)/shard_map/ppermute | solution.py:368
  118.8 6.5 %collective-permute-done.8.refs_3_ = bf16[520,256]{1,0:T(8,128)(2,1)S(1)} collective-permute-done((bf16[520,256]{1,0:T(8,128)(2,1)}, bf16[520,256]{1,0:T(8,128)(2,1)S(1)}, u32[]{:S(2)}, u32[]{:S(2)}) %collective-permute-start.8) | collective-permute-done | bytes 266272 | tf_op jit(solution)/shard_map/ppermute | solution.py:368
  129.7 6.1 %all-to-all-done.2.refs_3_ = bf16[32,64,256]{2,1,0:T(8,128)(2,1)S(1)} async-done(((bf16[32,64,256]{2,1,0:T(8,128)(2,1)}), bf16[32,64,256]{2,1,0:T(8,128)(2,1)S(1)}, u32[]{:S(2)}, u32[]{:S(2)}) %all-to-all-start.2) | async-done | bytes 1048608 | tf_op jit(solution)/shard_map/all_to_all | solution.py:360
  137.7 8.7 %all-to-all-start.3 = ((f32[64,8,128]{2,1,0:T(8,128)}), f32[64,8,128]{2,1,0:T(8,128)S(1)}, u32[]{:S(2)}, u32[]{:S(2)}) async-start(f32[64,8,128]{2,1,0:T(8,128)} %get-tuple-element.73), calls=%async_computation.3 | async-start | bytes 524288 | tf_op jit(solution)/shard_map/all_to_all | solution.py:360
  147.1 2.9 %shard_map.139 = bf16[256,256]{1,0:T(8,128)(2,1)} custom-call(bf16[256,256]{1,0:T(8,128)(2,1)} %get-tuple-element.74.refs_0_, bf16[256,256]{1,0:T(8,128)(2,1)} %refs_1_.1, bf16[256,2048]{1,0:T(8,128)(2,1)} %get-tuple-element.75.refs_2_, bf16[32,64,256]{2,1,0:T(8,128)(2,1)} %copy-done.2, f32[256,256]{1,0:T(8,128)} %get-tuple-element.76.refs_4_, ...), custom_call_target="tpu_custom_call" | custom-call | flops 20000000000 | bytes 1024 | tf_op jit(solution)/shard_map/pallas_call | solution.py:102
  150.0 9.6 %all-to-all-done.3 = f32[64,8,128]{2,1,0:T(8,128)S(1)} async-done(((f32[64,8,128]{2,1,0:T(8,128)}), f32[64,8,128]{2,1,0:T(8,128)S(1)}, u32[]{:S(2)}, u32[]{:S(2)}) %all-to-all-start.3) | async-done | bytes 262176 | tf_op jit(solution)/shard_map/all_to_all | solution.py:360
  159.7 5.2 %collective-permute-start.11 = (f32[256,256]{1,0:T(8,128)S(1)}, f32[256,256]{1,0:T(8,128)S(1)}, u32[]{:S(2)}, u32[]{:S(2)}) collective-permute-start(f32[256,256]{1,0:T(8,128)S(1)} %bitcast.15), channel_id=1, source_target_pairs={{0,1},{1,0},{2,3},{3,2},{4,5},{5,4},{6,7},{7,6},{8,9},{9,8},{10,11... | collective-permute-start | bytes 786440 | tf_op jit(solution)/shard_map/ppermute | solution.py:364
  (68 shorter events, 33.0 us)
Async XLA Ops:
  4.2 11.6 %collective-permute-start = (bf16[32,72,128]{2,1,0:T(8,128)(2,1)}, bf16[32,72,128]{2,1,0:T(8,128)(2,1)S(1)}, u32[]{:S(2)}, u32[]{:S(2)}) collective-permute-start(bf16[32,72,128]{2,1,0:T(8,128)(2,1)} %get-tuple-element.42), channel_id=1, source_target_pairs={{0,1},{1,0},{2,3},{3,2},{4,5},{5,4},{6,7},{7,6},{8,9},{9,8},{10,11... | collective-permute-start | bytes 1769480 | tf_op jit(solution)/shard_map/ppermute | solution.py:364
  13.0 21.1 %collective-permute-start.1 = (bf16[256,256]{1,0:T(8,128)(2,1)}, bf16[256,256]{1,0:T(8,128)(2,1)S(1)}, u32[]{:S(2)}, u32[]{:S(2)}) collective-permute-start(bf16[256,256]{1,0:T(8,128)(2,1)} %refs_2_.1), channel_id=1, source_target_pairs={{0,256},{256,0},{1,257},{257,1},{2,258},{258,2},{3,259},{259,3},{4... | collective-permute-start | bytes 393224 | tf_op jit(solution)/shard_map/ppermute | solution.py:364
  18.6 40.3 %all-to-all-start = ((bf16[32,144,128]{2,1,0:T(8,128)(2,1)}), bf16[32,144,128]{2,1,0:T(8,128)(2,1)S(1)}, u32[]{:S(2)}, u32[]{:S(2)}) async-start(bf16[32,144,128]{2,1,0:T(8,128)(2,1)} %shard_map.130), calls=%async_computation | async-start | bytes 2359296 | tf_op jit(solution)/shard_map/all_to_all | solution.py:360
  29.3 2.8 %copy-start.14 = (s32[1,8,4]{1,2,0:T(4,128)S(1)}, s32[1,8,4]{1,2,0:T(4,128)}, u32[]{:S(2)}) copy-start(s32[1,8,4]{1,2,0:T(4,128)} %param.15) | copy-start | bytes 388
  29.3 3.5 %copy-start.15 = (s32[1,8,4]{1,2,0:T(4,128)S(1)}, s32[1,8,4]{1,2,0:T(4,128)}, u32[]{:S(2)}) copy-start(s32[1,8,4]{1,2,0:T(4,128)} %param.16) | copy-start | bytes 388
  29.3 4.8 %copy-start.1 = (bf16[256,256]{1,0:T(8,128)(2,1)S(1)}, bf16[256,256]{1,0:T(8,128)(2,1)}, u32[]{:S(2)}) copy-start(bf16[256,256]{1,0:T(8,128)(2,1)} %refs_2_.1) | copy-start | bytes 393220
  34.1 16.7 %copy-start.6 = (bf16[256,256]{1,0:T(8,128)(2,1)}, bf16[256,256]{1,0:T(8,128)(2,1)S(1)}, u32[]{:S(2)}) copy-start(bf16[256,256]{1,0:T(8,128)(2,1)S(1)} %collective-permute-done.1.refs_3_) | copy-start | bytes 393220
  34.1 16.7 %collective-permute-start.2 = (bf16[512,256]{1,0:T(8,128)(2,1)S(1)}, bf16[512,256]{1,0:T(8,128)(2,1)S(1)}, u32[]{:S(2)}, u32[]{:S(2)}) collective-permute-start(bf16[512,256]{1,0:T(8,128)(2,1)S(1)} %pad_maximum_fusion), channel_id=1, source_target_pairs={{0,64},{64,128},{128,192},{192,0},{1,65},{65,129},{129,193},{193,1... | collective-permute-start | bytes 786440 | tf_op jit(solution)/shard_map/ppermute | solution.py:368
  37.3 13.9 %collective-permute-start.3 = (bf16[512,256]{1,0:T(8,128)(2,1)S(1)}, bf16[512,256]{1,0:T(8,128)(2,1)S(1)}, u32[]{:S(2)}, u32[]{:S(2)}) collective-permute-start(bf16[512,256]{1,0:T(8,128)(2,1)S(1)} %pad_maximum_fusion), channel_id=1, source_target_pairs={{0,128},{64,192},{128,0},{192,64},{1,129},{65,193},{129,1},{193,65... | collective-permute-start | bytes 786440 | tf_op jit(solution)/shard_map/ppermute | solution.py:368
  41.6 10.7 %collective-permute-start.4 = (bf16[512,256]{1,0:T(8,128)(2,1)S(1)}, bf16[512,256]{1,0:T(8,128)(2,1)S(1)}, u32[]{:S(2)}, u32[]{:S(2)}) collective-permute-start(bf16[512,256]{1,0:T(8,128)(2,1)S(1)} %pad_maximum_fusion), channel_id=1, source_target_pairs={{0,192},{64,0},{128,64},{192,128},{1,193},{65,1},{129,65},{193,129... | collective-permute-start | bytes 786440 | tf_op jit(solution)/shard_map/ppermute | solution.py:368
  64.9 20.2 %copy-start.16 = (bf16[32,32,256]{2,1,0:T(8,128)(2,1)S(1)}, bf16[32,32,256]{2,1,0:T(8,128)(2,1)}, u32[]{:S(2)}) copy-start(bf16[32,32,256]{2,1,0:T(8,128)(2,1)} %get-tuple-element.64) | copy-start | bytes 1572868
  64.9 5.8 %collective-permute-start.5 = (f32[256,256]{1,0:T(8,128)}, f32[256,256]{1,0:T(8,128)S(1)}, u32[]{:S(2)}, u32[]{:S(2)}) collective-permute-start(f32[256,256]{1,0:T(8,128)} %get-tuple-element.55), channel_id=1, source_target_pairs={{0,1},{1,0},{2,3},{3,2},{4,5},{5,4},{6,7},{7,6},{8,9},{9,8},{10,11... | collective-permute-start | bytes 786440 | tf_op jit(solution)/shard_map/ppermute | solution.py:364
  73.2 26.1 %all-to-all-start.1 = ((f32[64,8,128]{2,1,0:T(8,128)}), f32[64,8,128]{2,1,0:T(8,128)S(1)}, u32[]{:S(2)}, u32[]{:S(2)}) async-start(f32[64,8,128]{2,1,0:T(8,128)} %shard_map.134), calls=%async_computation.1 | async-start | bytes 524288 | tf_op jit(solution)/shard_map/all_to_all | solution.py:360
  85.1 6.5 %collective-permute-start.6 = (bf16[32,32,256]{2,1,0:T(8,128)(2,1)S(1)}, bf16[32,32,256]{2,1,0:T(8,128)(2,1)S(1)}, u32[]{:S(2)}, u32[]{:S(2)}) collective-permute-start(bf16[32,32,256]{2,1,0:T(8,128)(2,1)S(1)} %copy-done.16), channel_id=1, source_target_pairs={{0,1},{1,0},{2,3},{3,2},{4,5},{5,4},{6,7},{7,6},{8,9},{9,8},{10,11... | collective-permute-start | bytes 1572872 | tf_op jit(solution)/shard_map/ppermute | solution.py:364
  99.3 6.8 %copy-start.3 = (f32[64,8,128]{2,1,0:T(8,128)}, f32[64,8,128]{2,1,0:T(8,128)S(1)}, u32[]{:S(2)}) copy-start(f32[64,8,128]{2,1,0:T(8,128)S(1)} %all-to-all-done.1.refs_0_) | copy-start | bytes 786436
  99.3 36.5 %all-to-all-start.2 = ((bf16[32,64,256]{2,1,0:T(8,128)(2,1)}), bf16[32,64,256]{2,1,0:T(8,128)(2,1)S(1)}, u32[]{:S(2)}, u32[]{:S(2)}) async-start(bf16[32,64,256]{2,1,0:T(8,128)(2,1)} %shard_map.136), calls=%async_computation.2 | async-start | bytes 2097152 | tf_op jit(solution)/shard_map/all_to_all | solution.py:360
  107.8 11.0 %collective-permute-start.7 = (bf16[520,256]{1,0:T(8,128)(2,1)}, bf16[520,256]{1,0:T(8,128)(2,1)S(1)}, u32[]{:S(2)}, u32[]{:S(2)}) collective-permute-start(bf16[520,256]{1,0:T(8,128)(2,1)} %get-tuple-element.68), channel_id=1, source_target_pairs={{0,64},{64,128},{128,192},{192,0},{1,65},{65,129},{129,193},{193,1... | collective-permute-start | bytes 798728 | tf_op jit(solution)/shard_map/ppermute | solution.py:368
  110.8 14.6 %collective-permute-start.8 = (bf16[520,256]{1,0:T(8,128)(2,1)}, bf16[520,256]{1,0:T(8,128)(2,1)S(1)}, u32[]{:S(2)}, u32[]{:S(2)}) collective-permute-start(bf16[520,256]{1,0:T(8,128)(2,1)} %get-tuple-element.69), channel_id=1, source_target_pairs={{0,128},{64,192},{128,0},{192,64},{1,129},{65,193},{129,1},{193,65... | collective-permute-start | bytes 798728 | tf_op jit(solution)/shard_map/ppermute | solution.py:368
  115.1 11.6 %collective-permute-start.9 = (bf16[520,256]{1,0:T(8,128)(2,1)}, bf16[520,256]{1,0:T(8,128)(2,1)S(1)}, u32[]{:S(2)}, u32[]{:S(2)}) collective-permute-start(bf16[520,256]{1,0:T(8,128)(2,1)} %get-tuple-element.70), channel_id=1, source_target_pairs={{0,192},{64,0},{128,64},{192,128},{1,193},{65,1},{129,65},{193,129... | collective-permute-start | bytes 798728 | tf_op jit(solution)/shard_map/ppermute | solution.py:368
  118.8 7.9 %copy-start.7 = (bf16[520,256]{1,0:T(8,128)(2,1)}, bf16[520,256]{1,0:T(8,128)(2,1)S(1)}, u32[]{:S(2)}) copy-start(bf16[520,256]{1,0:T(8,128)(2,1)S(1)} %collective-permute-done.7.refs_2_) | copy-start | bytes 798724
  135.8 10.7 %copy-start.2 = (bf16[32,64,256]{2,1,0:T(8,128)(2,1)}, bf16[32,64,256]{2,1,0:T(8,128)(2,1)S(1)}, u32[]{:S(2)}) copy-start(bf16[32,64,256]{2,1,0:T(8,128)(2,1)S(1)} %all-to-all-done.2.refs_3_) | copy-start | bytes 3145732
  135.8 10.6 %collective-permute-start.10 = (f32[256,256]{1,0:T(8,128)}, f32[256,256]{1,0:T(8,128)S(1)}, u32[]{:S(2)}, u32[]{:S(2)}) collective-permute-start(f32[256,256]{1,0:T(8,128)} %get-tuple-element.78), channel_id=1, source_target_pairs={{0,256},{256,0},{1,257},{257,1},{2,258},{258,2},{3,259},{259,3},{4... | collective-permute-start | bytes 786440 | tf_op jit(solution)/shard_map/ppermute | solution.py:364
  137.7 22.0 %all-to-all-start.3 = ((f32[64,8,128]{2,1,0:T(8,128)}), f32[64,8,128]{2,1,0:T(8,128)S(1)}, u32[]{:S(2)}, u32[]{:S(2)}) async-start(f32[64,8,128]{2,1,0:T(8,128)} %get-tuple-element.73), calls=%async_computation.3 | async-start | bytes 524288 | tf_op jit(solution)/shard_map/all_to_all | solution.py:360
  159.7 6.3 %collective-permute-start.11 = (f32[256,256]{1,0:T(8,128)S(1)}, f32[256,256]{1,0:T(8,128)S(1)}, u32[]{:S(2)}, u32[]{:S(2)}) collective-permute-start(f32[256,256]{1,0:T(8,128)S(1)} %bitcast.15), channel_id=1, source_target_pairs={{0,1},{1,0},{2,3},{3,2},{4,5},{5,4},{6,7},{7,6},{8,9},{9,8},{10,11... | collective-permute-start | bytes 786440 | tf_op jit(solution)/shard_map/ppermute | solution.py:364
  (10 other events, 9.5 us)

commit v9 on v8

--- a/solution.py
+++ b/solution.py
@@ -12,7 +12,7 @@
 PIECES = 2
 SMALL = 1 << 10
 TILE_COST = 1 << 10
-PREPARE_COST = 20_000_000_000
+PREPARE_COST = 22_000_000_000
 PANEL_COST = 20_000_000_000
 FINAL_COST = 20_000_000_000
 NT = (((1,), (1,)), ((), ()))
@@ -151,7 +151,7 @@
 
 
 def prepare_kernel(
-    dest, source, core, hub_source, tiles, feat, row, col, weights, self_weight,
+    dest, source, core, hub_source, tiles, feat, row, weights, self_weight,
     place, back, onehot, onehot_t, hub_t, feat_t, feat_self, degree, wm_ref,
 ):
     t_ref = tiles()
@@ -162,11 +162,11 @@
     per = back_ref.shape[2] // tile
     for i in range(n):
         t = t_ref[i]
-        d = dest[i]
-        s = source[i]
+        q, k = i // per, i % per
+        d = dest[q, k]
+        s = source[q, k]
         zero = jnp.zeros_like(t)
         tt = t.T
-        q, k = i // per, i % per
         for b in range(nblk):
             place_ref[b * tile : (b + 1) * tile, i * tile : (i + 1) * tile] = jnp.where(d == b, t, zero)
             keep = jnp.logical_and(s == b, d < nblk)
@@ -179,8 +179,7 @@
     r = lax.broadcasted_iota(jnp.int32, (rows, slots), 0)
     onehot.ref[...] = jnp.where(r == row()[...], 1.0, 0.0).astype(BF16)
     onehot.send()
-    c = lax.broadcasted_iota(jnp.int32, (slots, rows), 1)
-    onehot_t.ref[...] = jnp.where(c == col()[...], 1.0, 0.0).astype(BF16)
+    onehot_t.ref[...] = onehot.ref[...].T
     onehot_t.send()
     w_ref = weights()
     owners, hub, _ = w_ref.shape
@@ -196,7 +195,7 @@
     feat_self.ref[...] = dot(x, self_weight()[...])
 
 
-def tiles_kernel(source, here, own, beside, *rest):
+def tiles_kernel(source, here_y, here_x, own, beside, *rest):
     pairs, (place, out, halo_ref, rhs_ref) = rest[:-4], rest[-4:]
     tile = LANES
     rows = out.ref.shape[0]
@@ -210,9 +209,9 @@
         halo_ref[2 * (i + 1) * rows : 2 * (i + 2) * rows, :] = pair()[...]
     for i in range(n):
         y, x = (i // per) // nx, (i // per) % nx
-        back = lax.rem(here[1] - x + nx, nx)
-        other = jnp.where(here[0] == y, 0, 1)
-        at = pl.multiple_of(((back * 2 + other) * nblk + source[i]) * tile, tile)
+        back = lax.rem(here_x[0] - x + nx, nx)
+        other = jnp.where(here_y[0] == y, 0, 1)
+        at = pl.multiple_of(((back * 2 + other) * nblk + source[i // per, i % per]) * tile, tile)
         rhs_ref[i * tile : (i + 1) * tile, :] = halo_ref[pl.ds(at, tile), :]
     out.ref[...] = dot(place()[...], rhs_ref[...])
 
@@ -290,7 +289,7 @@
     out.ref[...] = got()[...]
 
 
-def panels_kernel(dest, here, gn, back, *rest):
+def panels_kernel(dest, here_y, here_x, gn, back, *rest):
     outs, rhs_ref = rest[:-1], rest[-1]
     gn_ref, back_ref = gn(), back()
     panels, rows, depth = back_ref.shape
@@ -300,11 +299,11 @@
     nx = panels // 2
     for step in list(range(1, nx)) + [0]:
         out = outs[step]
-        x = lax.rem(here[1] + step, nx)
+        x = lax.rem(here_x[0] + step, nx)
         for other in range(2):
-            q = (here[0] if other == 0 else 1 - here[0]) * nx + x
+            q = (here_y[0] if other == 0 else 1 - here_y[0]) * nx + x
             for k in range(per):
-                d = jnp.minimum(dest[q * per + k], nblk - 1)
+                d = jnp.minimum(dest[q, k], nblk - 1)
                 at = pl.multiple_of(d * tile, tile)
                 rhs_ref[k * tile : (k + 1) * tile, :] = gn_ref[pl.ds(at, tile), :]
             part = dot(back_ref[q], rhs_ref[...])
@@ -387,7 +386,7 @@
     core = lax.axis_index("core").astype(jnp.int32)
     core1 = core.reshape(1)
     me = (lax.axis_index("far") * 2 + core).astype(jnp.int32).reshape(1)
-    here = jnp.stack([lax.axis_index("y"), lax.axis_index("x")]).astype(jnp.int32)
+    here = [lax.axis_index(name).astype(jnp.int32).reshape(1) for name in ("y", "x")]
     square = shape((rows, width), BF16)
     square32 = shape((rows, width), F32)
     beside = swap(node_feat, "y")
@@ -407,12 +406,11 @@
     got = exchange(msg, "far")
     pair = after(jnp.concatenate([node_feat, beside], axis=0), msg)
     pairs = [along_x(pair, k, nx) for k in range(1, nx)]
-    dest = tile_dest.reshape(n)
-    source = tile_source.reshape(n)
+    dest, source = tile_dest[0], tile_source[0]
     order = hub_slots.reshape(far, 2, hub)
     order = jnp.where(core == 0, order, order[:, ::-1])
     order = jnp.swapaxes(order, 0, 1)
-    slot_row, slot_col = order.reshape(1, slots), order.reshape(slots, 1)
+    slot_row = order.reshape(1, slots)
     place, back, onehot, onehot_t, hub_t, feat_t, feat_self, degree = call(
         prepare_kernel,
         [
@@ -427,13 +425,13 @@
         ],
         (dest, source, core1, hub_source[0]),
         (
-            tile_weights.reshape(n, tile, tile), after(node_feat, msg), slot_row, slot_col,
+            tile_weights.reshape(n, tile, tile), after(node_feat, msg), slot_row,
             hub_weights[0], self_weight,
         ),
         [pltpu.VMEM((slots, rows), BF16)], PREPARE_COST,
     )
     local = call(
-        tiles_kernel, [square32], (source, here), (node_feat, beside, *pairs, place),
+        tiles_kernel, [square32], (source, *here), (node_feat, beside, *pairs, place),
         [pltpu.VMEM((panels * rows, width), BF16), pltpu.VMEM((n * tile, width), BF16)],
         TILE_COST,
     )
@@ -463,7 +461,7 @@
         panels_kernel,
         [shape((2 * rows, width), F32)]
         + [(shape((tall, width), BF16), (slice(0, 2 * rows),))] * (nx - 1),
-        (dest, here), (after(gn, both), back), [pltpu.VMEM((per * tile, width), BF16)],
+        (dest, *here), (after(gn, both), back), [pltpu.VMEM((per * tile, width), BF16)],
         PANEL_COST,
     )
     terms = [terms] if nx == 1 else terms

time: 168 us -> 168 us (level)
  waiting for transfers between devices: 34.8 us -> 38.5 us
  local copies, waits for them, and re-layouts: 10.4 us -> 8.35 us
    ppermute x6, waiting for transfers between devices: 9.86 us -> 14.4 us  [along_x(): return lax.ppermute(x, 'x', [(i, (i + step) % nx) for i in range(nx)])]
    reshape x4 -> x1, local copies, waits for them, and re-layouts: 3.89 us -> 0.68 us  [per_device(): slot_row = order.reshape(1, slots)]
    unnamed x39 -> x37, local copies, waits for them, and re-layouts: 6.41 us -> 6.25 us
  transfers between devices with their start and end apart: 16 -> 16, of which waited for: 11 -> 10; matrix products, arithmetic and copies ran while one was open for 3% -> 2% of each run, Pallas kernels for 15% -> 15%
where the time goes in v9:
time: 168 us; the launch traced here: 167 us
  starting transfers between devices  82.9 us (49%)
  waiting for transfers between devices  38.5 us (23%)
  Pallas kernels  35.3 us (21%)
  local copies, waits for them, and re-layouts  8.35 us (5%)
    all_to_all x4, starting transfers between devices, exchange(): return lax.all_to_all(x, axis, split_axis=0, concat_axis=0, tiled=True)  38.3 us
    pallas_call x11, Pallas kernels, call(): pl.pallas_call(body, out_shape=[shape(x.shape, x.dtype) for x, _ in outs]...  35.3 us
    ppermute x6, starting transfers between devices, swap(): return lax.ppermute(x, axis, [(0, 1), (1, 0)])  24.8 us
    all_to_all x4, waiting for transfers between devices, exchange(): return lax.all_to_all(x, axis, split_axis=0, concat_axis=0, tiled=True)  21.6 us
    ppermute x6, starting transfers between devices, along_x(): return lax.ppermute(x, 'x', [(i, (i + step) % nx) for i in range(nx)])  19.8 us
    ppermute x6, waiting for transfers between devices, along_x(): return lax.ppermute(x, 'x', [(i, (i + step) % nx) for i in range(nx)])  14.4 us
    unnamed x37, local copies, waits for them, and re-layouts  6.25 us
  transfers between devices with their start and end apart: 16, of which 10 were waited for; matrix products, arithmetic and copies ran while one was open for 2% of the time, Pallas kernels for 15%

profile of v9, /device:TPU:1, one launch (start us, length us, event | category | flops | bytes accessed | tf_op | source)
XLA Modules:
  0.0 167.1 jit_solution(7708240724257693769)
XLA Ops:
  0.6 3.5 %shard_map.129 = (bf16[32,144,128]{2,1,0:T(8,128)(2,1)}, bf16[32,72,128]{2,1,0:T(8,128)(2,1)}) custom-call(s32[64]{0:T(128)} %bitcast.25, s32[1]{0:T(128)} %bitcast.refs_1_.refs_2_.refs_0_, bf16[64,32,128]{2,1,0:T(8,128)(2,1)} %bitcast.19, bf16[256,256]{1,0:T(8,128)(2,1)} %refs_3_.3), custom_call_target="tpu_custom_call" | custom-call | flops 1024 | bytes 1024 | tf_op jit(solution)/shard_map/pallas_call | solution.py:102
  4.2 8.8 %collective-permute-start = (bf16[32,72,128]{2,1,0:T(8,128)(2,1)}, bf16[32,72,128]{2,1,0:T(8,128)(2,1)S(1)}, u32[]{:S(2)}, u32[]{:S(2)}) collective-permute-start(bf16[32,72,128]{2,1,0:T(8,128)(2,1)} %get-tuple-element.42), channel_id=1, source_target_pairs={{0,1},{1,0},{2,3},{3,2},{4,5},{5,4},{6,7},{7,6},{8,9},{9,8},{10,11... | collective-permute-start | bytes 1769480 | tf_op jit(solution)/shard_map/ppermute | solution.py:363
  18.6 10.8 %all-to-all-start = ((bf16[32,144,128]{2,1,0:T(8,128)(2,1)}), bf16[32,144,128]{2,1,0:T(8,128)(2,1)S(1)}, u32[]{:S(2)}, u32[]{:S(2)}) async-start(bf16[32,144,128]{2,1,0:T(8,128)(2,1)} %shard_map.130), calls=%async_computation | async-start | bytes 2359296 | tf_op jit(solution)/shard_map/all_to_all | solution.py:359
  31.6 4.4 %collective-permute-start.4 = (bf16[512,256]{1,0:T(8,128)(2,1)S(1)}, bf16[512,256]{1,0:T(8,128)(2,1)S(1)}, u32[]{:S(2)}, u32[]{:S(2)}) collective-permute-start(bf16[512,256]{1,0:T(8,128)(2,1)S(1)} %pad_maximum_fusion), channel_id=1, source_target_pairs={{0,192},{64,0},{128,64},{192,128},{1,193},{65,1},{129,65},{193,129... | collective-permute-start | bytes 786440 | tf_op jit(solution)/shard_map/ppermute | solution.py:367
  38.4 2.5 %collective-permute-start.2 = (bf16[512,256]{1,0:T(8,128)(2,1)S(1)}, bf16[512,256]{1,0:T(8,128)(2,1)S(1)}, u32[]{:S(2)}, u32[]{:S(2)}) collective-permute-start(bf16[512,256]{1,0:T(8,128)(2,1)S(1)} %pad_maximum_fusion), channel_id=1, source_target_pairs={{0,64},{64,128},{128,192},{192,0},{1,65},{65,129},{129,193},{193,1... | collective-permute-start | bytes 786440 | tf_op jit(solution)/shard_map/ppermute | solution.py:367
  40.9 6.2 %shard_map.131 = (bf16[256,4096]{1,0:T(8,128)(2,1)}, bf16[8,256,512]{2,1,0:T(8,128)(2,1)}, bf16[256,2048]{1,0:T(8,128)(2,1)}, bf16[2048,256]{1,0:T(8,128)(2,1)},...) custom-call(s32[8,4]{1,0:T(8,128)} %copy.27.refs_0_, ...), custom_call_target="tpu_custom_call" | custom-call | flops 22000001024 | bytes 1024 | tf_op jit(solution)/shard_map/pallas_call | solution.py:102
  47.2 6.0 %collective-permute-done.2.refs_5_ = bf16[512,256]{1,0:T(8,128)(2,1)S(1)} collective-permute-done((bf16[512,256]{1,0:T(8,128)(2,1)S(1)}, bf16[512,256]{1,0:T(8,128)(2,1)S(1)}, u32[]{:S(2)}, u32[]{:S(2)}) %collective-permute-start.2) | collective-permute-done | bytes 262176 | tf_op jit(solution)/shard_map/ppermute | solution.py:367
  53.9 4.2 %shard_map.132.refs_4_ = f32[256,256]{1,0:T(8,128)} custom-call(s32[8,4]{1,0:T(8,128)} %copy.28.refs_1_.refs_0_, s32[1]{0:T(128)} %bitcast.9.refs_1_, s32[1]{0:T(128)} %bitcast.10.refs_2_, bf16[256,256]{1,0:T(8,128)(2,1)} %refs_3_.3, bf16[256,256]{1,0:T(8,128)(2,1)} %copy-done.6, bf16[512,256]{1,0:T(8,128)(2,1)} %copy-done.12, bf16[512,256]{1,0:T(8,128)(2,1)} %copy-done.11, ...), custom_call_target="tpu_custom_call" | custom-call | flops 1024 | bytes 1024 | tf_op jit(solution)/shard_map/pallas_call | solution.py:102
  60.1 4.9 %shard_map.133 = (bf16[256,256]{1,0:T(8,128)(2,1)}, bf16[256,256]{1,0:T(8,128)(2,1)}, bf16[256,256]{1,0:T(8,128)(2,1)}, f32[256,256]{1,0:T(8,128)}, f32[256,256]...) custom-call(s32[1]{0:T(128)} %bitcast.refs_1_.refs_2_.refs_0_, s32[1]{0:T(128)} %bitcast.1.refs_1_, ...), custom_call_target="tpu_custom_call" | custom-call | flops 1024 | bytes 1024 | tf_op jit(solution)/shard_map/pallas_call | solution.py:102
  65.1 4.5 %collective-permute-start.5 = (f32[256,256]{1,0:T(8,128)}, f32[256,256]{1,0:T(8,128)S(1)}, u32[]{:S(2)}, u32[]{:S(2)}) collective-permute-start(f32[256,256]{1,0:T(8,128)} %get-tuple-element.55), channel_id=1, source_target_pairs={{0,1},{1,0},{2,3},{3,2},{4,5},{5,4},{6,7},{7,6},{8,9},{9,8},{10,11... | collective-permute-start | bytes 786440 | tf_op jit(solution)/shard_map/ppermute | solution.py:363
  73.4 11.9 %all-to-all-start.1 = ((f32[64,8,128]{2,1,0:T(8,128)}), f32[64,8,128]{2,1,0:T(8,128)S(1)}, u32[]{:S(2)}, u32[]{:S(2)}) async-start(f32[64,8,128]{2,1,0:T(8,128)} %shard_map.134), calls=%async_computation.1 | async-start | bytes 524288 | tf_op jit(solution)/shard_map/all_to_all | solution.py:359
  85.3 2.6 %collective-permute-start.6 = (bf16[32,32,256]{2,1,0:T(8,128)(2,1)S(1)}, bf16[32,32,256]{2,1,0:T(8,128)(2,1)S(1)}, u32[]{:S(2)}, u32[]{:S(2)}) collective-permute-start(bf16[32,32,256]{2,1,0:T(8,128)(2,1)S(1)} %copy-done.16), channel_id=1, source_target_pairs={{0,1},{1,0},{2,3},{3,2},{4,5},{5,4},{6,7},{7,6},{8,9},{9,8},{10,11... | collective-permute-start | bytes 1572872 | tf_op jit(solution)/shard_map/ppermute | solution.py:363
  87.9 4.0 %shard_map.135 = (f32[512,256]{1,0:T(8,128)}, bf16[520,256]{1,0:T(8,128)(2,1)}, bf16[520,256]{1,0:T(8,128)(2,1)}, bf16[520,256]{1,0:T(8,128)(2,1)}) custom-call(s32[8,4]{1,0:T(8,128)} %copy.27.refs_0_, s32[1]{0:T(128)} %bitcast.9.refs_1_, s32[1]{0:T(128)} %bitcast.10.refs_2_, bf16[256,256]{1,0:T(8,128)(2,1)} %get-tuple-element.57.refs_3_, ...), custom_call_target="tpu_custom_call" | custom-call | flops 20000000000 | bytes 1024 | tf_op jit(solution)/shard_map/pallas_call | solution.py:102
  94.6 4.9 %all-to-all-done.1.refs_0_ = f32[64,8,128]{2,1,0:T(8,128)S(1)} async-done(((f32[64,8,128]{2,1,0:T(8,128)}), f32[64,8,128]{2,1,0:T(8,128)S(1)}, u32[]{:S(2)}, u32[]{:S(2)}) %all-to-all-start.1) | async-done | bytes 262176 | tf_op jit(solution)/shard_map/all_to_all | solution.py:359
  99.5 6.8 %all-to-all-start.2 = ((bf16[32,64,256]{2,1,0:T(8,128)(2,1)}), bf16[32,64,256]{2,1,0:T(8,128)(2,1)S(1)}, u32[]{:S(2)}, u32[]{:S(2)}) async-start(bf16[32,64,256]{2,1,0:T(8,128)(2,1)} %shard_map.136), calls=%async_computation.2 | async-start | bytes 2097152 | tf_op jit(solution)/shard_map/all_to_all | solution.py:359
  108.0 3.0 %collective-permute-start.7 = (bf16[520,256]{1,0:T(8,128)(2,1)}, bf16[520,256]{1,0:T(8,128)(2,1)S(1)}, u32[]{:S(2)}, u32[]{:S(2)}) collective-permute-start(bf16[520,256]{1,0:T(8,128)(2,1)} %get-tuple-element.68), channel_id=1, source_target_pairs={{0,64},{64,128},{128,192},{192,0},{1,65},{65,129},{129,193},{193,1... | collective-permute-start | bytes 798728 | tf_op jit(solution)/shard_map/ppermute | solution.py:367
  111.0 4.4 %collective-permute-start.8 = (bf16[520,256]{1,0:T(8,128)(2,1)}, bf16[520,256]{1,0:T(8,128)(2,1)S(1)}, u32[]{:S(2)}, u32[]{:S(2)}) collective-permute-start(bf16[520,256]{1,0:T(8,128)(2,1)} %get-tuple-element.69), channel_id=1, source_target_pairs={{0,128},{64,192},{128,0},{192,64},{1,129},{65,193},{129,1},{193,65... | collective-permute-start | bytes 798728 | tf_op jit(solution)/shard_map/ppermute | solution.py:367
  115.4 3.2 %collective-permute-start.9 = (bf16[520,256]{1,0:T(8,128)(2,1)}, bf16[520,256]{1,0:T(8,128)(2,1)S(1)}, u32[]{:S(2)}, u32[]{:S(2)}) collective-permute-start(bf16[520,256]{1,0:T(8,128)(2,1)} %get-tuple-element.70), channel_id=1, source_target_pairs={{0,192},{64,0},{128,64},{192,128},{1,193},{65,1},{129,65},{193,129... | collective-permute-start | bytes 798728 | tf_op jit(solution)/shard_map/ppermute | solution.py:367
  119.0 6.5 %collective-permute-done.8.refs_3_ = bf16[520,256]{1,0:T(8,128)(2,1)S(1)} collective-permute-done((bf16[520,256]{1,0:T(8,128)(2,1)}, bf16[520,256]{1,0:T(8,128)(2,1)S(1)}, u32[]{:S(2)}, u32[]{:S(2)}) %collective-permute-start.8) | collective-permute-done | bytes 266272 | tf_op jit(solution)/shard_map/ppermute | solution.py:367
  129.9 6.1 %all-to-all-done.2.refs_3_ = bf16[32,64,256]{2,1,0:T(8,128)(2,1)S(1)} async-done(((bf16[32,64,256]{2,1,0:T(8,128)(2,1)}), bf16[32,64,256]{2,1,0:T(8,128)(2,1)S(1)}, u32[]{:S(2)}, u32[]{:S(2)}) %all-to-all-start.2) | async-done | bytes 1048608 | tf_op jit(solution)/shard_map/all_to_all | solution.py:359
  137.9 8.7 %all-to-all-start.3 = ((f32[64,8,128]{2,1,0:T(8,128)}), f32[64,8,128]{2,1,0:T(8,128)S(1)}, u32[]{:S(2)}, u32[]{:S(2)}) async-start(f32[64,8,128]{2,1,0:T(8,128)} %get-tuple-element.73), calls=%async_computation.3 | async-start | bytes 524288 | tf_op jit(solution)/shard_map/all_to_all | solution.py:359
  147.4 2.9 %shard_map.139 = bf16[256,256]{1,0:T(8,128)(2,1)} custom-call(bf16[256,256]{1,0:T(8,128)(2,1)} %get-tuple-element.74.refs_0_, bf16[256,256]{1,0:T(8,128)(2,1)} %refs_1_.1, bf16[256,2048]{1,0:T(8,128)(2,1)} %get-tuple-element.75.refs_2_, bf16[32,64,256]{2,1,0:T(8,128)(2,1)} %copy-done.2, f32[256,256]{1,0:T(8,128)} %get-tuple-element.76.refs_4_, ...), custom_call_target="tpu_custom_call" | custom-call | flops 20000000000 | bytes 1024 | tf_op jit(solution)/shard_map/pallas_call | solution.py:102
  150.3 9.6 %all-to-all-done.3 = f32[64,8,128]{2,1,0:T(8,128)S(1)} async-done(((f32[64,8,128]{2,1,0:T(8,128)}), f32[64,8,128]{2,1,0:T(8,128)S(1)}, u32[]{:S(2)}, u32[]{:S(2)}) %all-to-all-start.3) | async-done | bytes 262176 | tf_op jit(solution)/shard_map/all_to_all | solution.py:359
  159.9 5.2 %collective-permute-start.11 = (f32[256,256]{1,0:T(8,128)S(1)}, f32[256,256]{1,0:T(8,128)S(1)}, u32[]{:S(2)}, u32[]{:S(2)}) collective-permute-start(f32[256,256]{1,0:T(8,128)S(1)} %bitcast.17), channel_id=1, source_target_pairs={{0,1},{1,0},{2,3},{3,2},{4,5},{5,4},{6,7},{7,6},{8,9},{9,8},{10,11... | collective-permute-start | bytes 786440 | tf_op jit(solution)/shard_map/ppermute | solution.py:363
  (64 shorter events, 30.4 us)
Async XLA Ops:
  4.2 11.6 %collective-permute-start = (bf16[32,72,128]{2,1,0:T(8,128)(2,1)}, bf16[32,72,128]{2,1,0:T(8,128)(2,1)S(1)}, u32[]{:S(2)}, u32[]{:S(2)}) collective-permute-start(bf16[32,72,128]{2,1,0:T(8,128)(2,1)} %get-tuple-element.42), channel_id=1, source_target_pairs={{0,1},{1,0},{2,3},{3,2},{4,5},{5,4},{6,7},{7,6},{8,9},{9,8},{10,11... | collective-permute-start | bytes 1769480 | tf_op jit(solution)/shard_map/ppermute | solution.py:363
  13.0 18.6 %collective-permute-start.1 = (bf16[256,256]{1,0:T(8,128)(2,1)}, bf16[256,256]{1,0:T(8,128)(2,1)S(1)}, u32[]{:S(2)}, u32[]{:S(2)}) collective-permute-start(bf16[256,256]{1,0:T(8,128)(2,1)} %refs_3_.3), channel_id=1, source_target_pairs={{0,256},{256,0},{1,257},{257,1},{2,258},{258,2},{3,259},{259,3},{4... | collective-permute-start | bytes 393224 | tf_op jit(solution)/shard_map/ppermute | solution.py:363
  18.6 10.9 %copy-start.14 = (s32[1,8,4]{1,2,0:T(4,128)S(1)}, s32[1,8,4]{1,2,0:T(4,128)}, u32[]{:S(2)}) copy-start(s32[1,8,4]{1,2,0:T(4,128)} %param.15) | copy-start | bytes 388
  18.6 11.6 %copy-start.15 = (s32[1,8,4]{1,2,0:T(4,128)S(1)}, s32[1,8,4]{1,2,0:T(4,128)}, u32[]{:S(2)}) copy-start(s32[1,8,4]{1,2,0:T(4,128)} %param.16) | copy-start | bytes 388
  18.6 12.9 %copy-start.1 = (bf16[256,256]{1,0:T(8,128)(2,1)S(1)}, bf16[256,256]{1,0:T(8,128)(2,1)}, u32[]{:S(2)}) copy-start(bf16[256,256]{1,0:T(8,128)(2,1)} %refs_3_.3) | copy-start | bytes 393220
  18.6 40.5 %all-to-all-start = ((bf16[32,144,128]{2,1,0:T(8,128)(2,1)}), bf16[32,144,128]{2,1,0:T(8,128)(2,1)S(1)}, u32[]{:S(2)}, u32[]{:S(2)}) async-start(bf16[32,144,128]{2,1,0:T(8,128)(2,1)} %shard_map.130), calls=%async_computation | async-start | bytes 2359296 | tf_op jit(solution)/shard_map/all_to_all | solution.py:359
  31.6 15.6 %copy-start.6 = (bf16[256,256]{1,0:T(8,128)(2,1)}, bf16[256,256]{1,0:T(8,128)(2,1)S(1)}, u32[]{:S(2)}) copy-start(bf16[256,256]{1,0:T(8,128)(2,1)S(1)} %collective-permute-done.1.refs_4_) | copy-start | bytes 393220
  31.6 15.6 %collective-permute-start.4 = (bf16[512,256]{1,0:T(8,128)(2,1)S(1)}, bf16[512,256]{1,0:T(8,128)(2,1)S(1)}, u32[]{:S(2)}, u32[]{:S(2)}) collective-permute-start(bf16[512,256]{1,0:T(8,128)(2,1)S(1)} %pad_maximum_fusion), channel_id=1, source_target_pairs={{0,192},{64,0},{128,64},{192,128},{1,193},{65,1},{129,65},{193,129... | collective-permute-start | bytes 786440 | tf_op jit(solution)/shard_map/ppermute | solution.py:367
  36.0 11.2 %collective-permute-start.3 = (bf16[512,256]{1,0:T(8,128)(2,1)S(1)}, bf16[512,256]{1,0:T(8,128)(2,1)S(1)}, u32[]{:S(2)}, u32[]{:S(2)}) collective-permute-start(bf16[512,256]{1,0:T(8,128)(2,1)S(1)} %pad_maximum_fusion), channel_id=1, source_target_pairs={{0,128},{64,192},{128,0},{192,64},{1,129},{65,193},{129,1},{193,65... | collective-permute-start | bytes 786440 | tf_op jit(solution)/shard_map/ppermute | solution.py:367
  38.4 14.8 %collective-permute-start.2 = (bf16[512,256]{1,0:T(8,128)(2,1)S(1)}, bf16[512,256]{1,0:T(8,128)(2,1)S(1)}, u32[]{:S(2)}, u32[]{:S(2)}) collective-permute-start(bf16[512,256]{1,0:T(8,128)(2,1)S(1)} %pad_maximum_fusion), channel_id=1, source_target_pairs={{0,64},{64,128},{128,192},{192,0},{1,65},{65,129},{129,193},{193,1... | collective-permute-start | bytes 786440 | tf_op jit(solution)/shard_map/ppermute | solution.py:367
  65.1 20.2 %copy-start.16 = (bf16[32,32,256]{2,1,0:T(8,128)(2,1)S(1)}, bf16[32,32,256]{2,1,0:T(8,128)(2,1)}, u32[]{:S(2)}) copy-start(bf16[32,32,256]{2,1,0:T(8,128)(2,1)} %get-tuple-element.64) | copy-start | bytes 1572868
  65.1 5.8 %collective-permute-start.5 = (f32[256,256]{1,0:T(8,128)}, f32[256,256]{1,0:T(8,128)S(1)}, u32[]{:S(2)}, u32[]{:S(2)}) collective-permute-start(f32[256,256]{1,0:T(8,128)} %get-tuple-element.55), channel_id=1, source_target_pairs={{0,1},{1,0},{2,3},{3,2},{4,5},{5,4},{6,7},{7,6},{8,9},{9,8},{10,11... | collective-permute-start | bytes 786440 | tf_op jit(solution)/shard_map/ppermute | solution.py:363
  73.4 26.1 %all-to-all-start.1 = ((f32[64,8,128]{2,1,0:T(8,128)}), f32[64,8,128]{2,1,0:T(8,128)S(1)}, u32[]{:S(2)}, u32[]{:S(2)}) async-start(f32[64,8,128]{2,1,0:T(8,128)} %shard_map.134), calls=%async_computation.1 | async-start | bytes 524288 | tf_op jit(solution)/shard_map/all_to_all | solution.py:359
  85.3 6.5 %collective-permute-start.6 = (bf16[32,32,256]{2,1,0:T(8,128)(2,1)S(1)}, bf16[32,32,256]{2,1,0:T(8,128)(2,1)S(1)}, u32[]{:S(2)}, u32[]{:S(2)}) collective-permute-start(bf16[32,32,256]{2,1,0:T(8,128)(2,1)S(1)} %copy-done.16), channel_id=1, source_target_pairs={{0,1},{1,0},{2,3},{3,2},{4,5},{5,4},{6,7},{7,6},{8,9},{9,8},{10,11... | collective-permute-start | bytes 1572872 | tf_op jit(solution)/shard_map/ppermute | solution.py:363
  99.5 6.9 %copy-start.3 = (f32[64,8,128]{2,1,0:T(8,128)}, f32[64,8,128]{2,1,0:T(8,128)S(1)}, u32[]{:S(2)}) copy-start(f32[64,8,128]{2,1,0:T(8,128)S(1)} %all-to-all-done.1.refs_0_) | copy-start | bytes 786436
  99.5 36.5 %all-to-all-start.2 = ((bf16[32,64,256]{2,1,0:T(8,128)(2,1)}), bf16[32,64,256]{2,1,0:T(8,128)(2,1)S(1)}, u32[]{:S(2)}, u32[]{:S(2)}) async-start(bf16[32,64,256]{2,1,0:T(8,128)(2,1)} %shard_map.136), calls=%async_computation.2 | async-start | bytes 2097152 | tf_op jit(solution)/shard_map/all_to_all | solution.py:359
  108.0 11.0 %collective-permute-start.7 = (bf16[520,256]{1,0:T(8,128)(2,1)}, bf16[520,256]{1,0:T(8,128)(2,1)S(1)}, u32[]{:S(2)}, u32[]{:S(2)}) collective-permute-start(bf16[520,256]{1,0:T(8,128)(2,1)} %get-tuple-element.68), channel_id=1, source_target_pairs={{0,64},{64,128},{128,192},{192,0},{1,65},{65,129},{129,193},{193,1... | collective-permute-start | bytes 798728 | tf_op jit(solution)/shard_map/ppermute | solution.py:367
  111.0 14.6 %collective-permute-start.8 = (bf16[520,256]{1,0:T(8,128)(2,1)}, bf16[520,256]{1,0:T(8,128)(2,1)S(1)}, u32[]{:S(2)}, u32[]{:S(2)}) collective-permute-start(bf16[520,256]{1,0:T(8,128)(2,1)} %get-tuple-element.69), channel_id=1, source_target_pairs={{0,128},{64,192},{128,0},{192,64},{1,129},{65,193},{129,1},{193,65... | collective-permute-start | bytes 798728 | tf_op jit(solution)/shard_map/ppermute | solution.py:367
  115.4 11.6 %collective-permute-start.9 = (bf16[520,256]{1,0:T(8,128)(2,1)}, bf16[520,256]{1,0:T(8,128)(2,1)S(1)}, u32[]{:S(2)}, u32[]{:S(2)}) collective-permute-start(bf16[520,256]{1,0:T(8,128)(2,1)} %get-tuple-element.70), channel_id=1, source_target_pairs={{0,192},{64,0},{128,64},{192,128},{1,193},{65,1},{129,65},{193,129... | collective-permute-start | bytes 798728 | tf_op jit(solution)/shard_map/ppermute | solution.py:367
  119.0 7.9 %copy-start.7 = (bf16[520,256]{1,0:T(8,128)(2,1)}, bf16[520,256]{1,0:T(8,128)(2,1)S(1)}, u32[]{:S(2)}) copy-start(bf16[520,256]{1,0:T(8,128)(2,1)S(1)} %collective-permute-done.7.refs_2_) | copy-start | bytes 798724
  136.0 10.7 %copy-start.2 = (bf16[32,64,256]{2,1,0:T(8,128)(2,1)}, bf16[32,64,256]{2,1,0:T(8,128)(2,1)S(1)}, u32[]{:S(2)}) copy-start(bf16[32,64,256]{2,1,0:T(8,128)(2,1)S(1)} %all-to-all-done.2.refs_3_) | copy-start | bytes 3145732
  136.0 10.6 %collective-permute-start.10 = (f32[256,256]{1,0:T(8,128)}, f32[256,256]{1,0:T(8,128)S(1)}, u32[]{:S(2)}, u32[]{:S(2)}) collective-permute-start(f32[256,256]{1,0:T(8,128)} %get-tuple-element.78), channel_id=1, source_target_pairs={{0,256},{256,0},{1,257},{257,1},{2,258},{258,2},{3,259},{259,3},{4... | collective-permute-start | bytes 786440 | tf_op jit(solution)/shard_map/ppermute | solution.py:363
  137.9 22.0 %all-to-all-start.3 = ((f32[64,8,128]{2,1,0:T(8,128)}), f32[64,8,128]{2,1,0:T(8,128)S(1)}, u32[]{:S(2)}, u32[]{:S(2)}) async-start(f32[64,8,128]{2,1,0:T(8,128)} %get-tuple-element.73), calls=%async_computation.3 | async-start | bytes 524288 | tf_op jit(solution)/shard_map/all_to_all | solution.py:359
  159.9 6.3 %collective-permute-start.11 = (f32[256,256]{1,0:T(8,128)S(1)}, f32[256,256]{1,0:T(8,128)S(1)}, u32[]{:S(2)}, u32[]{:S(2)}) collective-permute-start(f32[256,256]{1,0:T(8,128)S(1)} %bitcast.17), channel_id=1, source_target_pairs={{0,1},{1,0},{2,3},{3,2},{4,5},{5,4},{6,7},{7,6},{8,9},{9,8},{10,11... | collective-permute-start | bytes 786440 | tf_op jit(solution)/shard_map/ppermute | solution.py:363
  (10 other events, 18.9 us)
